TPU v7x, 32 devices: a whole 2x2x4 slice. The times are simulated.
32 devices in a mesh: member: 2 (over core), atm: 4 (over z), ocn: 4 (over y, x).
Axes of the slice: x: 2, y: 2, z: 4, core: 2. Of those that a mesh axis runs over, the one named last changes fastest.
Arguments:
- atmos_state: float32 [4, 137, 65536], P(None, None, ('member', 'atm', 'ocn')), parts along dimension 2, may hold values from -6 to 6
- inverses: float32 [4, 4, 137, 137], P('atm'), may hold values from -1 to 2
- flux_weight: float32 [4, 137, 128], replicated, may hold values from -0.25 to 0.25
- surface_weight: float32 [4, 137, 128], replicated, may hold values from -0.5 to 0.5
- area_table: float32 [64], replicated, may hold values from 0.25 to 1
- xc_column: int32 [65536], P(('atm', 'ocn')), may hold values from 0 to 2047, as said below
- xc_dest: int32 [65536, 1], P(('atm', 'ocn')), may hold values from 0 to 15, as said below
- xc_cell: int32 [65536], P(('atm', 'ocn')), may hold values from 0 to 4095, as said below
- xc_class: int32 [65536], P(('atm', 'ocn')), may hold values from 0 to 63
- tracer: float32 [75, 128, 1024], P(None, 'atm', ('member', 'ocn')), parts along dimension 2, may hold values from -6 to 6
- land_sea: int32 [128, 512], P('atm', 'ocn'), may hold values 0 or 1
- forcing_weight: float32 [75, 128], replicated, may hold values from -0.25 to 0.25
- surface_map: float32 [75, 128], replicated, may hold values from -0.75 to 0.75
- diffusivity: float32 [75], replicated, may hold values from 0.04 to 0.24
Outputs:
- final_state: float32 [4, 137, 65536], P(None, None, ('member', 'atm', 'ocn')), parts along dimension 2
- tracer_out: float32 [75, 128, 1024], P(None, 'atm', ('member', 'ocn')), parts along dimension 2
There are 2 independent parts, one for each index of `member`. A program takes and returns all parts, laid end to end along the dimension named above; an argument that names none is the same for every part. Nothing has to cross between parts.
Inputs may be any that keep to these rules, and one draw needn't show every extreme that they name: `xc_column`: each column of a device is named by exactly two of that device's exchange cells. `xc_dest`: the exchange cells of the device at index r along atm and index q along ocn name only ocean tiles r * 4 to r * 4 + 3; the tile r * 4 + q gets exactly 3072 of them and every other tile at most 3072; all devices of one index along atm send equally many cells to the tiles at the same offset along ocn, counted modulo 4. `xc_cell`: every ocean cell of the grid is named by exactly one exchange cell, together with xc_dest.
All inputs are finite; a program needn't handle non-finite values. No bound on the sum of `land_sea` on one device may be relied on, other than what follows from the above.
Results may differ from a plain program's by a relative error of at most 0.0025.
Values may be sent and summed in bfloat16 or wider, within the bound.
No kernel may reach another device: no remote copies, remote signals or barrier semaphores. Data moves between devices by JAX's collectives and lax.ppermute only.
A program may use at most 128 MiB of HBM per device.

v0:
```python
import jax
import jax.numpy as jnp
from jax import lax
from jax.sharding import PartitionSpec as P

OSTEPS = 4


highest = lax.Precision.HIGHEST


def padded_2(value, sides, width):
    for axis, dim in sides:
        count, length = (lax.axis_size(axis), value.shape[dim])
        up = [(i, (i + 1) % count) for i in range(count - 1)]
        down = [(j, i) for i, j in up]
        last = lax.slice_in_dim(value, length - width, length, axis=dim)
        leading = lax.slice_in_dim(value, 0, width, axis=dim)
        before = lax.ppermute(last, axis, up)
        after = lax.ppermute(leading, axis, down)
        value = jnp.concatenate([before, value, after], axis=dim)
    return value


def diffuse(padded, wet_pad, forcing, diffusivity):
    centre = padded[:, 1:-1, 1:-1]
    span_rows = centre.shape[1]
    span_cols = centre.shape[2]
    laplace_sum = jnp.zeros_like(centre)
    for row_from, col_from in ((0, 1), (2, 1), (1, 0), (1, 2)):
        neighbour = padded[:, row_from : row_from + span_rows, col_from : col_from + span_cols]
        neighbour_wet = wet_pad[row_from : row_from + span_rows, col_from : col_from + span_cols]
        laplace_sum = laplace_sum + neighbour_wet * (neighbour - centre)
    return centre + wet_pad[1:-1, 1:-1] * (diffusivity[:, None, None] * laplace_sum + forcing)


def column_solve(inverse_set, column_field):
    return jnp.einsum("vkj,vjc->vkc", inverse_set, column_field, precision=highest)


def class_areas(classes, area_table):
    class_hot = (
        classes[:, None] == jnp.arange(area_table.shape[0], dtype=jnp.int32)[None, :]
    ).astype(jnp.float32)
    return jnp.dot(class_hot, area_table, precision=highest)


def on_device(
    atmos_state,
    inverses,
    flux_weight,
    surface_weight,
    area_table,
    xc_column,
    xc_dest,
    xc_cell,
    xc_class,
    tracer,
    land_sea,
    forcing_weight,
    surface_map,
    diffusivity,
):
    peer_count = lax.axis_size("ocn")
    columns = atmos_state.shape[2]
    capacity = 3 * (2 * columns) // peer_count
    levels = tracer.shape[0]
    tile_rows = tracer.shape[1]
    tile_cols = tracer.shape[2]
    ocean_cells = tile_rows * tile_cols
    flux_width = flux_weight.shape[2]
    slot_total = peer_count * capacity
    diffused = column_solve(inverses[0], atmos_state)
    flux_rows = jnp.einsum("vkc,vkf->cf", diffused, flux_weight, precision=highest)
    cell_area = class_areas(xc_class, area_table)
    target = xc_dest[:, 0] % peer_count
    dest_hot = (target[:, None] == jnp.arange(peer_count, dtype=jnp.int32)[None, :]).astype(
        jnp.int32
    )
    slot_rank = jnp.sum(jnp.cumsum(dest_hot, axis=0) * dest_hot, axis=1) - 1
    slot_index = target * capacity + slot_rank
    out_cells = jnp.full((slot_total,), ocean_cells, jnp.int32).at[slot_index].set(xc_cell)
    cell_rows = (cell_area[:, None] * flux_rows[xc_column]).astype(jnp.bfloat16)
    outgoing = jnp.zeros((slot_total, flux_width), jnp.bfloat16).at[slot_index].set(cell_rows)
    received, recv_cells = (
        lax.all_to_all(outgoing, "ocn", split_axis=0, concat_axis=0, tiled=True),
        lax.all_to_all(out_cells, "ocn", split_axis=0, concat_axis=0, tiled=True),
    )
    forcing_rows = jax.ops.segment_sum(received.astype(jnp.float32), recv_cells, ocean_cells + 1)[
        :ocean_cells
    ]
    forcing = jnp.einsum("lf,cf->lc", forcing_weight, forcing_rows, precision=highest).reshape(
        levels, tile_rows, tile_cols
    )
    wet_cells = land_sea.astype(jnp.float32)
    current = tracer
    for substep in range(OSTEPS):
        stacked = jnp.concatenate([current, wet_cells[None]], axis=0)
        padded = padded_2(stacked, (("atm", 1), ("ocn", 2)), 1)
        current = diffuse(padded[:levels], padded[levels], forcing, diffusivity)
    surface = jnp.einsum(
        "lc,lf->cf", current.reshape(levels, ocean_cells), surface_map, precision=highest
    ).astype(jnp.bfloat16)
    surface_padded = jnp.concatenate([surface, jnp.zeros((1, flux_width), jnp.bfloat16)], axis=0)
    back_rows = surface_padded[recv_cells]
    returned = lax.all_to_all(back_rows, "ocn", split_axis=0, concat_axis=0, tiled=True)
    returned_rows = returned[slot_index]
    contrib = cell_area[:, None] * returned_rows.astype(jnp.float32)
    surface_sum = jax.ops.segment_sum(contrib, xc_column, columns)
    surface_tend = jnp.einsum("vkf,cf->vkc", surface_weight, surface_sum, precision=highest)
    final_state = column_solve(inverses[0], diffused + surface_tend)
    return (final_state, current)


def solution(mesh):
    in_specs = (
        P(None, None, ("member", "atm", "ocn")),
        P("atm", None, None, None),
        P(),
        P(),
        P(),
        P(("atm", "ocn")),
        P(("atm", "ocn"), None),
        P(("atm", "ocn")),
        P(("atm", "ocn")),
        P(None, "atm", ("member", "ocn")),
        P("atm", "ocn"),
        P(),
        P(),
        P(),
    )
    out_specs = (P(None, None, ("member", "atm", "ocn")), P(None, "atm", ("member", "ocn")))
    return jax.shard_map(
        on_device, mesh=mesh, in_specs=in_specs, out_specs=out_specs, check_vma=False
    )
```

profile of v0, /device:TPU:0, one launch (start us, length us, event | category | flops | bytes accessed | tf_op | source)
XLA Modules:
  0.0 435.3 jit_solution(16953689737927741074)
XLA Ops:
  4.1 16.3 %scatter_custom_fusion = s32[12288]{0:T(1024)} fusion(s32[4096]{0:T(1024)S(1)} %bitcast.87, s32[4096]{0:T(1024)} %param.21, s32[]{:T(128)} %constant.13.clone.1), kind=kCustom, calls=%fused_computation.209 | custom fusion | bytes 49664 | tf_op jit(solution)/shard_map/scatter | solution.py:82
  20.4 5.2 %all-to-all-start = ((s32[4,3072,1]{1,2,0:T(1,128)}), s32[4,3072,1]{1,2,0:T(1,128)S(1)}, u32[]{:S(2)}, u32[]{:S(2)}) async-start(s32[4,3072,1]{1,2,0:T(1,128)} %bitcast.10), calls=%async_computation | async-start | bytes 98304 | tf_op jit(solution)/shard_map/all_to_all | solution.py:87
  25.6 2.1 fusion.11
  27.7 9.4 %fusion.3 = f32[4,137,2048]{2,1,0:T(8,128)S(1)} fusion(f32[4,137,2048]{2,0,1:T(4,128)} %param.14, f32[4,137,137]{2,0,1:T(4,128)S(1)} %bitcast.78), kind=kOutput, calls=%fused_computation.12 | convolution fusion | flops 1845067776 | bytes 9278736 | tf_op jit(solution)/shard_map/vkj,vjc->vkc/dot_general | solution.py:38
  37.2 8.7 %convolution_bitcast_fusion = f32[2048,128]{1,0:T(8,128)S(1)} fusion(f32[4,137,2048]{2,1,0:T(8,128)S(1)} %fusion.3, f32[4,137,128]{2,0,1:T(4,128)S(1)} %copy-done.17), kind=kOutput, calls=%fused_computation.35 | convolution fusion | flops 1723858944 | bytes 5818368 | tf_op jit(solution)/shard_map/vkc,vkf->cf/dot_general | solution.py:74
  46.0 26.2 %scatter_custom_fusion.1 = bf16[12288,128]{1,0:T(8,128)(2,1)} fusion(s32[4096]{0:T(1024)S(1)} %bitcast.88, bf16[]{:T(256)} %constant.38.clone.1, f32[4096]{0:T(1024)S(1)} %bitcast.85, f32[2048,128]{1,0:T(8,128)S(1)} %convolution_bitcast_fusion, s32[4096]{0:T(1024)S(1)} %fusion.154), kind=kCustom, calls=%fused_computation.44 | custom fusion | flops 1048576 | bytes 4227074 | tf_op jit(solution)/shard_map/scatter | solution.py:84
  72.2 4.8 %all-to-all-start.1 = ((bf16[4,3072,128]{2,1,0:T(8,128)(2,1)}), bf16[4,3072,128]{2,1,0:T(8,128)(2,1)}, u32[]{:S(2)}, u32[]{:S(2)}) async-start(bf16[4,3072,128]{2,1,0:T(8,128)(2,1)} %bitcast.72), calls=%async_computation.1 | async-start | bytes 6291456 | tf_op jit(solution)/shard_map/all_to_all | solution.py:86
  77.1 3.5 collective-permute-start
  82.2 4.2 collective-permute-done.1
  86.7 2.2 fusion.162
  89.0 1.9 copy.46
  90.9 3.9 collective-permute-start.2
  94.8 1.9 copy.47
  97.9 13.3 %collective-permute-done.2 = f32[76,34,1]{0,2,1:T(1,128)S(1)} collective-permute-done((f32[76,34,1]{0,2,1:T(1,128)S(1)}, f32[76,34,1]{0,2,1:T(1,128)S(1)}, u32[]{:S(2)}, u32[]{:S(2)}) %collective-permute-start.2) | collective-permute-done | bytes 10368 | tf_op jit(solution)/shard_map/ppermute | solution.py:19
  111.3 1.8 copy.48
  113.8 1.8 copy.49
  116.5 80.7 %scatter_custom_fusion.2 = f32[4097,128]{1,0:T(8,128)} fusion(s32[12288]{0:T(1024)S(1)} %bitcast.80, bf16[12288,128]{1,0:T(8,128)(2,1)} %bitcast.26, f32[]{:T(128)} %constant.12.clone.1), kind=kCustom, calls=%fused_computation.7 | custom fusion | flops 3145728 | bytes 5243396 | tf_op jit(solution)/shard_map/scatter-add | solution.py:89
  197.3 4.1 fusion.6
  203.2 2.6 fusion.31
  205.9 3.5 collective-permute-start.4
  211.1 4.2 collective-permute-done.5
  217.2 1.9 copy.54
  219.1 3.7 collective-permute-start.6
  225.4 4.3 collective-permute-done.7
  233.3 3.8 fusion.41
  237.2 3.5 collective-permute-start.8
  242.3 4.2 collective-permute-done.9
  246.8 2.1 fusion.160
  249.0 1.9 copy.60
  250.8 4.8 %collective-permute-start.10 = (f32[76,34,1]{0,2,1:T(1,128)S(1)}, f32[76,34,1]{0,2,1:T(1,128)S(1)}, u32[]{:S(2)}, u32[]{:S(2)}) collective-permute-start(f32[76,34,1]{0,2,1:T(1,128)S(1)} %copy.60), channel_id=1, source_target_pairs={{0,1},{1,2},{2,3},{4,5},{5,6},{6,7},{8,9},{9,10},{10,11},{12,13},{... | collective-permute-start | bytes 31016 | tf_op jit(solution)/shard_map/ppermute | solution.py:19
  255.7 1.9 copy.61
  258.9 1.8 copy.62
  260.7 2.5 collective-permute-done.11
  267.3 2.6 fusion.51
  270.0 3.5 collective-permute-start.12
  275.1 4.2 collective-permute-done.13
  281.2 1.9 copy.66
  285.0 4.8 %collective-permute-start.14 = (f32[76,34,1]{0,2,1:T(1,128)S(1)}, f32[76,34,1]{0,2,1:T(1,128)S(1)}, u32[]{:S(2)}, u32[]{:S(2)}) collective-permute-start(f32[76,34,1]{0,2,1:T(1,128)S(1)} %copy.66), channel_id=1, source_target_pairs={{0,1},{1,2},{2,3},{4,5},{5,6},{6,7},{8,9},{9,10},{10,11},{12,13},{... | collective-permute-start | bytes 31016 | tf_op jit(solution)/shard_map/ppermute | solution.py:19
  291.6 1.7 copy.69
  295.2 2.6 fusion.61
  299.7 3.5 convolution_convert_fusion
  303.2 43.7 %gather_fusion = bf16[12288,128]{1,0:T(8,128)(2,1)} fusion(bf16[4097,128]{1,0:T(8,128)(2,1)S(1)} %concatenate.115, s32[12288]{0:T(1024)S(1)} %broadcast_clamp_fusion), kind=kCustom, calls=%fused_computation.1 | custom fusion | bytes 6340608 | tf_op jit(solution)/shard_map/gather | solution.py:105
  347.0 4.8 %all-to-all-start.2 = ((bf16[4,3072,128]{2,1,0:T(8,128)(2,1)}), bf16[4,3072,128]{2,1,0:T(8,128)(2,1)S(1)}, u32[]{:S(2)}, u32[]{:S(2)}) async-start(bf16[4,3072,128]{2,1,0:T(8,128)(2,1)} %bitcast.74), calls=%async_computation.2 | async-start | bytes 6291456 | tf_op jit(solution)/shard_map/all_to_all | solution.py:106
  351.8 27.2 %all-to-all-done.2 = bf16[4,3072,128]{2,1,0:T(8,128)(2,1)S(1)} async-done(((bf16[4,3072,128]{2,1,0:T(8,128)(2,1)}), bf16[4,3072,128]{2,1,0:T(8,128)(2,1)S(1)}, u32[]{:S(2)}, u32[]{:S(2)}) %all-to-all-start.2) | async-done | bytes 3145760 | tf_op jit(solution)/shard_map/all_to_all | solution.py:106
  379.0 37.9 %scatter_custom_fusion.3 = f32[2048,128]{1,0:T(8,128)} fusion(s32[4096]{0:T(1024)S(1)} %copy-done.21, f32[4096]{0:T(1024)S(1)} %bitcast.86, f32[]{:T(128)} %constant.12.clone.1, bf16[12288,128]{1,0:T(8,128)(2,1)S(1)} %bitcast.73, s32[4096]{0:T(1024)S(1)} %broadcast_clamp_fusion.1), kind=kCustom, calls=%fused_computation.38 | custom fusion | flops 1572864 | bytes 4227076 | tf_op jit(solution)/shard_map/scatter-add | solution.py:109
  416.9 5.2 %fusion.115 = f32[2048,4,137]{0,2,1:T(8,128)S(1)} fusion(f32[2048,128]{1,0:T(8,128)} %scatter_custom_fusion.3, f32[4,137,128]{2,0,1:T(4,128)S(1)} %copy-done), kind=kOutput, calls=%fused_computation.152 | convolution fusion | flops 1723858944 | bytes 5818368 | tf_op jit(solution)/shard_map/vkf,cf->vkc/dot_general | solution.py:110
  422.1 7.7 %fusion.5 = f32[4,137,2048]{2,1,0:T(8,128)S(1)} fusion(f32[4,137,2048]{2,1,0:T(8,128)} %copy-done.1, f32[2048,4,137]{0,2,1:T(8,128)S(1)} %fusion.115, f32[4,137,137]{2,0,1:T(4,128)S(1)} %bitcast.79), kind=kOutput, calls=%fused_computation.18 | convolution fusion | flops 1846190080 | bytes 13767952 | tf_op jit(solution)/shard_map/vkj,vjc->vkc/dot_general | solution.py:38
  429.9 5.0 %copy.74 = f32[4,137,2048]{2,0,1:T(4,128)} copy(f32[4,137,2048]{2,1,0:T(8,128)S(1)} %fusion.5) | data formatting | bytes 8978432
  (107 shorter events, 38.2 us)
Async XLA Ops:
  0.6 416.3 %copy-start = (f32[4,137,128]{2,0,1:T(4,128)S(1)}, f32[4,137,128]{2,0,1:T(4,128)}, u32[]{:S(2)}) copy-start(f32[4,137,128]{2,0,1:T(4,128)} %param.17) | copy-start | bytes 841732
  0.6 27.1 %copy-start.15 = (f32[1,4,137,137]{3,1,2,0:T(4,128)S(1)}, f32[1,4,137,137]{3,1,2,0:T(4,128)}, u32[]{:S(2)}) copy-start(f32[1,4,137,137]{3,1,2,0:T(4,128)} %param.15) | copy-start | bytes 900916
  20.4 51.8 %all-to-all-start = ((s32[4,3072,1]{1,2,0:T(1,128)}), s32[4,3072,1]{1,2,0:T(1,128)S(1)}, u32[]{:S(2)}, u32[]{:S(2)}) async-start(s32[4,3072,1]{1,2,0:T(1,128)} %bitcast.10), calls=%async_computation | async-start | bytes 98304 | tf_op jit(solution)/shard_map/all_to_all | solution.py:87
  27.7 9.5 %copy-start.17 = (f32[4,137,128]{2,0,1:T(4,128)S(1)}, f32[4,137,128]{2,0,1:T(4,128)}, u32[]{:S(2)}) copy-start(f32[4,137,128]{2,0,1:T(4,128)} %param.16) | copy-start | bytes 841732
  37.2 8.8 %copy-start.1 = (f32[4,137,2048]{2,1,0:T(8,128)}, f32[4,137,2048]{2,1,0:T(8,128)S(1)}, u32[]{:S(2)}) copy-start(f32[4,137,2048]{2,1,0:T(8,128)S(1)} %fusion.3) | copy-start | bytes 13467652
  37.2 8.8 %copy-start.21 = (s32[4096]{0:T(1024)S(1)}, s32[4096]{0:T(1024)}, u32[]{:S(2)}) copy-start(s32[4096]{0:T(1024)} %param.19) | copy-start | bytes 49156
  72.2 4.8 %copy-start.20 = (s32[32,128]{1,0:T(8,128)S(1)}, s32[32,128]{1,0:T(8,128)}, u32[]{:S(2)}) copy-start(s32[32,128]{1,0:T(8,128)} %param.24) | copy-start | bytes 49156
  72.2 4.9 %copy-start.6 = (f32[75,32,128]{2,1,0:T(8,128)S(1)}, f32[75,32,128]{2,1,0:T(8,128)}, u32[]{:S(2)}) copy-start(f32[75,32,128]{2,1,0:T(8,128)} %param.23) | copy-start | bytes 3686404
  72.2 44.3 %all-to-all-start.1 = ((bf16[4,3072,128]{2,1,0:T(8,128)(2,1)}), bf16[4,3072,128]{2,1,0:T(8,128)(2,1)}, u32[]{:S(2)}, u32[]{:S(2)}) async-start(bf16[4,3072,128]{2,1,0:T(8,128)(2,1)} %bitcast.72), calls=%async_computation.1 | async-start | bytes 6291456 | tf_op jit(solution)/shard_map/all_to_all | solution.py:86
  77.1 5.1 %collective-permute-start = (f32[76,1,128]{2,1,0:T(1,128)S(1)}, f32[76,1,128]{2,1,0:T(1,128)S(1)}, u32[]{:S(2)}, u32[]{:S(2)}) collective-permute-start(f32[76,1,128]{2,1,0:T(1,128)S(1)} %get-tuple-element.10), channel_id=1, source_target_pairs={{0,4},{4,8},{8,12},{1,5},{5,9},{9,13},{2,6},{6,10},{10,14},{3,7},{... | collective-permute-start | bytes 116744 | tf_op jit(solution)/shard_map/ppermute | solution.py:19
  80.6 5.9 %collective-permute-start.1 = (f32[76,1,128]{2,1,0:T(1,128)S(1)}, f32[76,1,128]{2,1,0:T(1,128)S(1)}, u32[]{:S(2)}, u32[]{:S(2)}) collective-permute-start(f32[76,1,128]{2,1,0:T(1,128)S(1)} %get-tuple-element.20), channel_id=1, source_target_pairs={{4,0},{8,4},{12,8},{5,1},{9,5},{13,9},{6,2},{10,6},{14,10},{7,3},{... | collective-permute-start | bytes 116744 | tf_op jit(solution)/shard_map/ppermute | solution.py:20
  90.9 20.4 %collective-permute-start.2 = (f32[76,34,1]{0,2,1:T(1,128)S(1)}, f32[76,34,1]{0,2,1:T(1,128)S(1)}, u32[]{:S(2)}, u32[]{:S(2)}) collective-permute-start(f32[76,34,1]{0,2,1:T(1,128)S(1)} %copy.46), channel_id=1, source_target_pairs={{0,1},{1,2},{2,3},{4,5},{5,6},{6,7},{8,9},{9,10},{10,11},{12,13},{... | collective-permute-start | bytes 31016 | tf_op jit(solution)/shard_map/ppermute | solution.py:19
  96.6 17.2 %collective-permute-start.3 = (f32[76,34,1]{0,2,1:T(1,128)S(1)}, f32[76,34,1]{0,2,1:T(1,128)S(1)}, u32[]{:S(2)}, u32[]{:S(2)}) collective-permute-start(f32[76,34,1]{0,2,1:T(1,128)S(1)} %copy.47), channel_id=1, source_target_pairs={{1,0},{2,1},{3,2},{5,4},{6,5},{7,6},{9,8},{10,9},{11,10},{13,12},{... | collective-permute-start | bytes 31016 | tf_op jit(solution)/shard_map/ppermute | solution.py:20
  116.5 80.8 %copy-start.18 = (f32[75,128]{1,0:T(8,128)S(1)}, f32[75,128]{1,0:T(8,128)}, u32[]{:S(2)}) copy-start(f32[75,128]{1,0:T(8,128)} %param.25) | copy-start | bytes 115204
  197.3 4.3 copy-start.8
  201.3 1.9 copy-start.7
  201.3 1.9 copy-start.22
  201.6 4.3 copy-start.2
  205.9 5.1 %collective-permute-start.4 = (f32[76,1,128]{2,1,0:T(1,128)S(1)}, f32[76,1,128]{2,1,0:T(1,128)S(1)}, u32[]{:S(2)}, u32[]{:S(2)}) collective-permute-start(f32[76,1,128]{2,1,0:T(1,128)S(1)} %get-tuple-element.25), channel_id=1, source_target_pairs={{0,4},{4,8},{8,12},{1,5},{5,9},{9,13},{2,6},{6,10},{10,14},{3,7},{... | collective-permute-start | bytes 116744 | tf_op jit(solution)/shard_map/ppermute | solution.py:19
  209.4 5.9 %collective-permute-start.5 = (f32[76,1,128]{2,1,0:T(1,128)S(1)}, f32[76,1,128]{2,1,0:T(1,128)S(1)}, u32[]{:S(2)}, u32[]{:S(2)}) collective-permute-start(f32[76,1,128]{2,1,0:T(1,128)S(1)} %get-tuple-element.26), channel_id=1, source_target_pairs={{4,0},{8,4},{12,8},{5,1},{9,5},{13,9},{6,2},{10,6},{14,10},{7,3},{... | collective-permute-start | bytes 116744 | tf_op jit(solution)/shard_map/ppermute | solution.py:20
  219.1 5.7 %collective-permute-start.6 = (f32[76,34,1]{0,2,1:T(1,128)S(1)}, f32[76,34,1]{0,2,1:T(1,128)S(1)}, u32[]{:S(2)}, u32[]{:S(2)}) collective-permute-start(f32[76,34,1]{0,2,1:T(1,128)S(1)} %copy.54), channel_id=1, source_target_pairs={{0,1},{1,2},{2,3},{4,5},{5,6},{6,7},{8,9},{9,10},{10,11},{12,13},{... | collective-permute-start | bytes 31016 | tf_op jit(solution)/shard_map/ppermute | solution.py:19
  223.3 6.5 %collective-permute-start.7 = (f32[76,34,1]{0,2,1:T(1,128)S(1)}, f32[76,34,1]{0,2,1:T(1,128)S(1)}, u32[]{:S(2)}, u32[]{:S(2)}) collective-permute-start(f32[76,34,1]{0,2,1:T(1,128)S(1)} %copy.55), channel_id=1, source_target_pairs={{1,0},{2,1},{3,2},{5,4},{6,5},{7,6},{9,8},{10,9},{11,10},{13,12},{... | collective-permute-start | bytes 31016 | tf_op jit(solution)/shard_map/ppermute | solution.py:20
  225.4 7.1 %copy-start.9 = (f32[76,34,1]{2,1,0:T(8,128)}, f32[76,34,1]{2,1,0:T(8,128)S(1)}, u32[]{:S(2)}) copy-start(f32[76,34,1]{2,1,0:T(8,128)S(1)} %copy.56) | copy-start | bytes 31012
  231.5 1.3 copy-start.3
  231.5 1.8 copy-start.12
  237.2 5.1 %collective-permute-start.8 = (f32[76,1,128]{2,1,0:T(1,128)S(1)}, f32[76,1,128]{2,1,0:T(1,128)S(1)}, u32[]{:S(2)}, u32[]{:S(2)}) collective-permute-start(f32[76,1,128]{2,1,0:T(1,128)S(1)} %get-tuple-element.23), channel_id=1, source_target_pairs={{0,4},{4,8},{8,12},{1,5},{5,9},{9,13},{2,6},{6,10},{10,14},{3,7},{... | collective-permute-start | bytes 116744 | tf_op jit(solution)/shard_map/ppermute | solution.py:19
  240.7 5.9 %collective-permute-start.9 = (f32[76,1,128]{2,1,0:T(1,128)S(1)}, f32[76,1,128]{2,1,0:T(1,128)S(1)}, u32[]{:S(2)}, u32[]{:S(2)}) collective-permute-start(f32[76,1,128]{2,1,0:T(1,128)S(1)} %get-tuple-element.24), channel_id=1, source_target_pairs={{4,0},{8,4},{12,8},{5,1},{9,5},{13,9},{6,2},{10,6},{14,10},{7,3},{... | collective-permute-start | bytes 116744 | tf_op jit(solution)/shard_map/ppermute | solution.py:20
  250.8 8.0 %collective-permute-start.10 = (f32[76,34,1]{0,2,1:T(1,128)S(1)}, f32[76,34,1]{0,2,1:T(1,128)S(1)}, u32[]{:S(2)}, u32[]{:S(2)}) collective-permute-start(f32[76,34,1]{0,2,1:T(1,128)S(1)} %copy.60), channel_id=1, source_target_pairs={{0,1},{1,2},{2,3},{4,5},{5,6},{6,7},{8,9},{9,10},{10,11},{12,13},{... | collective-permute-start | bytes 31016 | tf_op jit(solution)/shard_map/ppermute | solution.py:19
  257.6 5.6 %collective-permute-start.11 = (f32[76,34,1]{0,2,1:T(1,128)S(1)}, f32[76,34,1]{0,2,1:T(1,128)S(1)}, u32[]{:S(2)}, u32[]{:S(2)}) collective-permute-start(f32[76,34,1]{0,2,1:T(1,128)S(1)} %copy.61), channel_id=1, source_target_pairs={{1,0},{2,1},{3,2},{5,4},{6,5},{7,6},{9,8},{10,9},{11,10},{13,12},{... | collective-permute-start | bytes 31016 | tf_op jit(solution)/shard_map/ppermute | solution.py:20
  265.0 1.3 copy-start.4
  265.0 1.8 copy-start.10
  265.0 2.3 copy-start.13
  270.0 5.1 %collective-permute-start.12 = (f32[76,1,128]{2,1,0:T(1,128)S(1)}, f32[76,1,128]{2,1,0:T(1,128)S(1)}, u32[]{:S(2)}, u32[]{:S(2)}) collective-permute-start(f32[76,1,128]{2,1,0:T(1,128)S(1)} %get-tuple-element.21), channel_id=1, source_target_pairs={{0,4},{4,8},{8,12},{1,5},{5,9},{9,13},{2,6},{6,10},{10,14},{3,7},{... | collective-permute-start | bytes 116744 | tf_op jit(solution)/shard_map/ppermute | solution.py:19
  273.5 5.9 %collective-permute-start.13 = (f32[76,1,128]{2,1,0:T(1,128)S(1)}, f32[76,1,128]{2,1,0:T(1,128)S(1)}, u32[]{:S(2)}, u32[]{:S(2)}) collective-permute-start(f32[76,1,128]{2,1,0:T(1,128)S(1)} %get-tuple-element.22), channel_id=1, source_target_pairs={{4,0},{8,4},{12,8},{5,1},{9,5},{13,9},{6,2},{10,6},{14,10},{7,3},{... | collective-permute-start | bytes 116744 | tf_op jit(solution)/shard_map/ppermute | solution.py:20
  283.6 8.0 %collective-permute-start.15 = (f32[76,34,1]{0,2,1:T(1,128)S(1)}, f32[76,34,1]{0,2,1:T(1,128)S(1)}, u32[]{:S(2)}, u32[]{:S(2)}) collective-permute-start(f32[76,34,1]{0,2,1:T(1,128)S(1)} %copy.67), channel_id=1, source_target_pairs={{1,0},{2,1},{3,2},{5,4},{6,5},{7,6},{9,8},{10,9},{11,10},{13,12},{... | collective-permute-start | bytes 31016 | tf_op jit(solution)/shard_map/ppermute | solution.py:20
  285.0 6.0 %collective-permute-start.14 = (f32[76,34,1]{0,2,1:T(1,128)S(1)}, f32[76,34,1]{0,2,1:T(1,128)S(1)}, u32[]{:S(2)}, u32[]{:S(2)}) collective-permute-start(f32[76,34,1]{0,2,1:T(1,128)S(1)} %copy.66), channel_id=1, source_target_pairs={{0,1},{1,2},{2,3},{4,5},{5,6},{6,7},{8,9},{9,10},{10,11},{12,13},{... | collective-permute-start | bytes 31016 | tf_op jit(solution)/shard_map/ppermute | solution.py:19
  293.4 1.3 copy-start.5
  293.4 1.8 copy-start.11
  297.8 1.0 copy-start.14
  298.9 0.8 copy-start.19
  347.0 32.0 %all-to-all-start.2 = ((bf16[4,3072,128]{2,1,0:T(8,128)(2,1)}), bf16[4,3072,128]{2,1,0:T(8,128)(2,1)S(1)}, u32[]{:S(2)}, u32[]{:S(2)}) async-start(bf16[4,3072,128]{2,1,0:T(8,128)(2,1)} %bitcast.74), calls=%async_computation.2 | async-start | bytes 6291456 | tf_op jit(solution)/shard_map/all_to_all | solution.py:106
  416.9 5.2 %copy-start.16 = (f32[1,4,137,137]{3,1,2,0:T(4,128)S(1)}, f32[1,4,137,137]{3,1,2,0:T(4,128)}, u32[]{:S(2)}) copy-start(f32[1,4,137,137]{3,1,2,0:T(4,128)} %param.15) | copy-start | bytes 900916
where the time goes:
time: 441 us; the launch traced here: 435 us
  other arithmetic  165 us (37%)
  local copies, waits for them, and re-layouts  104 us (24%)
  waiting for transfers between devices  67.5 us (15%)
  starting transfers between devices  56.4 us (13%)
  matrix products  40.8 us (9%)
    scatter-add x1, other arithmetic, on_device(): jax.ops.segment_sum(received.astype(jnp.float32), recv_cells, ocean_cells...  80.7 us
    gather x1, local copies, waits for them, and re-layouts, on_device(): back_rows = surface_padded[recv_cells]  43.7 us
    scatter-add x1, other arithmetic, on_device(): surface_sum = jax.ops.segment_sum(contrib, xc_column, columns)  37.9 us
    ppermute x8, starting transfers between devices, padded_2(): before = lax.ppermute(last, axis, up)  31.1 us
    all_to_all x1, waiting for transfers between devices, on_device(): lax.all_to_all(back_rows, 'ocn', split_axis=0, concat_axis=0, tiled=True)  27.2 us
    scatter x1, other arithmetic, on_device(): jnp.zeros((slot_total, flux_width), jnp.bfloat16).at[slot_index]  26.2 us
    ppermute x8, waiting for transfers between devices, padded_2(): after = lax.ppermute(leading, axis, down)  24.5 us
    dot_general x2, matrix products, column_solve(): jnp.einsum('vkj,vjc->vkc', inverse_set, column_field, precision=highest)  17.2 us
  transfers between devices with their start and end apart: 19, of which 14 were waited for; matrix products, arithmetic and copies ran while one was open for 14% of the time, Pallas kernels for 0%

commit v1 on v0

v1 whole, which is shorter than its diff:
```python
import functools
import jax
import jax.numpy as jnp
from jax import lax
from jax.experimental import pallas as pl
from jax.experimental.pallas import tpu as pltpu
from jax.sharding import PartitionSpec as P

OSTEPS = 4
OY = 32
OX = 128
OCELLS = OY * OX
STRIPS = 8
f32 = jnp.float32
bf16 = jnp.bfloat16
i32 = jnp.int32


def nn(a, b):
    return jnp.dot(a, b, preferred_element_type=f32)


def nt(a, b):
    return lax.dot_general(a, b, (((1,), (1,)), ((), ())), preferred_element_type=f32)


def split(x):
    high = x.astype(bf16)
    return high, (x - high.astype(f32)).astype(bf16)


def three(dot, a, b):
    ah, al = split(a)
    bh, bl = split(b)
    return dot(ah, bh) + dot(ah, bl) + dot(al, bh)


def iota(shape, dim):
    return lax.broadcasted_iota(i32, shape, dim)


def flat(x):
    return jnp.concatenate([x[i : i + 1, :] for i in range(x.shape[0])], axis=1)


def onehot(row, size):
    return jnp.where(iota((size, row.shape[1]), 0) == row, 1.0, 0.0).astype(bf16)


def place(high, low, payloads, rows):
    lines = iota((rows, high.shape[1]), 0) == high
    left = jnp.concatenate([jnp.where(lines, p, 0.0) for p in payloads], axis=0).astype(bf16)
    out = nt(left, onehot(low, 128))
    return [out[i * rows : (i + 1) * rows] for i in range(len(payloads))]


def stacked(x):
    return jnp.concatenate([x[:, h : h + 256] for h in range(0, x.shape[1], 256)], axis=0)


def gather(source, low, high, width, chunk=512):
    count = source.shape[0] // width
    outs = []
    for start in range(0, low.shape[1], chunk):
        stop = min(start + chunk, low.shape[1])
        part = nn(source, onehot(low[:, start:stop], 256))
        hc = high[:, start:stop]
        total = jnp.where(hc == 0, part[:width], 0.0)
        for h in range(1, count):
            total = jnp.where(hc == h, part[h * width : (h + 1) * width], total)
        outs.append(total)
    return outs[0] if len(outs) == 1 else jnp.concatenate(outs, axis=1)


def pick(level_rows, lane_rows, base):
    index = iota(level_rows.shape, 0)
    for i, row in enumerate(lane_rows):
        level_rows = jnp.where(index == base + i, row, level_rows)
    return level_rows


def roll(x, shift):
    shift = shift % 128
    return x if shift == 0 else pltpu.roll(x, shift, 1)


def row_of(x, y):
    return x[:, y * OX : (y + 1) * OX]


def border_block(x, lane):
    blocks = []
    for i in range(2):
        block = jnp.zeros((x.shape[0], OX), f32)
        for b in range(4):
            for j in range(4):
                first = b * 32 + j * 8
                moved = roll(row_of(x, b * 8 + i * 4 + j), first + 4)
                block = jnp.where((lane >= first) & (lane < first + 8), moved, block)
        blocks.append(block)
    return jnp.concatenate(blocks, axis=1)


def strips(x, halo, lane):
    outs = []
    for j in range(STRIPS):
        side = roll(row_of(halo, j // 4), 8 - (j % 4) * 8)
        for b in range(4):
            line = row_of(x, b * 8 + j)
            first = b * 32
            side = jnp.where((lane >= first) & (lane < first + 8), roll(line, first + 8), side)
            side = jnp.where(
                (lane >= first + 16) & (lane < first + 24), roll(line, first + 16), side
            )
        outs.append(side)
    return outs


def send_kernel(
    peers, levels, width, borders,
    area_ref, col_ref, dest_ref, cell_ref, class_ref, inv_ref, flux_ref, fw_ref, state_ref,
    tracer_ref, land_ref,
    packed_ref, *rest,
):
    side_refs = rest[: len(borders)]
    forcing_ref, t_ref, omap_ref, oarea_ref, smap_ref, sarea_ref, fw_pad = rest[len(borders) :]
    me = lax.axis_index("ocn")
    slots = packed_ref.shape[1]
    slot_rows = slots // 128
    slot_pad = -(-slot_rows // 8) * 8
    lines = col_ref.shape[0]
    lane = iota((1, 128), 1)

    offset = (dest_ref[...] - me) & (peers - 1)
    cells = cell_ref[...]
    classes = class_ref[...]
    cols = col_ref[...]
    area = jnp.zeros(cols.shape, f32)
    for i in range(area_ref.shape[0]):
        area = jnp.where(classes == i, area_ref[i], area)

    hits = [jnp.where(offset == k, 1.0, 0.0) for k in range(1, peers)]
    hot = jnp.concatenate(hits, axis=0)
    upper = jnp.where(iota((128, 128), 0) <= iota((128, 128), 1), 1.0, 0.0).astype(bf16)
    running = nn(hot.astype(bf16), upper)
    count = running.shape[0]
    totals = jnp.broadcast_to(running[:, 127:128], running.shape).astype(bf16)
    below = jnp.where(iota((count, count), 1) < iota((count, count), 0), 1.0, 0.0).astype(bf16)
    before = nn(below, totals)
    place_of = running + before - 1.0
    slot = jnp.full(cols.shape, -1.0, f32)
    for k in range(1, peers):
        at = (k - 1) * lines
        slot = jnp.where(offset == k, place_of[at : at + lines], slot)
    slot = slot.astype(i32)
    position = iota((slot_pad, 128), 0) * 128 + iota((slot_pad, 128), 1)
    segment = jnp.full((slot_pad, 128), 1, i32)
    for k in range(2, peers):
        at = (k - 1) * lines
        start = before[at : at + 1, :].astype(i32)
        segment = segment + jnp.where(position >= start, 1, 0)

    a1 = area.astype(bf16).astype(f32)
    a2 = (area - a1).astype(bf16).astype(f32)
    a3 = area - a1 - a2
    slot_f, cell_f = flat(slot), flat(cells)
    col_f = flat(cols)
    areas = [flat(a1), flat(a2), flat(a3)]
    col_low = (col_f & 255).astype(f32)
    col_high = lax.shift_right_arithmetic(col_f, 8).astype(f32)
    cell_low = cell_f & 127
    cell_high = lax.shift_right_arithmetic(cell_f, 7)
    got = place(
        lax.shift_right_arithmetic(slot_f, 7), slot_f & 127,
        [col_low, col_high] + areas + [cell_high.astype(f32), cell_low.astype(f32)], slot_pad,
    )
    keep = [flat(g[:slot_rows]) for g in got]
    s_low, s_high = keep[0].astype(i32), keep[1].astype(i32)
    s_area = keep[2] + keep[3] + keep[4]
    smap_ref[0:1, :] = s_low
    smap_ref[1:2, :] = s_high
    smap_ref[2:3, :] = flat(segment[:slot_rows])
    sarea_ref[...] = s_area

    local_high = jnp.where(flat(offset) == 0, cell_high, -1)
    own = place(local_high, cell_low, [col_low, col_high + 1.0] + areas, OY)
    o_low, o_high = own[0].astype(i32), own[1].astype(i32) - 1
    o_area = own[2] + own[3] + own[4]
    omap_ref[0:1, :] = flat(o_low)
    omap_ref[1:2, :] = flat(o_high)
    oarea_ref[...] = flat(o_area)

    blank = jnp.zeros((2, 128), f32)
    edge = []
    for m in (own[0], own[1], o_area):
        block = blank
        for b in range(4):
            part = m[b * 8 : (b + 1) * 8]
            for j in range(4):
                first = b * 32 + j * 8
                moved = roll(part, first + 4)
                pair = jnp.concatenate([moved[j : j + 1], moved[4 + j : 5 + j]], axis=0)
                block = jnp.where((lane >= first) & (lane < first + 8), pair, block)
        edge.append(flat(block))

    fw_pad[...] = jnp.zeros_like(fw_pad)
    fw_pad[0:levels, :] = fw_ref[...]
    fw = fw_pad[...]
    forcing = None
    for v in range(flux_ref.shape[0]):
        pulled = three(nn, three(nt, fw, flux_ref[v]), inv_ref[0, v])
        term = three(nn, pulled, state_ref[v])
        forcing = term if forcing is None else forcing + term
    forcing = forcing.astype(bf16)
    forcing_ref[...] = forcing
    source = stacked(forcing)

    for y in range(OY):
        at = pl.ds(y * OX, OX)
        t_ref[0:levels, at] = tracer_ref[pl.ds(y, levels, stride=OY), :]
        t_ref[levels : levels + 1, at] = land_ref[y : y + 1, :].astype(f32)
        t_ref[levels + 1 : width, at] = jnp.zeros((width - levels - 1, OX), f32)

    rows = gather(source, s_low, s_high, width) * s_area
    rows = pick(rows, keep[5:7], levels + 1).astype(bf16)
    packed_ref[...] = rows
    f_edge = gather(source, edge[0].astype(i32), edge[1].astype(i32) - 1, width) * edge[2]
    t_edge = border_block(t_ref[...], lane)
    lead = (lane & 7) < 4
    to_right, to_left = [], []
    for i in range(2):
        fe, te = row_of(f_edge, i), row_of(t_edge, i)
        to_right.append(jnp.where(lead, fe, roll(te, 4)))
        to_left.append(jnp.where(lead, roll(fe, -4), te))
    to_right = jnp.concatenate(to_right, axis=1)
    to_left = jnp.concatenate(to_left, axis=1)
    for mask, ref in zip(borders, side_refs):
        ref[:, 0:slots] = rows
        ref[:, slots : slots + 256] = jnp.where((me ^ mask) == me + 1, to_right, to_left).astype(
            bf16
        )


def local_kernel(width, forcing_ref, omap_ref, oarea_ref, out_ref):
    source = stacked(forcing_ref[...])
    out_ref[...] = gather(source, omap_ref[0:1, :], omap_ref[1:2, :], width) * oarea_ref[...]


def receive_kernel(peers, levels, width, borders, packed_ref, smap_ref, local_ref, t_ref, *rest):
    got = rest[: peers - 1]
    f_ref, fs_ref, ts_ref, cmap_ref, even_ref, odd_ref = rest[peers - 1 :]
    me = lax.axis_index("ocn")
    slots = packed_ref.shape[1]
    lane = iota((1, 128), 1)
    segment = smap_ref[2:3, :]
    chunks = slots // 256

    def meant_for(tile):
        total = jnp.zeros((width, slots), f32)
        for mask in range(peers):
            ref = packed_ref if mask == 0 else got[mask - 1]
            step = (tile - (me ^ mask)) & (peers - 1)
            total = jnp.where(segment == step, ref[:, 0:slots].astype(f32), total)
        high = total[levels + 1 : levels + 2, :].astype(i32)
        low = total[levels + 2 : levels + 3, :].astype(i32)
        return stacked(total.astype(bf16)), high, low

    index = iota((1, slots), 1)
    payload = [(index & 255).astype(f32), (lax.shift_right_arithmetic(index, 8) + 1).astype(f32)]

    source, high, low = meant_for(me)
    cell = high * 128 + low
    cmap_ref[0:1, :] = cell & 255
    cmap_ref[1:2, :] = lax.shift_right_arithmetic(cell, 8)
    where_low, where_high = place(high, low, payload, OY)
    f_ref[...] = local_ref[...] + gather(
        source, flat(where_low).astype(i32), flat(where_high).astype(i32) - 1, width
    )

    halo_f = None
    for step in (-1, 1):
        source, high, low = meant_for(me + step)
        at = low - 120 if step < 0 else low
        inside = (low >= 124) if step < 0 else (low < 4)
        block = lax.shift_right_arithmetic(high & 7, 2)
        spot = lax.shift_right_arithmetic(high, 3) * 32 + (high & 3) * 8 + at
        where_low, where_high = place(jnp.where(inside, block, -1), spot, payload, 8)
        part = gather(
            source, flat(where_low[:2]).astype(i32), flat(where_high[:2]).astype(i32) - 1, width
        )
        halo_f = part if halo_f is None else halo_f + part

    def side_from(tile):
        block = jnp.zeros((width, 256), f32)
        for mask in borders:
            block = jnp.where(
                (me ^ mask) == tile, got[mask - 1][:, slots : slots + 256].astype(f32), block
            )
        return block

    from_left, from_right = side_from(me - 1), side_from(me + 1)
    lead = (lane & 7) < 4
    side_f, side_t = [], []
    for i in range(2):
        fl, fr = row_of(from_left, i), row_of(from_right, i)
        side_f.append(jnp.where(lead, fr, roll(fl, 4)) + row_of(halo_f, i))
        side_t.append(jnp.where(lead, roll(fr, -4), fl))
    f_strips = strips(f_ref[...], jnp.concatenate(side_f, axis=1), lane)
    t_strips = strips(t_ref[...], jnp.concatenate(side_t, axis=1), lane)
    for j in range(STRIPS):
        fs_ref[:, j * OX : (j + 1) * OX] = f_strips[j]
        ts_ref[:, j * OX : (j + 1) * OX] = t_strips[j]

    def corner(parts, top):
        block = jnp.zeros((width, OX), f32)
        for m in range(4):
            inside = (lane >= m * 32) & (lane < m * 32 + 32)
            moved = roll(parts[m], 32 * m) if top else roll(parts[4 + m], 32 * (m - 3))
            block = jnp.where(inside, moved, block)
        return block

    top = jnp.concatenate(
        [f_ref[:, 0 : 3 * OX], corner(f_strips, True), t_ref[:, 0 : 4 * OX],
         corner(t_strips, True)], axis=1,
    )
    bottom = jnp.concatenate(
        [f_ref[:, 29 * OX : 32 * OX], corner(f_strips, False), t_ref[:, 28 * OX : 32 * OX],
         corner(t_strips, False)], axis=1,
    )
    is_even = (lax.axis_index("atm") & 1) == 0
    even_ref[...] = jnp.where(is_even, bottom, top).astype(bf16)
    odd_ref[...] = jnp.where(is_even, top, bottom).astype(bf16)


def ocean_kernel(
    levels, width,
    f_ref, fs_ref, t_ref, ts_ref, even_ref, odd_ref, dif_ref, cmap_ref,
    out_ref, tt_ref, back_ref,
    s, fx, ss, fsx, w8, n8, ws8, ns8, d8,
):
    row = lax.axis_index("atm")
    me = lax.axis_index("ocn")
    rows_atm = lax.axis_size("atm")
    peers = lax.axis_size("ocn")
    is_even = (row & 1) == 0
    lane = iota((1, 128), 1)
    block = lax.shift_right_arithmetic(lane, 5)
    even, odd = even_ref[...].astype(f32), odd_ref[...].astype(f32)
    top = jnp.where(is_even, odd, even)
    bottom = jnp.where(is_even, even, odd)
    spot = lane & 31
    outside = ((me == 0) & (spot >= 12) & (spot < 16)) | (
        (me == peers - 1) & (spot >= 8) & (spot < 12)
    )
    top_wet = jnp.where(row > 0, top[levels : levels + 1, 512:1152], 0.0)
    bottom_wet = jnp.where(row < rows_atm - 1, bottom[levels : levels + 1, 512:1152], 0.0)
    main_wet = t_ref[levels : levels + 1, :]
    rows_all = OY + 8
    w8[:, 0 : 4 * OX] = jnp.broadcast_to(top_wet[:, 0:512], (8, 512))
    w8[:, 4 * OX : 36 * OX] = jnp.broadcast_to(main_wet, (8, OCELLS))
    w8[:, 36 * OX : 40 * OX] = jnp.broadcast_to(bottom_wet[:, 0:512], (8, 512))
    for j in range(STRIPS + 2):
        if j == 0:
            line = top_wet[:, 512:640]
        elif j == STRIPS + 1:
            line = bottom_wet[:, 512:640]
        else:
            line = ts_ref[levels : levels + 1, (j - 1) * OX : j * OX]
        ws8[:, j * OX : (j + 1) * OX] = jnp.broadcast_to(jnp.where(outside, 0.0, line), (8, OX))

    def at(ref, y):
        return ref[:, y * OX : (y + 1) * OX]

    def ends(parts, j):
        if j == 0:
            return roll(parts[0], 32), roll(jnp.where(block == 0, parts[1], parts[0]), 96)
        if j == 1:
            return roll(jnp.where(block == 3, parts[0], parts[STRIPS]), 32), parts[2]
        if j == STRIPS:
            return parts[STRIPS - 1], roll(
                jnp.where(block == 0, parts[STRIPS + 1], parts[1]), 96
            )
        if j == STRIPS + 1:
            return roll(jnp.where(block == 3, parts[STRIPS], parts[j]), 32), roll(parts[j], 96)
        return parts[j - 1], parts[j + 1]

    for y in range(1, rows_all - 1):
        here = at(w8, y)
        n8[:, y * OX : (y + 1) * OX] = (
            at(w8, y - 1) + at(w8, y + 1) + roll(here, 1) + roll(here, -1)
        )
    parts = [at(ws8, j) for j in range(STRIPS + 2)]
    for j in range(STRIPS + 2):
        up, down = ends(parts, j)
        ns8[:, j * OX : (j + 1) * OX] = up + down + roll(parts[j], 1) + roll(parts[j], -1)

    diag = iota((width, levels), 0) == iota((width, levels), 1)
    column = jnp.sum(jnp.where(diag, dif_ref[...], 0.0), axis=1, keepdims=True)
    d8[...] = jnp.broadcast_to(column, (width, OX))

    fx[:, OX : 4 * OX] = top[:, 0:384]
    fx[:, 4 * OX : 36 * OX] = f_ref[...]
    fx[:, 36 * OX : 39 * OX] = bottom[:, 0:384]
    fsx[:, 0:OX] = top[:, 384:512]
    fsx[:, OX : 9 * OX] = fs_ref[...]
    fsx[:, 9 * OX : 10 * OX] = bottom[:, 384:512]
    s[:, 0 : 4 * OX] = top[:, 512:1024] * w8[0:1, 0 : 4 * OX]
    s[:, 4 * OX : 36 * OX] = t_ref[...] * w8[0:1, 4 * OX : 36 * OX]
    s[:, 36 * OX : 40 * OX] = bottom[:, 512:1024] * w8[0:1, 36 * OX : 40 * OX]
    ss[:, 0:OX] = top[:, 1024:1152] * ws8[0:1, 0:OX]
    ss[:, OX : 9 * OX] = ts_ref[...] * ws8[0:1, OX : 9 * OX]
    ss[:, 9 * OX : 10 * OX] = bottom[:, 1024:1152] * ws8[0:1, 9 * OX : 10 * OX]

    def group(g, carry):
        lev = pl.ds(pl.multiple_of(g * 8, 8), 8)

        def load(ref, y):
            return ref[lev, y * OX : (y + 1) * OX]

        dif = d8[lev, :]
        for step in range(OSTEPS):
            before, here = load(s, step), load(s, step + 1)
            for y in range(step + 1, rows_all - 1 - step):
                after = load(s, y + 1)
                lap = before + after + roll(here, 1) + roll(here, -1) - at(n8, y) * here
                s[lev, y * OX : (y + 1) * OX] = here + at(w8, y) * (dif * lap + load(fx, y))
                before, here = here, after
        now = [load(ss, j) for j in range(STRIPS + 2)]
        for step in range(OSTEPS):
            new = []
            for j in range(STRIPS + 2):
                up, down = ends(now, j)
                here = now[j]
                lap = up + down + roll(here, 1) + roll(here, -1) - at(ns8, j) * here
                new.append(here + at(ws8, j) * (dif * lap + load(fsx, j)))
            now = new
        for y in range(OY):
            b, j = y // 8, y % 8
            line = now[j + 1]
            value = load(s, y + 4)
            value = jnp.where(lane < 4, roll(line, -(b * 32 + 16)), value)
            value = jnp.where(lane >= 124, roll(line, 120 - b * 32), value)
            tt_ref[lev, y * OX : (y + 1) * OX] = jnp.where(
                at(w8, y + 4) > 0.0, value, load(t_ref, y)
            )
        return carry

    lax.fori_loop(0, width // 8, group, 0)
    for y in range(OY):
        out_ref[pl.ds(y, levels, stride=OY), :] = tt_ref[0:levels, y * OX : (y + 1) * OX]
    source = stacked(tt_ref[...].astype(bf16))
    back_ref[...] = gather(source, cmap_ref[0:1, :], cmap_ref[1:2, :], width).astype(bf16)


def state_kernel(levels, width, inv_ref, sw_ref, sm_ref, state_ref, out_ref, h_ref, sm_pad, high, low):
    vars_, size = inv_ref.shape[1], inv_ref.shape[2]

    @pl.when(pl.program_id(0) == 0)
    def _():
        sm_pad[...] = jnp.zeros_like(sm_pad)
        sm_pad[0:levels, :] = sm_ref[...]
        for v in range(vars_):
            inv = inv_ref[0, v]
            h_ref[v] = three(nn, inv, three(nt, sw_ref[v], sm_pad[...]))
            high[v], low[v] = split(three(nn, inv, inv))

    for v in range(vars_):
        sh, sl = split(state_ref[v])
        out_ref[v] = nn(high[v], sh) + nn(high[v], sl) + nn(low[v], sh)


def sum_kernel(width, tt_ref, omap_ref, oarea_ref, out_ref):
    count = out_ref.shape[1] // 256
    chunk = 1024
    total = None
    for start in range(0, OCELLS, chunk):
        value = tt_ref[:, start : start + chunk] * oarea_ref[:, start : start + chunk]
        high = omap_ref[1:2, start : start + chunk]
        left = jnp.concatenate(
            [jnp.where(high == h, value, 0.0) for h in range(count)], axis=0
        ).astype(bf16)
        part = nt(left, onehot(omap_ref[0:1, start : start + chunk], 256))
        total = part if total is None else total + part
    for h in range(count):
        out_ref[:, h * 256 : (h + 1) * 256] = total[h * width : (h + 1) * width]


def final_kernel(
    peers, width, smap_ref, sarea_ref, sum_ref, h_ref, base_ref, *rest
):
    got = rest[: peers - 1]
    out_ref, value = rest[peers - 1 :]
    step = pl.program_id(0)
    columns = sum_ref.shape[1]
    count = columns // 256

    @pl.when(step == 0)
    def _():
        me = lax.axis_index("ocn")
        segment = smap_ref[2:3, :]
        total = jnp.zeros(value.shape, f32)
        for mask in range(1, peers):
            offset = ((me ^ mask) - me) & (peers - 1)
            total = jnp.where(segment == offset, got[mask - 1][...].astype(f32), total)
        value[...] = total * sarea_ref[...]

    back = value[...]
    high = smap_ref[1:2, :] - step * count
    left = jnp.concatenate(
        [jnp.where(high == h, back, 0.0) for h in range(count)], axis=0
    ).astype(bf16)
    part = nt(left, onehot(smap_ref[0:1, :], 256))
    sums = jnp.concatenate([part[h * width : (h + 1) * width] for h in range(count)], axis=1)
    sums = sums + sum_ref[...]
    sh, sl = split(sums)
    for v in range(out_ref.shape[0]):
        hh, hl = split(h_ref[v])
        out_ref[v] = base_ref[v] + (nn(hh, sh) + nn(hh, sl) + nn(hl, sh))


def on_device(
    atmos_state, inverses, flux_weight, surface_weight, area_table, xc_column, xc_dest, xc_cell,
    xc_class, tracer, land_sea, forcing_weight, surface_map, diffusivity,
):
    peers, tiles = lax.axis_size("ocn"), lax.axis_size("atm")
    vars_, size, columns = atmos_state.shape
    cells = xc_column.shape[0]
    levels = tracer.shape[0]
    slots = cells - 3 * cells // peers
    width = -(-(levels + 3) // 16) * 16
    borders = sorted({i ^ (i + 1) for i in range(peers - 1)})
    sds = jax.ShapeDtypeStruct
    params = pltpu.CompilerParams(vmem_limit_bytes=56 * 1024 * 1024)
    smem = pl.BlockSpec(memory_space=pltpu.SMEM)
    vmem = pl.BlockSpec(memory_space=pltpu.VMEM)

    def swap(x, axis, pairs):
        return lax.ppermute(x, axis, pairs)

    def xor_swap(x, mask):
        return swap(x, "ocn", [(i, i ^ mask) for i in range(peers)])

    grid_of = lambda x: x.reshape(cells // 128, 128)
    outs = pl.pallas_call(
        functools.partial(send_kernel, peers, levels, width, borders),
        out_shape=[sds((width, slots), bf16)]
        + [sds((width, slots + 256), bf16)] * len(borders)
        + [
            sds((width, columns), bf16), sds((width, OCELLS), f32), sds((2, OCELLS), i32),
            sds((1, OCELLS), f32), sds((3, slots), i32), sds((1, slots), f32),
        ],
        in_specs=[smem] + [vmem] * 10,
        out_specs=[vmem] * (7 + len(borders)),
        scratch_shapes=[pltpu.VMEM((width, forcing_weight.shape[1]), f32)],
        compiler_params=params,
        name="send",
    )(
        area_table, grid_of(xc_column), grid_of(xc_dest), grid_of(xc_cell), grid_of(xc_class),
        inverses, flux_weight, forcing_weight, atmos_state,
        tracer.reshape(levels * OY, OX), land_sea,
    )
    packed, sides = outs[0], outs[1 : 1 + len(borders)]
    forcing_cols, t0, omap, oarea, smap, sarea = outs[1 + len(borders) :]
    got = []
    for mask in range(1, peers):
        buffer = sides[borders.index(mask)] if mask in borders else packed
        got.append(xor_swap(buffer, mask))

    local = pl.pallas_call(
        functools.partial(local_kernel, width),
        out_shape=sds((width, OCELLS), f32),
        in_specs=[vmem] * 3, out_specs=vmem, compiler_params=params, name="local",
    )(forcing_cols, omap, oarea)

    send_rows = 4 * OX + OX + 4 * OX
    f_all, fs, ts, cmap, even, odd = pl.pallas_call(
        functools.partial(receive_kernel, peers, levels, width, borders),
        out_shape=[
            sds((width, OCELLS), f32), sds((width, STRIPS * OX), f32),
            sds((width, STRIPS * OX), f32), sds((2, slots), i32),
            sds((width, send_rows), bf16), sds((width, send_rows), bf16),
        ],
        in_specs=[vmem] * (3 + peers), out_specs=[vmem] * 6, compiler_params=params,
        name="receive",
    )(packed, smap, local, t0, *got)

    first = [(i, i ^ 1) for i in range(tiles)]
    second = [(i, (i + 1) % tiles if i & 1 else (i - 1) % tiles) for i in range(tiles)]
    even, odd = swap(even, "atm", first), swap(odd, "atm", second)

    block = 512
    base, back_map = pl.pallas_call(
        functools.partial(state_kernel, levels, width),
        out_shape=[sds((vars_, size, columns), f32), sds((vars_, size, width), f32)],
        grid=(columns // block,),
        in_specs=[
            pl.BlockSpec(inverses.shape, lambda i: (0, 0, 0, 0)),
            pl.BlockSpec(surface_weight.shape, lambda i: (0, 0, 0)),
            pl.BlockSpec(surface_map.shape, lambda i: (0, 0)),
            pl.BlockSpec((vars_, size, block), lambda i: (0, 0, i)),
        ],
        out_specs=[
            pl.BlockSpec((vars_, size, block), lambda i: (0, 0, i)),
            pl.BlockSpec((vars_, size, width), lambda i: (0, 0, 0)),
        ],
        scratch_shapes=[
            pltpu.VMEM((width, surface_map.shape[1]), f32),
            pltpu.VMEM((vars_, size, size), bf16), pltpu.VMEM((vars_, size, size), bf16),
        ],
        compiler_params=params, name="state",
    )(inverses, surface_weight, surface_map, atmos_state)

    long = (OY + 8) * OX
    thin = (STRIPS + 2) * OX
    tracer_out, t4, back = pl.pallas_call(
        functools.partial(ocean_kernel, levels, width),
        out_shape=[
            sds((levels * OY, OX), f32), sds((width, OCELLS), f32), sds((width, slots), bf16),
        ],
        in_specs=[vmem] * 8, out_specs=[vmem] * 3,
        scratch_shapes=[
            pltpu.VMEM((width, long), f32), pltpu.VMEM((width, long), f32),
            pltpu.VMEM((width, thin), f32), pltpu.VMEM((width, thin), f32),
            pltpu.VMEM((8, long), f32), pltpu.VMEM((8, long), f32),
            pltpu.VMEM((8, thin), f32), pltpu.VMEM((8, thin), f32),
            pltpu.VMEM((width, OX), f32),
        ],
        compiler_params=params, name="ocean",
    )(f_all, fs, t0, ts, even, odd, diffusivity.reshape(1, levels), cmap)

    returned = [xor_swap(back, mask) for mask in range(1, peers)]
    sums = pl.pallas_call(
        functools.partial(sum_kernel, width),
        out_shape=sds((width, columns), f32),
        in_specs=[vmem] * 3, out_specs=vmem, compiler_params=params, name="sum",
    )(t4, omap, oarea)

    final_state = pl.pallas_call(
        functools.partial(final_kernel, peers, width),
        out_shape=sds((vars_, size, columns), f32),
        grid=(columns // block,),
        in_specs=[
            pl.BlockSpec(smap.shape, lambda i: (0, 0)),
            pl.BlockSpec(sarea.shape, lambda i: (0, 0)),
            pl.BlockSpec((width, block), lambda i: (0, i)),
            pl.BlockSpec(back_map.shape, lambda i: (0, 0, 0)),
            pl.BlockSpec((vars_, size, block), lambda i: (0, 0, i)),
        ]
        + [pl.BlockSpec((width, slots), lambda i: (0, 0))] * (peers - 1),
        out_specs=pl.BlockSpec((vars_, size, block), lambda i: (0, 0, i)),
        scratch_shapes=[pltpu.VMEM((width, slots), f32)],
        compiler_params=params, name="final",
    )(smap, sarea, sums, back_map, base, *returned)
    return (final_state, tracer_out.reshape(tracer.shape))


def solution(mesh):
    in_specs = (
        P(None, None, ("member", "atm", "ocn")),
        P("atm", None, None, None),
        P(),
        P(),
        P(),
        P(("atm", "ocn")),
        P(("atm", "ocn"), None),
        P(("atm", "ocn")),
        P(("atm", "ocn")),
        P(None, "atm", ("member", "ocn")),
        P("atm", "ocn"),
        P(),
        P(),
        P(),
    )
    out_specs = (P(None, None, ("member", "atm", "ocn")), P(None, "atm", ("member", "ocn")))
    return jax.shard_map(
        on_device, mesh=mesh, in_specs=in_specs, out_specs=out_specs, check_vma=False
    )
```

time: 441 us -> 98.5 us (0.22); the launches traced: 435 us -> 98.1 us
  other arithmetic: 165 us -> 0 us
  local copies, waits for them, and re-layouts: 104 us -> 20.1 us
  waiting for transfers between devices: 67.5 us -> 13.2 us
  Pallas kernels: 0 us -> 52 us
  starting transfers between devices: 56.4 us -> 12.1 us
  matrix products: 40.8 us -> 0 us
    scatter-add x2 -> x0, other arithmetic: 119 us -> none  [the longest x1 80.7 us: on_device(): jax.ops.segment_sum(received.astype(jnp.float32), recv_cells, ocean_cells...]
    pallas_call x0 -> x7, Pallas kernels: none -> 52 us  [the longest x1 13.1 us: on_device(): pl.pallas_call(functools.partial(ocean_kernel, levels, width), out_shape=...]
    gather x1 -> x0, local copies, waits for them, and re-layouts: 43.7 us -> none  [on_device(): back_rows = surface_padded[recv_cells]]
    dot_general x7 -> x0, matrix products: 40.8 us -> none  [the longest x2 17.2 us: column_solve(): jnp.einsum('vkj,vjc->vkc', inverse_set, column_field, precision=highest)]
    ppermute x16 -> x8, starting transfers between devices: 41.6 us -> 12.1 us  [swap(): return lax.ppermute(x, axis, pairs)]
    all_to_all x3 -> x0, waiting for transfers between devices: 27.2 us -> none  [the longest x1 27.2 us: on_device(): lax.all_to_all(back_rows, 'ocn', split_axis=0, concat_axis=0, tiled=True)]
    ppermute x16 -> x8, waiting for transfers between devices: 40.3 us -> 13.2 us  [swap(): return lax.ppermute(x, axis, pairs)]
    scatter x1 -> x0, other arithmetic: 26.2 us -> none  [on_device(): jnp.zeros((slot_total, flux_width), jnp.bfloat16).at[slot_index]]
  transfers between devices with their start and end apart: 19 -> 8, of which waited for: 14 -> 3; matrix products, arithmetic and copies ran while one was open for 14% -> 1% of each run, Pallas kernels for 0% -> 16%
where the time goes in v1:
time: 98.5 us; the launch traced here: 98.1 us
  Pallas kernels  52 us (53%)
  local copies, waits for them, and re-layouts  20.1 us (20%)
  waiting for transfers between devices  13.2 us (13%)
  starting transfers between devices  12.1 us (12%)
    unnamed x25, local copies, waits for them, and re-layouts  20.1 us
    ppermute x8, waiting for transfers between devices, swap(): return lax.ppermute(x, axis, pairs)  13.2 us
    pallas_call x1, Pallas kernels, on_device(): pl.pallas_call(functools.partial(ocean_kernel, levels, width), out_shape=...  13.1 us
    ppermute x8, starting transfers between devices, swap(): return lax.ppermute(x, axis, pairs)  12.1 us
    pallas_call x1, Pallas kernels, on_device(): pl.pallas_call(functools.partial(send_kernel, peers, levels, width, borde...  9.15 us
    pallas_call x1, Pallas kernels, on_device(): pl.pallas_call(functools.partial(final_kernel, peers, width), out_shape=s...  8.19 us
    pallas_call x1, Pallas kernels, on_device(): pl.pallas_call(functools.partial(state_kernel, levels, width), out_shape=...  7.95 us
    pallas_call x1, Pallas kernels, on_device(): pl.pallas_call(functools.partial(receive_kernel, peers, levels, width, bo...  6 us
  transfers between devices with their start and end apart: 8, of which 3 were waited for; matrix products, arithmetic and copies ran while one was open for 1% of the time, Pallas kernels for 16%

profile of v1, /device:TPU:0, one launch (start us, length us, event | category | flops | bytes accessed | tf_op | source)
XLA Modules:
  0.0 98.1 jit_solution(11037314454353237841)
XLA Ops:
  0.6 0.0 copy-start
  0.6 2.0 %copy.16.inv_ref = f32[1,4,137,137]{3,2,1,0:T(8,128)} copy(f32[1,4,137,137]{3,1,2,0:T(4,128)} %param.15) | data formatting | bytes 600608 | tf_op args[1]
  2.7 0.0 copy-done
  2.7 0.7 copy.17.flux_ref
  3.4 7.0 %copy.18.state_ref = f32[4,137,2048]{2,1,0:T(8,128)} copy(f32[4,137,2048]{2,0,1:T(4,128)} %param.14) | data formatting | bytes 8978432 | tf_op args[0]
  10.4 9.1 %send.1 = (bf16[80,1024]{1,0:T(8,128)(2,1)}, bf16[80,1280]{1,0:T(8,128)(2,1)}, bf16[80,1280]{1,0:T(8,128)(2,1)}, bf16[80,2048]{1,0:T(8,128)(2,1)}, f32[80,4096]{...) custom-call(f32[64]{0:T(128)} %area_ref.1, s32[32,128]{1,0:T(8,128)} %bitcast.8, ...), custom_call_target="tpu_custom_call" | custom-call | tf_op jit(solution)/shard_map/send/pallas_call | solution.py:544
  19.6 3.0 %collective-permute-start = (bf16[80,1280]{1,0:T(8,128)(2,1)}, bf16[80,1280]{1,0:T(8,128)(2,1)S(1)}, u32[]{:S(2)}, u32[]{:S(2)}) collective-permute-start(bf16[80,1280]{1,0:T(8,128)(2,1)} %get-tuple-element.29), channel_id=1, source_target_pairs={{0,1},{1,0},{2,3},{3,2},{4,5},{5,4},{6,7},{7,6},{8,9},{9,8},{10,11... | collective-permute-start | bytes 614408 | tf_op jit(solution)/shard_map/ppermute | solution.py:538
  22.6 1.5 %collective-permute-start.2 = (bf16[80,1280]{1,0:T(8,128)(2,1)}, bf16[80,1280]{1,0:T(8,128)(2,1)S(1)}, u32[]{:S(2)}, u32[]{:S(2)}) collective-permute-start(bf16[80,1280]{1,0:T(8,128)(2,1)} %get-tuple-element.30), channel_id=1, source_target_pairs={{0,3},{1,2},{2,1},{3,0},{4,7},{5,6},{6,5},{7,4},{8,11},{9,10},{10,... | collective-permute-start | bytes 614408 | tf_op jit(solution)/shard_map/ppermute | solution.py:538
  24.1 0.1 collective-permute-start.1
  24.1 3.8 %local.1.local_ref = f32[80,4096]{1,0:T(8,128)} custom-call(bf16[80,2048]{1,0:T(8,128)(2,1)} %get-tuple-element.25.forcing_ref, s32[2,4096]{1,0:T(2,128)} %get-tuple-element.26.omap_ref, f32[1,4096]{1,0:T(1,128)} %get-tuple-element.27.oarea_ref), custom_call_target="tpu_custom_call" | custom-call | tf_op jit(solution)/shard_map/local/pallas_call | solution.py:569
  28.0 6.1 %collective-permute-done.1.rest_1_ = bf16[80,1024]{1,0:T(8,128)(2,1)S(1)} collective-permute-done((bf16[80,1024]{1,0:T(8,128)(2,1)}, bf16[80,1024]{1,0:T(8,128)(2,1)S(1)}, u32[]{:S(2)}, u32[]{:S(2)}) %collective-permute-start.1) | collective-permute-done | bytes 163872 | tf_op jit(solution)/shard_map/ppermute | solution.py:538
  34.0 0.0 copy-start.6
  34.0 0.0 collective-permute-done.rest_0_
  34.0 0.0 copy-start.2
  34.0 0.0 collective-permute-done.2.rest_2_
  34.1 0.0 copy-start.3
  34.1 0.6 copy-done.6
  34.7 0.1 copy-done.2
  34.8 0.1 copy-done.3
  34.9 6.0 %receive.1 = (f32[80,4096]{1,0:T(8,128)}, f32[80,1024]{1,0:T(8,128)}, f32[80,1024]{1,0:T(8,128)}, s32[2,1024]{1,0:T(2,128)}, bf16[80,1152]{1,0:T(8,128)(2,1)}, /*index=5*/bf16[80,1152]{1,0:T(8,128)(2,1)}) custom-call(bf16[80,1024]{1,0:T(8,128)(2,1)} %get-tuple-element.24.packed_ref, s32[3,1024]{1,0:T(4,128)} %get-tuple-element.22.smap_ref, ...), custom_call_target="tpu_custom_call" | custom-call | tf_op jit(solution)/shard_map/receive/pallas_call | solution.py:576
  40.9 1.6 %collective-permute-start.3 = (bf16[80,1152]{1,0:T(8,128)(2,1)}, bf16[80,1152]{1,0:T(8,128)(2,1)S(1)}, u32[]{:S(2)}, u32[]{:S(2)}) collective-permute-start(bf16[80,1152]{1,0:T(8,128)(2,1)} %get-tuple-element.34), channel_id=1, source_target_pairs={{0,4},{4,0},{8,12},{12,8},{1,5},{5,1},{9,13},{13,9},{2,6},{6,2},{1... | collective-permute-start | bytes 552968 | tf_op jit(solution)/shard_map/ppermute | solution.py:538
  42.4 2.5 %collective-permute-start.4 = (bf16[80,1152]{1,0:T(8,128)(2,1)}, bf16[80,1152]{1,0:T(8,128)(2,1)S(1)}, u32[]{:S(2)}, u32[]{:S(2)}) collective-permute-start(bf16[80,1152]{1,0:T(8,128)(2,1)} %get-tuple-element.35), channel_id=1, source_target_pairs={{0,12},{4,8},{8,4},{12,0},{1,13},{5,9},{9,5},{13,1},{2,14},{6,10},... | collective-permute-start | bytes 552968 | tf_op jit(solution)/shard_map/ppermute | solution.py:538
  44.9 3.1 %collective-permute-done.3.even_ref = bf16[80,1152]{1,0:T(8,128)(2,1)S(1)} collective-permute-done((bf16[80,1152]{1,0:T(8,128)(2,1)}, bf16[80,1152]{1,0:T(8,128)(2,1)S(1)}, u32[]{:S(2)}, u32[]{:S(2)}) %collective-permute-start.3) | collective-permute-done | bytes 184352 | tf_op jit(solution)/shard_map/ppermute | solution.py:538
  48.0 0.0 copy-start.4
  48.0 4.0 %collective-permute-done.4.odd_ref = bf16[80,1152]{1,0:T(8,128)(2,1)S(1)} collective-permute-done((bf16[80,1152]{1,0:T(8,128)(2,1)}, bf16[80,1152]{1,0:T(8,128)(2,1)S(1)}, u32[]{:S(2)}, u32[]{:S(2)}) %collective-permute-start.4) | collective-permute-done | bytes 184352 | tf_op jit(solution)/shard_map/ppermute | solution.py:538
  52.0 0.0 copy-start.5
  52.0 0.0 copy-done.4
  52.0 0.7 copy-done.5
  52.7 0.0 copy-start.1
  52.7 13.1 %ocean.1 = (f32[2400,128]{1,0:T(8,128)}, f32[80,4096]{1,0:T(8,128)}, bf16[80,1024]{1,0:T(8,128)(2,1)}) custom-call(f32[80,4096]{1,0:T(8,128)} %get-tuple-element.31.f_ref, f32[80,1024]{1,0:T(8,128)} %get-tuple-element.32.fs_ref, f32[80,4096]{1,0:T(8,128)} %get-tuple-element.28.t_ref, f32[80,1024]{1,0:T(8,128)} %get-tuple-element.33.ts_ref, ...), custom_call_target="tpu_custom_call" | custom-call | tf_op jit(solution)/shard_map/ocean/pallas_call | solution.py:615
  65.9 1.5 %collective-permute-start.5 = (bf16[80,1024]{1,0:T(8,128)(2,1)}, bf16[80,1024]{1,0:T(8,128)(2,1)S(1)}, u32[]{:S(2)}, u32[]{:S(2)}) collective-permute-start(bf16[80,1024]{1,0:T(8,128)(2,1)} %get-tuple-element.40), channel_id=1, source_target_pairs={{0,1},{1,0},{2,3},{3,2},{4,5},{5,4},{6,7},{7,6},{8,9},{9,8},{10,11... | collective-permute-start | bytes 491528 | tf_op jit(solution)/shard_map/ppermute | solution.py:538
  67.3 0.5 collective-permute-start.6
  67.8 1.5 %collective-permute-start.7 = (bf16[80,1024]{1,0:T(8,128)(2,1)}, bf16[80,1024]{1,0:T(8,128)(2,1)S(1)}, u32[]{:S(2)}, u32[]{:S(2)}) collective-permute-start(bf16[80,1024]{1,0:T(8,128)(2,1)} %get-tuple-element.40), channel_id=1, source_target_pairs={{0,3},{1,2},{2,1},{3,0},{4,7},{5,6},{6,5},{7,4},{8,11},{9,10},{10,... | collective-permute-start | bytes 491528 | tf_op jit(solution)/shard_map/ppermute | solution.py:538
  69.3 0.0 copy-done.1
  69.4 0.7 copy.20.sw_ref
  70.1 7.9 %state.1 = (f32[4,137,2048]{2,1,0:T(8,128)}, f32[4,137,80]{2,1,0:T(8,128)}) custom-call(f32[1,4,137,137]{3,2,1,0:T(8,128)} %copy.16.inv_ref, f32[4,137,128]{2,1,0:T(8,128)} %copy.20.sw_ref, f32[75,128]{1,0:T(8,128)} %sm_ref.1, f32[4,137,2048]{2,1,0:T(8,128)} %copy.18.state_ref), custom_call_target="tpu_custom_call" | custom-call | tf_op jit(solution)/shard_map/state/pallas_call | solution.py:592
  78.0 3.7 %sum.1.sum_ref = f32[80,2048]{1,0:T(8,128)} custom-call(f32[80,4096]{1,0:T(8,128)} %get-tuple-element.37.tt_ref, s32[2,4096]{1,0:T(2,128)} %get-tuple-element.26.omap_ref, f32[1,4096]{1,0:T(1,128)} %get-tuple-element.27.oarea_ref), custom_call_target="tpu_custom_call" | custom-call | tf_op jit(solution)/shard_map/sum/pallas_call | solution.py:632
  81.8 0.0 collective-permute-done.5.rest_0_
  81.8 0.0 copy-start.7
  81.8 0.0 collective-permute-done.6.rest_1_
  81.8 0.0 copy-start.8
  81.8 0.0 collective-permute-done.7.rest_2_
  81.8 0.0 copy-start.9
  81.8 0.6 copy-done.7
  82.4 0.1 copy-done.8
  82.5 0.1 copy-done.9
  82.6 8.2 %final.1 = f32[4,137,2048]{2,1,0:T(8,128)} custom-call(s32[3,1024]{1,0:T(4,128)} %get-tuple-element.22.smap_ref, f32[1,1024]{1,0:T(1,128)} %get-tuple-element.23.sarea_ref, f32[80,2048]{1,0:T(8,128)} %sum.1.sum_ref, f32[4,137,80]{2,1,0:T(8,128)} %get-tuple-element.38.h_ref, f32[4,137,2048]{2,1,0:T(8,128)} %get-tuple-element.39.base_ref, ...), custom_call_target="tpu_custom_call" | custom-call | tf_op jit(solution)/shard_map/final/pallas_call | solution.py:638
  90.8 7.3 %copy.22 = f32[4,137,2048]{2,0,1:T(4,128)} copy(f32[4,137,2048]{2,1,0:T(8,128)} %final.1) | data formatting | bytes 8978432
Async XLA Ops:
  0.6 2.0 %copy-start = (f32[4,137,128]{2,0,1:T(4,128)S(1)}, f32[4,137,128]{2,0,1:T(4,128)}, u32[]{:S(2)}) copy-start(f32[4,137,128]{2,0,1:T(4,128)} %param.16) | copy-start | bytes 841732
  19.6 14.5 %collective-permute-start = (bf16[80,1280]{1,0:T(8,128)(2,1)}, bf16[80,1280]{1,0:T(8,128)(2,1)S(1)}, u32[]{:S(2)}, u32[]{:S(2)}) collective-permute-start(bf16[80,1280]{1,0:T(8,128)(2,1)} %get-tuple-element.29), channel_id=1, source_target_pairs={{0,1},{1,0},{2,3},{3,2},{4,5},{5,4},{6,7},{7,6},{8,9},{9,8},{10,11... | collective-permute-start | bytes 614408 | tf_op jit(solution)/shard_map/ppermute | solution.py:538
  22.6 11.5 %collective-permute-start.2 = (bf16[80,1280]{1,0:T(8,128)(2,1)}, bf16[80,1280]{1,0:T(8,128)(2,1)S(1)}, u32[]{:S(2)}, u32[]{:S(2)}) collective-permute-start(bf16[80,1280]{1,0:T(8,128)(2,1)} %get-tuple-element.30), channel_id=1, source_target_pairs={{0,3},{1,2},{2,1},{3,0},{4,7},{5,6},{6,5},{7,4},{8,11},{9,10},{10,... | collective-permute-start | bytes 614408 | tf_op jit(solution)/shard_map/ppermute | solution.py:538
  24.1 10.0 %collective-permute-start.1 = (bf16[80,1024]{1,0:T(8,128)(2,1)}, bf16[80,1024]{1,0:T(8,128)(2,1)S(1)}, u32[]{:S(2)}, u32[]{:S(2)}) collective-permute-start(bf16[80,1024]{1,0:T(8,128)(2,1)} %get-tuple-element.24.packed_ref), channel_id=1, source_target_pairs={{0,2},{1,3},{2,0},{3,1},{4,6},{5,7},{6,4},{7,5},{8,10},{9,11},{10,... | collective-permute-start | bytes 491528 | tf_op jit(solution)/shard_map/ppermute | solution.py:538
  34.0 0.7 copy-start.6
  34.0 0.7 copy-start.2
  34.1 0.8 copy-start.3
  40.9 7.1 %collective-permute-start.3 = (bf16[80,1152]{1,0:T(8,128)(2,1)}, bf16[80,1152]{1,0:T(8,128)(2,1)S(1)}, u32[]{:S(2)}, u32[]{:S(2)}) collective-permute-start(bf16[80,1152]{1,0:T(8,128)(2,1)} %get-tuple-element.34), channel_id=1, source_target_pairs={{0,4},{4,0},{8,12},{12,8},{1,5},{5,1},{9,13},{13,9},{2,6},{6,2},{1... | collective-permute-start | bytes 552968 | tf_op jit(solution)/shard_map/ppermute | solution.py:538
  42.4 9.6 %collective-permute-start.4 = (bf16[80,1152]{1,0:T(8,128)(2,1)}, bf16[80,1152]{1,0:T(8,128)(2,1)S(1)}, u32[]{:S(2)}, u32[]{:S(2)}) collective-permute-start(bf16[80,1152]{1,0:T(8,128)(2,1)} %get-tuple-element.35), channel_id=1, source_target_pairs={{0,12},{4,8},{8,4},{12,0},{1,13},{5,9},{9,5},{13,1},{2,14},{6,10},... | collective-permute-start | bytes 552968 | tf_op jit(solution)/shard_map/ppermute | solution.py:538
  48.0 4.0 %copy-start.4 = (bf16[80,1152]{1,0:T(8,128)(2,1)}, bf16[80,1152]{1,0:T(8,128)(2,1)S(1)}, u32[]{:S(2)}) copy-start(bf16[80,1152]{1,0:T(8,128)(2,1)S(1)} %collective-permute-done.3.even_ref) | copy-start | bytes 552964
  52.0 0.7 copy-start.5
  52.7 16.6 %copy-start.1 = (f32[4,137,128]{2,0,1:T(4,128)S(1)}, f32[4,137,128]{2,0,1:T(4,128)}, u32[]{:S(2)}) copy-start(f32[4,137,128]{2,0,1:T(4,128)} %param.17) | copy-start | bytes 841732
  65.9 15.9 %collective-permute-start.5 = (bf16[80,1024]{1,0:T(8,128)(2,1)}, bf16[80,1024]{1,0:T(8,128)(2,1)S(1)}, u32[]{:S(2)}, u32[]{:S(2)}) collective-permute-start(bf16[80,1024]{1,0:T(8,128)(2,1)} %get-tuple-element.40), channel_id=1, source_target_pairs={{0,1},{1,0},{2,3},{3,2},{4,5},{5,4},{6,7},{7,6},{8,9},{9,8},{10,11... | collective-permute-start | bytes 491528 | tf_op jit(solution)/shard_map/ppermute | solution.py:538
  67.3 14.4 %collective-permute-start.6 = (bf16[80,1024]{1,0:T(8,128)(2,1)}, bf16[80,1024]{1,0:T(8,128)(2,1)S(1)}, u32[]{:S(2)}, u32[]{:S(2)}) collective-permute-start(bf16[80,1024]{1,0:T(8,128)(2,1)} %get-tuple-element.40), channel_id=1, source_target_pairs={{0,2},{1,3},{2,0},{3,1},{4,6},{5,7},{6,4},{7,5},{8,10},{9,11},{10,... | collective-permute-start | bytes 491528 | tf_op jit(solution)/shard_map/ppermute | solution.py:538
  67.8 14.0 %collective-permute-start.7 = (bf16[80,1024]{1,0:T(8,128)(2,1)}, bf16[80,1024]{1,0:T(8,128)(2,1)S(1)}, u32[]{:S(2)}, u32[]{:S(2)}) collective-permute-start(bf16[80,1024]{1,0:T(8,128)(2,1)} %get-tuple-element.40), channel_id=1, source_target_pairs={{0,3},{1,2},{2,1},{3,0},{4,7},{5,6},{6,5},{7,4},{8,11},{9,10},{10,... | collective-permute-start | bytes 491528 | tf_op jit(solution)/shard_map/ppermute | solution.py:538
  81.8 0.7 copy-start.7
  81.8 0.7 copy-start.8
  81.8 0.8 copy-start.9

commit v2 on v1

v2 whole, which is shorter than its diff:
```python
import functools
import jax
import jax.numpy as jnp
from jax import lax
from jax.experimental import pallas as pl
from jax.experimental.pallas import tpu as pltpu
from jax.sharding import PartitionSpec as P

OSTEPS = 4
NVAR = 4
OY = 32
OX = 128
OCELLS = OY * OX
STRIPS = 8
f32 = jnp.float32
bf16 = jnp.bfloat16
i32 = jnp.int32


def nn(a, b):
    return jnp.dot(a, b, preferred_element_type=f32)


def nt(a, b):
    return lax.dot_general(a, b, (((1,), (1,)), ((), ())), preferred_element_type=f32)


def split(x):
    high = x.astype(bf16)
    return high, (x - high.astype(f32)).astype(bf16)


def three(dot, a, b):
    ah, al = split(a)
    bh, bl = split(b)
    return dot(ah, bh) + dot(ah, bl) + dot(al, bh)


def doubled(x):
    return jnp.concatenate(list(split(x)), axis=0)


def wide(left, right, dot=nn):
    count = left.shape[0] // 2
    high, low = split(right)
    both = dot(left, high)
    return both[:count] + both[count:] + dot(left[:count], low)


def column_block(ref, var, first, blocks):
    size, rows, lanes = ref.shape
    lines = ref.reshape(size * rows, lanes)
    step = NVAR
    return jnp.concatenate(
        [lines[pl.ds((first + i) * step + var, size, stride=rows), :] for i in range(blocks)],
        axis=1,
    )


def iota(shape, dim):
    return lax.broadcasted_iota(i32, shape, dim)


def flat(x):
    return jnp.concatenate([x[i : i + 1, :] for i in range(x.shape[0])], axis=1)


def onehot(row, size):
    return jnp.where(iota((size, row.shape[1]), 0) == row, 1.0, 0.0).astype(bf16)


def place(high, low, payloads, rows):
    lines = iota((rows, high.shape[1]), 0) == high
    left = jnp.concatenate([jnp.where(lines, p, 0.0) for p in payloads], axis=0).astype(bf16)
    out = nt(left, onehot(low, 128))
    return [out[i * rows : (i + 1) * rows] for i in range(len(payloads))]


def stacked(x):
    return jnp.concatenate([x[:, h : h + 256] for h in range(0, x.shape[1], 256)], axis=0)


def two_terms(ref):
    return jnp.concatenate([stacked(ref[0]), stacked(ref[1])], axis=1)


def gather(source, low, high, width, chunk=512):
    count = source.shape[0] // width
    outs = []
    for start in range(0, low.shape[1], chunk):
        stop = min(start + chunk, low.shape[1])
        hot = onehot(low[:, start:stop], 256)
        if source.shape[1] == 512:
            hot = jnp.concatenate([hot, hot], axis=0)
        part = nn(source, hot)
        hc = high[:, start:stop]
        total = jnp.where(hc == 0, part[:width], 0.0)
        for h in range(1, count):
            total = jnp.where(hc == h, part[h * width : (h + 1) * width], total)
        outs.append(total)
    return outs[0] if len(outs) == 1 else jnp.concatenate(outs, axis=1)


def spread(value, low, high, count):
    vh, vl = split(value)
    hot = onehot(low, 256)
    outs = []
    for term in (vh, vl):
        parts = [jnp.where(high == h, term.astype(f32), 0.0) for h in range(count)]
        outs.append(nt(jnp.concatenate(parts, axis=0).astype(bf16), hot))
    return outs[0] + outs[1]


def pick(level_rows, lane_rows, base):
    index = iota(level_rows.shape, 0)
    for i, row in enumerate(lane_rows):
        level_rows = jnp.where(index == base + i, row, level_rows)
    return level_rows


def roll(x, shift):
    shift = shift % 128
    return x if shift == 0 else pltpu.roll(x, shift, 1)


def row_of(x, y):
    return x[:, y * OX : (y + 1) * OX]


def border_block(x, lane):
    blocks = []
    for i in range(2):
        block = jnp.zeros((x.shape[0], OX), f32)
        for b in range(4):
            for j in range(4):
                first = b * 32 + j * 8
                moved = roll(row_of(x, b * 8 + i * 4 + j), first + 4)
                block = jnp.where((lane >= first) & (lane < first + 8), moved, block)
        blocks.append(block)
    return jnp.concatenate(blocks, axis=1)


def strips(x, halo, lane):
    outs = []
    for j in range(STRIPS):
        side = roll(row_of(halo, j // 4), 8 - (j % 4) * 8)
        for b in range(4):
            line = row_of(x, b * 8 + j)
            first = b * 32
            side = jnp.where((lane >= first) & (lane < first + 8), roll(line, first + 8), side)
            side = jnp.where(
                (lane >= first + 16) & (lane < first + 24), roll(line, first + 16), side
            )
        outs.append(side)
    return outs


def send_kernel(
    peers, levels, width, borders,
    *refs,
):
    sources, rest = refs[:11], refs[11:]
    packed_ref, rest = rest[0], rest[1:]
    side_refs, rest = rest[: len(borders)], rest[len(borders) :]
    (even_ref, odd_ref), rest = rest[:2], rest[2:]
    forcing_ref, t_ref, omap_ref, oarea_ref, smap_ref, sarea_ref, state_ref = rest[:7]
    staged, fw_pad, sems, state_sems = rest[7:17], rest[17], rest[18], rest[19]
    (area_ref, col_ref, dest_ref, cell_ref, class_ref, inv_ref, flux_ref, fw_ref, tracer_ref,
     land_ref) = staged
    loads = [
        pltpu.make_async_copy(a, b, sems.at[i])
        for i, (a, b) in enumerate(zip(sources[:10], staged))
    ]
    for load in loads:
        load.start()
    state_hbm = sources[10]
    parts = state_sems.shape[0]
    part_rows = state_ref.shape[1] // parts
    state_loads = []
    for i in range(parts):
        at = pl.ds(i * part_rows, part_rows)
        state_loads.append(
            pltpu.make_async_copy(
                state_hbm.at[:, at, :], state_ref.at[:, at, :], state_sems.at[i]
            )
        )
        state_loads[i].start()
    for load in loads[:5]:
        load.wait()
    me = lax.axis_index("ocn")
    slots = packed_ref.shape[1]
    slot_rows = slots // 128
    slot_pad = -(-slot_rows // 8) * 8
    lines = col_ref.shape[0]
    lane = iota((1, 128), 1)

    offset = (dest_ref[...] - me) & (peers - 1)
    cells = cell_ref[...]
    classes = class_ref[...]
    cols = col_ref[...]
    area = jnp.zeros(cols.shape, f32)
    for i in range(area_ref.shape[0]):
        area = jnp.where(classes == i, area_ref[i], area)

    hits = [jnp.where(offset == k, 1.0, 0.0) for k in range(1, peers)]
    hot = jnp.concatenate(hits, axis=0)
    upper = jnp.where(iota((128, 128), 0) <= iota((128, 128), 1), 1.0, 0.0).astype(bf16)
    running = nn(hot.astype(bf16), upper)
    count = running.shape[0]
    totals = jnp.broadcast_to(running[:, 127:128], running.shape).astype(bf16)
    below = jnp.where(iota((count, count), 1) < iota((count, count), 0), 1.0, 0.0).astype(bf16)
    before = nn(below, totals)
    place_of = running + before - 1.0
    slot = jnp.full(cols.shape, -1.0, f32)
    for k in range(1, peers):
        at = (k - 1) * lines
        slot = jnp.where(offset == k, place_of[at : at + lines], slot)
    slot = slot.astype(i32)
    position = iota((slot_pad, 128), 0) * 128 + iota((slot_pad, 128), 1)
    segment = jnp.full((slot_pad, 128), 1, i32)
    for k in range(2, peers):
        at = (k - 1) * lines
        start = before[at : at + 1, :].astype(i32)
        segment = segment + jnp.where(position >= start, 1, 0)

    a1 = area.astype(bf16).astype(f32)
    a2 = (area - a1).astype(bf16).astype(f32)
    a3 = area - a1 - a2
    slot_f, cell_f = flat(slot), flat(cells)
    col_f = flat(cols)
    areas = [flat(a1), flat(a2), flat(a3)]
    col_low = (col_f & 255).astype(f32)
    col_high = lax.shift_right_arithmetic(col_f, 8).astype(f32)
    cell_low = cell_f & 127
    cell_high = lax.shift_right_arithmetic(cell_f, 7)
    got = place(
        lax.shift_right_arithmetic(slot_f, 7), slot_f & 127,
        [col_low, col_high] + areas + [cell_high.astype(f32), cell_low.astype(f32)], slot_pad,
    )
    keep = [flat(g[:slot_rows]) for g in got]
    s_low, s_high = keep[0].astype(i32), keep[1].astype(i32)
    s_area = keep[2] + keep[3] + keep[4]
    smap_ref[0:1, :] = s_low
    smap_ref[1:2, :] = s_high
    smap_ref[2:3, :] = flat(segment[:slot_rows])
    sarea_ref[...] = s_area

    local_high = jnp.where(flat(offset) == 0, cell_high, -1)
    own = place(local_high, cell_low, [col_low, col_high + 1.0] + areas, OY)
    o_low, o_high = own[0].astype(i32), own[1].astype(i32) - 1
    o_area = own[2] + own[3] + own[4]
    omap_ref[0:1, :] = flat(o_low)
    omap_ref[1:2, :] = flat(o_high)
    oarea_ref[...] = flat(o_area)

    blank = jnp.zeros((2, 128), f32)
    edge = []
    for m in (own[0], own[1], o_area):
        block = blank
        for b in range(4):
            part = m[b * 8 : (b + 1) * 8]
            for j in range(4):
                first = b * 32 + j * 8
                moved = roll(part, first + 4)
                pair = jnp.concatenate([moved[j : j + 1], moved[4 + j : 5 + j]], axis=0)
                block = jnp.where((lane >= first) & (lane < first + 8), pair, block)
        edge.append(flat(block))

    for load in loads[5:]:
        load.wait()
    fw_pad[...] = jnp.zeros_like(fw_pad)
    fw_pad[0:levels, :] = fw_ref[...]
    fw = fw_pad[...]
    pulled = []
    for v in range(NVAR):
        left = wide(doubled(wide(doubled(fw), flux_ref[:, v, :], nt)), inv_ref[:, v, :])
        pulled.append(doubled(left))

    for y in range(OY):
        at = pl.ds(y * OX, OX)
        t_ref[0:levels, at] = tracer_ref[pl.ds(y, levels, stride=OY), :]
        t_ref[levels : levels + 1, at] = land_ref[y : y + 1, :].astype(f32)
        t_ref[levels + 1 : width, at] = jnp.zeros((width - levels - 1, OX), f32)

    is_even = (lax.axis_index("atm") & 1) == 0
    top, bottom = t_ref[:, 0 : 4 * OX], t_ref[:, 28 * OX : 32 * OX]
    even_ref[...] = jnp.where(is_even, bottom, top).astype(bf16)
    odd_ref[...] = jnp.where(is_even, top, bottom).astype(bf16)

    for i in range(parts):
        state_loads[i].wait()
        for c in range(i * part_rows // NVAR, (i + 1) * part_rows // NVAR, 2):
            total = None
            for v in range(NVAR):
                term = wide(pulled[v], column_block(state_ref, v, c, 2))
                total = term if total is None else total + term
            at = slice(c * 128, (c + 2) * 128)
            forcing_ref[0, :, at], forcing_ref[1, :, at] = split(total)
    source = two_terms(forcing_ref)

    rows = gather(source, s_low, s_high, width) * s_area
    rows = pick(rows, keep[5:7], levels + 1).astype(bf16)
    packed_ref[...] = rows
    f_edge = gather(source, edge[0].astype(i32), edge[1].astype(i32) - 1, width) * edge[2]
    t_edge = border_block(t_ref[...], lane)
    lead = (lane & 7) < 4
    to_right, to_left = [], []
    for i in range(2):
        fe, te = row_of(f_edge, i), row_of(t_edge, i)
        to_right.append(jnp.where(lead, fe, roll(te, 4)))
        to_left.append(jnp.where(lead, roll(fe, -4), te))
    to_right = jnp.concatenate(to_right, axis=1)
    to_left = jnp.concatenate(to_left, axis=1)
    for mask, ref in zip(borders, side_refs):
        ref[:, 0:slots] = rows
        ref[:, slots : slots + 256] = jnp.where((me ^ mask) == me + 1, to_right, to_left).astype(
            bf16
        )


def local_kernel(width, forcing_ref, omap_ref, oarea_ref, out_ref):
    source = two_terms(forcing_ref)
    out_ref[...] = gather(source, omap_ref[0:1, :], omap_ref[1:2, :], width) * oarea_ref[...]


def receive_kernel(
    peers, levels, width, borders, early0, early1, packed_ref, smap_ref, local_ref, t_ref, *rest
):
    got = rest[: peers - 1]
    f_ref, fs_ref, ts_ref, cmap_ref, even_ref, odd_ref, edge_ref = rest[peers - 1 :]
    me = lax.axis_index("ocn")
    slots = packed_ref.shape[1]
    lane = iota((1, 128), 1)
    segment = smap_ref[2:3, :]
    chunks = slots // 256

    def meant_for(tile):
        total = jnp.zeros((width, slots), f32)
        for mask in range(peers):
            ref = packed_ref if mask == 0 else got[mask - 1]
            step = (tile - (me ^ mask)) & (peers - 1)
            total = jnp.where(segment == step, ref[:, 0:slots].astype(f32), total)
        high = total[levels + 1 : levels + 2, :].astype(i32)
        low = total[levels + 2 : levels + 3, :].astype(i32)
        return stacked(total.astype(bf16)), high, low

    index = iota((1, slots), 1)
    payload = [(index & 255).astype(f32), (lax.shift_right_arithmetic(index, 8) + 1).astype(f32)]

    source, high, low = meant_for(me)
    cell = high * 128 + low
    cmap_ref[0:1, :] = cell & 255
    cmap_ref[1:2, :] = lax.shift_right_arithmetic(cell, 8)
    where_low, where_high = place(high, low, payload, OY)
    f_ref[...] = local_ref[...] + gather(
        source, flat(where_low).astype(i32), flat(where_high).astype(i32) - 1, width
    )

    halo_f = None
    for step in (-1, 1):
        source, high, low = meant_for(me + step)
        at = low - 120 if step < 0 else low
        inside = (low >= 124) if step < 0 else (low < 4)
        block = lax.shift_right_arithmetic(high & 7, 2)
        spot = lax.shift_right_arithmetic(high, 3) * 32 + (high & 3) * 8 + at
        where_low, where_high = place(jnp.where(inside, block, -1), spot, payload, 8)
        part = gather(
            source, flat(where_low[:2]).astype(i32), flat(where_high[:2]).astype(i32) - 1, width
        )
        halo_f = part if halo_f is None else halo_f + part

    def side_from(tile):
        block = jnp.zeros((width, 256), f32)
        for mask in borders:
            block = jnp.where(
                (me ^ mask) == tile, got[mask - 1][:, slots : slots + 256].astype(f32), block
            )
        return block

    from_left, from_right = side_from(me - 1), side_from(me + 1)
    lead = (lane & 7) < 4
    side_f, side_t = [], []
    for i in range(2):
        fl, fr = row_of(from_left, i), row_of(from_right, i)
        side_f.append(jnp.where(lead, fr, roll(fl, 4)) + row_of(halo_f, i))
        side_t.append(jnp.where(lead, roll(fr, -4), fl))
    f_strips = strips(f_ref[...], jnp.concatenate(side_f, axis=1), lane)
    t_strips = strips(t_ref[...], jnp.concatenate(side_t, axis=1), lane)
    for j in range(STRIPS):
        fs_ref[:, j * OX : (j + 1) * OX] = f_strips[j]
        ts_ref[:, j * OX : (j + 1) * OX] = t_strips[j]

    def four(parts, first, source):
        block = jnp.zeros((width, OX), f32)
        for m in range(4):
            inside = (lane >= m * 32) & (lane < m * 32 + 32)
            block = jnp.where(inside, roll(parts[first + m], 32 * (m - source)), block)
        return block

    edges = [four(p, first, source) for p in (f_strips, t_strips)
             for first, source in ((0, 0), (4, 0), (0, 3), (4, 3))]
    edge_ref[...] = jnp.concatenate(edges, axis=1)
    top = jnp.concatenate([f_ref[:, 0 : 3 * OX], edges[0], edges[4]], axis=1)
    bottom = jnp.concatenate([f_ref[:, 29 * OX : 32 * OX], edges[3], edges[7]], axis=1)
    is_even = (lax.axis_index("atm") & 1) == 0
    even_ref[...] = jnp.where(is_even, bottom, top).astype(bf16)
    odd_ref[...] = jnp.where(is_even, top, bottom).astype(bf16)


def tile_row(ref, y):
    return ref[:, y * OX : (y + 1) * OX]


def not_there(lane):
    me, peers = lax.axis_index("ocn"), lax.axis_size("ocn")
    spot = lane & 31
    return ((me == 0) & (spot >= 12) & (spot < 16)) | (
        (me == peers - 1) & (spot >= 8) & (spot < 12)
    )


def fill_diffusivity(ref, dif_ref):
    width, levels = ref.shape[0], dif_ref.shape[1]
    diag = iota((width, levels), 0) == iota((width, levels), 1)
    column = jnp.sum(jnp.where(diag, dif_ref[...], 0.0), axis=1, keepdims=True)
    ref[...] = jnp.broadcast_to(column, ref.shape)


def count_rows(w8, n8, rows):
    for y in rows:
        here = tile_row(w8, y)
        n8[:, y * OX : (y + 1) * OX] = (
            tile_row(w8, y - 1) + tile_row(w8, y + 1) + roll(here, 1) + roll(here, -1)
        )


def substep_rows(rows, forcing, wet, counts, dif):
    for step in range(OSTEPS):
        new = list(rows)
        for y in range(step + 1, len(rows) - 1 - step):
            here = rows[y]
            lap = rows[y - 1] + rows[y + 1] + roll(here, 1) + roll(here, -1) - counts(y) * here
            new[y] = here + wet(y) * (dif * lap + forcing(y))
        rows = new
    return rows


def substep_strips(now, forcing, wet, counts, dif, ends):
    for step in range(OSTEPS):
        new = []
        for j, here in enumerate(now):
            up, down = ends(now, j)
            lap = up + down + roll(here, 1) + roll(here, -1) - counts[j] * here
            new.append(here + wet[j] * (dif * lap + forcing[j]))
        now = new
    return now


def merged(line, value, lane, b):
    value = jnp.where(lane < 4, roll(line, -(b * 32 + 16)), value)
    return jnp.where(lane >= 124, roll(line, 120 - b * 32), value)


def inner_kernel(
    levels, width, f_ref, fs_ref, t_ref, ts_ref, dif_ref, tt_ref, w8, n8, ws8, ns8, d8
):
    lane = iota((1, 128), 1)
    w8[...] = jnp.broadcast_to(t_ref[levels : levels + 1, :], w8.shape)
    count_rows(w8, n8, range(1, OY - 1))
    outside = not_there(lane)
    for j in range(STRIPS):
        line = tile_row(ts_ref, j)[levels : levels + 1, :]
        ws8[:, j * OX : (j + 1) * OX] = jnp.broadcast_to(jnp.where(outside, 0.0, line), (8, OX))

    def ends(parts, j):
        up = roll(parts[STRIPS - 1], 32) if j == 0 else parts[j - 1]
        down = roll(parts[0], 96) if j == STRIPS - 1 else parts[j + 1]
        return up, down

    parts = [tile_row(ws8, j) for j in range(STRIPS)]
    for j in range(STRIPS):
        up, down = ends(parts, j)
        ns8[:, j * OX : (j + 1) * OX] = up + down + roll(parts[j], 1) + roll(parts[j], -1)
    fill_diffusivity(d8, dif_ref)

    def group(g, carry):
        lev = pl.ds(pl.multiple_of(g * 8, 8), 8)
        dif = d8[lev, :]

        def load(ref, j):
            return ref[lev, j * OX : (j + 1) * OX]

        rows = substep_rows(
            [load(t_ref, y) * tile_row(w8, y) for y in range(OY)], lambda y: load(f_ref, y),
            lambda y: tile_row(w8, y), lambda y: tile_row(n8, y), dif,
        )
        wet = [tile_row(ws8, j) for j in range(STRIPS)]
        now = substep_strips(
            [load(ts_ref, j) * wet[j] for j in range(STRIPS)],
            [load(fs_ref, j) for j in range(STRIPS)], wet,
            [tile_row(ns8, j) for j in range(STRIPS)], dif, ends,
        )
        for y in range(4, OY - 4):
            value = merged(now[y % 8], rows[y], lane, y // 8)
            tt_ref[lev, y * OX : (y + 1) * OX] = jnp.where(
                tile_row(w8, y) > 0.0, value, load(t_ref, y)
            )
        return carry

    lax.fori_loop(0, width // 8, group, 0)


def slab_kernel(levels, t_ref, even_ref, odd_ref, s, w8, n8):
    row, rows_atm = lax.axis_index("atm"), lax.axis_size("atm")
    is_even = (row & 1) == 0
    even, odd = even_ref[...].astype(f32), odd_ref[...].astype(f32)
    top, bottom = jnp.where(is_even, odd, even), jnp.where(is_even, even, odd)
    tops = jnp.where(row > 0, 1.0, 0.0)
    bottoms = jnp.where(row < rows_atm - 1, 1.0, 0.0)

    def wide_wet(x):
        return jnp.broadcast_to(x[levels : levels + 1, :], (8, x.shape[1]))

    w8[:, 0 : 4 * OX] = wide_wet(top) * tops
    w8[:, 4 * OX : 12 * OX] = wide_wet(t_ref[:, 0 : 8 * OX])
    w8[:, 12 * OX : 20 * OX] = wide_wet(t_ref[:, 24 * OX : 32 * OX])
    w8[:, 20 * OX : 24 * OX] = wide_wet(bottom) * bottoms
    for y in (0, 11, 12, 23):
        n8[:, y * OX : (y + 1) * OX] = jnp.zeros((8, OX), f32)
    count_rows(w8, n8, list(range(1, 11)) + list(range(13, 23)))
    s[:, 0 : 4 * OX] = top * w8[0:1, 0 : 4 * OX]
    s[:, 4 * OX : 12 * OX] = t_ref[:, 0 : 8 * OX] * w8[0:1, 4 * OX : 12 * OX]
    s[:, 12 * OX : 20 * OX] = t_ref[:, 24 * OX : 32 * OX] * w8[0:1, 12 * OX : 20 * OX]
    s[:, 20 * OX : 24 * OX] = bottom * w8[0:1, 20 * OX : 24 * OX]


def outer_kernel(
    levels, width,
    f_ref, t_ref, edge_ref, inner_ref, even_ref, odd_ref, s, w8, n8, dif_ref, cmap_ref,
    tt_ref, back_ref,
    fx, se, we8, ne8, d8,
):
    row, rows_atm = lax.axis_index("atm"), lax.axis_size("atm")
    is_even = (row & 1) == 0
    lane = iota((1, 128), 1)
    block = lax.shift_right_arithmetic(lane, 5)
    even, odd = even_ref[...].astype(f32), odd_ref[...].astype(f32)
    top, bottom = jnp.where(is_even, odd, even), jnp.where(is_even, even, odd)
    tops = jnp.where(row > 0, 1.0, 0.0)
    bottoms = jnp.where(row < rows_atm - 1, 1.0, 0.0)

    def wide_wet(x):
        return jnp.broadcast_to(x[levels : levels + 1, :], (8, x.shape[1]))

    fx[:, OX : 4 * OX] = top[:, 0 : 3 * OX]
    fx[:, 4 * OX : 12 * OX] = f_ref[:, 0 : 8 * OX]
    fx[:, 12 * OX : 20 * OX] = f_ref[:, 24 * OX : 32 * OX]
    fx[:, 20 * OX : 23 * OX] = bottom[:, 0 : 3 * OX]
    outside = not_there(lane)
    for at, f_part, t_part, there in (
        (0, top[:, 384:512], top[:, 512:640], tops),
        (1, edge_ref[:, 0:128], edge_ref[:, 512:640], None),
        (2, edge_ref[:, 128:256], edge_ref[:, 640:768], None),
        (3, edge_ref[:, 256:384], edge_ref[:, 768:896], None),
        (4, edge_ref[:, 384:512], edge_ref[:, 896:1024], None),
        (5, bottom[:, 384:512], bottom[:, 512:640], bottoms),
    ):
        wet = jnp.where(outside, 0.0, wide_wet(t_part))
        wet = wet if there is None else wet * there
        we8[:, at * OX : (at + 1) * OX] = wet
        se[:, at * OX : (at + 1) * OX] = t_part * wet[0:1, :]
        se[:, (6 + at) * OX : (7 + at) * OX] = f_part

    def ends(parts, j):
        before = parts[j] if j % 3 == 0 else jnp.where(block == 3, parts[j - 1], parts[j])
        after = parts[j] if j % 3 == 2 else jnp.where(block == 0, parts[j + 1], parts[j])
        return roll(before, 32), roll(after, 96)

    parts = [tile_row(we8, j) for j in range(6)]
    for j in range(6):
        up, down = ends(parts, j)
        ne8[:, j * OX : (j + 1) * OX] = up + down + roll(parts[j], 1) + roll(parts[j], -1)
    fill_diffusivity(d8, dif_ref)
    tt_ref[:, 4 * OX : 28 * OX] = inner_ref[:, 4 * OX : 28 * OX]

    def group(g, carry):
        lev = pl.ds(pl.multiple_of(g * 8, 8), 8)
        dif = d8[lev, :]

        def load(ref, j):
            return ref[lev, j * OX : (j + 1) * OX]

        slabs = []
        for base in (0, 12):
            slabs += substep_rows(
                [load(s, base + y) for y in range(12)], lambda y: load(fx, base + y),
                lambda y: tile_row(w8, base + y), lambda y: tile_row(n8, base + y), dif,
            )
        now = substep_strips(
            [load(se, j) for j in range(6)], [load(se, 6 + j) for j in range(6)],
            [tile_row(we8, j) for j in range(6)], [tile_row(ne8, j) for j in range(6)], dif, ends,
        )
        for m in range(4):
            for y, slab, line in ((m, 4 + m, now[1]), (28 + m, 16 + m, now[4])):
                value = merged(line, slabs[slab], lane, m)
                tt_ref[lev, y * OX : (y + 1) * OX] = jnp.where(
                    tile_row(w8, slab) > 0.0, value, load(t_ref, y)
                )
        return carry

    lax.fori_loop(0, width // 8, group, 0)
    source = stacked(tt_ref[...].astype(bf16))
    back_ref[...] = gather(source, cmap_ref[0:1, :], cmap_ref[1:2, :], width).astype(bf16)


def state_kernel(levels, inv_ref, sw_ref, sm_ref, state_ref, out_ref, h_ref, sm_pad):
    sm_pad[...] = jnp.zeros_like(sm_pad)
    sm_pad[0:levels, :] = sm_ref[...]
    blocks = state_ref.shape[1] // NVAR
    for v in range(NVAR):
        inv = inv_ref[:, v, :]
        both = split(three(nn, inv, three(nt, sw_ref[:, v, :], sm_pad[...])))
        h_ref[v, 0], h_ref[v, 1] = both
        high, low = split(three(nn, inv, inv))
        for c in range(0, blocks, 2):
            sh, sl = split(column_block(state_ref, v, c, 2))
            out_ref[v, :, c * 128 : (c + 2) * 128] = nn(high, sh) + nn(high, sl) + nn(low, sh)


def sum_kernel(levels, width, tt_ref, omap_ref, oarea_ref, out_ref, tracer_ref):
    for y in range(OY):
        tracer_ref[pl.ds(y, levels, stride=OY), :] = tt_ref[0:levels, y * OX : (y + 1) * OX]
    count = out_ref.shape[1] // 256
    chunk = 1024
    total = None
    for start in range(0, OCELLS, chunk):
        at = slice(start, start + chunk)
        value = tt_ref[:, at] * oarea_ref[:, at]
        part = spread(value, omap_ref[0:1, at], omap_ref[1:2, at], count)
        total = part if total is None else total + part
    for h in range(count):
        out_ref[:, h * 256 : (h + 1) * 256] = total[h * width : (h + 1) * width]


def final_kernel(peers, width, smap_ref, sarea_ref, sum_ref, h_ref, base_ref, *rest):
    got = rest[: peers - 1]
    out_ref, sums = rest[peers - 1 :]
    step = pl.program_id(0)
    columns = sum_ref.shape[1]
    count = columns // 256

    @pl.when(step == 0)
    def _():
        me = lax.axis_index("ocn")
        segment = smap_ref[2:3, :]
        total = jnp.zeros((width, segment.shape[1]), f32)
        for mask in range(1, peers):
            offset = ((me ^ mask) - me) & (peers - 1)
            total = jnp.where(segment == offset, got[mask - 1][...].astype(f32), total)
        part = spread(total * sarea_ref[...], smap_ref[0:1, :], smap_ref[1:2, :], count)
        for h in range(count):
            at = slice(h * 256, (h + 1) * 256)
            sums[:, at] = part[h * width : (h + 1) * width] + sum_ref[:, at]

    size, rows, lanes = out_ref.shape
    lines = out_ref.reshape(size * rows, lanes)
    blocks = rows // NVAR
    first = pl.multiple_of(step * (blocks * 128), blocks * 128)
    sh, sl = split(sums[:, pl.ds(first, blocks * 128)])
    for v in range(NVAR):
        hh, hl = h_ref[v, 0], h_ref[v, 1]
        value = base_ref[v] + (nn(hh, sh) + nn(hh, sl) + nn(hl, sh))
        for c in range(blocks):
            lines[pl.ds(c * NVAR + v, size, stride=rows), :] = value[:, c * 128 : (c + 1) * 128]


def on_device(
    atmos_state, inverses, flux_weight, surface_weight, area_table, xc_column, xc_dest, xc_cell,
    xc_class, tracer, land_sea, forcing_weight, surface_map, diffusivity,
):
    peers, tiles = lax.axis_size("ocn"), lax.axis_size("atm")
    vars_, size, columns = atmos_state.shape
    cells = xc_column.shape[0]
    levels = tracer.shape[0]
    slots = cells - 3 * cells // peers
    width = -(-(levels + 3) // 16) * 16
    borders = sorted({i ^ (i + 1) for i in range(peers - 1)})
    sds = jax.ShapeDtypeStruct
    params = pltpu.CompilerParams(vmem_limit_bytes=30 * 1024 * 1024)
    vmem = pl.BlockSpec(memory_space=pltpu.VMEM)

    def swap(x, axis, pairs):
        return lax.ppermute(x, axis, pairs)

    def xor_swap(x, mask):
        return swap(x, "ocn", [(i, i ^ mask) for i in range(peers)])

    blocks = columns // 128
    by_level = lambda x: x.transpose(1, 0, 2)
    state = atmos_state.reshape(vars_, size, blocks, 128).transpose(1, 2, 0, 3)
    state = state.reshape(size, blocks * vars_, 128)
    inverse = by_level(inverses[0])
    hbm = pl.BlockSpec(memory_space=pltpu.HBM)
    anywhere = pl.BlockSpec(memory_space=pl.ANY)
    grid_of = lambda x: x.reshape(cells // 128, 128)
    small = [
        area_table, grid_of(xc_column), grid_of(xc_dest), grid_of(xc_cell), grid_of(xc_class),
        inverse, by_level(flux_weight), forcing_weight, tracer.reshape(levels * OY, OX), land_sea,
    ]
    outs = pl.pallas_call(
        functools.partial(send_kernel, peers, levels, width, borders),
        out_shape=[sds((width, slots), bf16)]
        + [sds((width, slots + 256), bf16)] * len(borders)
        + [sds((width, 4 * OX), bf16)] * 2
        + [
            sds((2, width, columns), bf16), sds((width, OCELLS), f32), sds((2, OCELLS), i32),
            sds((1, OCELLS), f32), sds((3, slots), i32), sds((1, slots), f32),
            sds(state.shape, f32),
        ],
        in_specs=[hbm] * 11,
        out_specs=[vmem] * (10 + len(borders)),
        scratch_shapes=[pltpu.SMEM(small[0].shape, f32)]
        + [pltpu.VMEM(x.shape, x.dtype) for x in small[1:]]
        + [
            pltpu.VMEM((width, forcing_weight.shape[1]), f32),
            pltpu.SemaphoreType.DMA((len(small),)), pltpu.SemaphoreType.DMA((4,)),
        ],
        compiler_params=params,
        name="send",
    )(*[pltpu.with_memory_space_constraint(x, pltpu.HBM) for x in small + [state]])
    packed, sides = outs[0], outs[1 : 1 + len(borders)]
    even_t, odd_t, forcing_cols, t0, omap, oarea, smap, sarea, state = outs[1 + len(borders) :]
    got = []
    for mask in range(1, peers):
        buffer = sides[borders.index(mask)] if mask in borders else packed
        got.append(xor_swap(buffer, mask))

    first = [(i, i ^ 1) for i in range(tiles)]
    second = [(i, (i + 1) % tiles if i & 1 else (i - 1) % tiles) for i in range(tiles)]
    even_t, odd_t = swap(even_t, "atm", first), swap(odd_t, "atm", second)

    local = pl.pallas_call(
        functools.partial(local_kernel, width),
        out_shape=sds((width, OCELLS), f32),
        in_specs=[vmem] * 3, out_specs=vmem, compiler_params=params, name="local",
    )(forcing_cols, omap, oarea)

    slab = 24 * OX
    slabs = pl.pallas_call(
        functools.partial(slab_kernel, levels),
        out_shape=[sds((width, slab), f32), sds((8, slab), f32), sds((8, slab), f32)],
        in_specs=[vmem] * 3, out_specs=[vmem] * 3, compiler_params=params, name="slab",
    )(t0, even_t, odd_t)

    base, back_map = pl.pallas_call(
        functools.partial(state_kernel, levels),
        out_shape=[sds((vars_, size, columns), f32), sds((vars_, 2, size, width), bf16)],
        in_specs=[vmem] * 4, out_specs=[vmem] * 2,
        scratch_shapes=[pltpu.VMEM((width, surface_map.shape[1]), f32)],
        compiler_params=params, name="state",
    )(inverse, by_level(surface_weight), surface_map, state)

    send_rows = 5 * OX
    f_all, fs, ts, cmap, even, odd, edge = pl.pallas_call(
        functools.partial(receive_kernel, peers, levels, width, borders),
        out_shape=[
            sds((width, OCELLS), f32), sds((width, STRIPS * OX), f32),
            sds((width, STRIPS * OX), f32), sds((2, slots), i32),
            sds((width, send_rows), bf16), sds((width, send_rows), bf16),
            sds((width, 8 * OX), f32),
        ],
        in_specs=[anywhere] * 2 + [vmem] * (3 + peers), out_specs=[vmem] * 7,
        compiler_params=params, name="receive",
    )(slabs[2], back_map, packed, smap, local, t0, *got)
    even, odd = swap(even, "atm", first), swap(odd, "atm", second)

    dif = diffusivity.reshape(1, levels)
    scratch = lambda *shapes: [pltpu.VMEM(shape, f32) for shape in shapes]
    inner = pl.pallas_call(
        functools.partial(inner_kernel, levels, width),
        out_shape=sds((width, OCELLS), f32),
        in_specs=[vmem] * 5, out_specs=vmem,
        scratch_shapes=scratch(
            (8, OCELLS), (8, OCELLS), (8, STRIPS * OX), (8, STRIPS * OX), (width, OX),
        ),
        compiler_params=params, name="inner",
    )(f_all, fs, t0, ts, dif)
    t4, back = pl.pallas_call(
        functools.partial(outer_kernel, levels, width),
        out_shape=[sds((width, OCELLS), f32), sds((width, slots), bf16)],
        in_specs=[vmem] * 11, out_specs=[vmem] * 2,
        scratch_shapes=scratch(
            (width, slab), (width, 12 * OX), (8, 6 * OX), (8, 6 * OX), (width, OX),
        ),
        compiler_params=params, name="outer",
    )(f_all, t0, edge, inner, even, odd, *slabs, dif, cmap)

    returned = [xor_swap(back, mask) for mask in range(1, peers)]
    sums, tracer_out = pl.pallas_call(
        functools.partial(sum_kernel, levels, width),
        out_shape=[sds((width, columns), f32), sds((levels * OY, OX), f32)],
        in_specs=[vmem] * 3, out_specs=[vmem] * 2, compiler_params=params, name="sum",
    )(t4, omap, oarea)

    block = 512
    final_state = pl.pallas_call(
        functools.partial(final_kernel, peers, width),
        out_shape=sds((size, blocks * vars_, 128), f32),
        grid=(columns // block,),
        in_specs=[
            pl.BlockSpec(smap.shape, lambda i: (0, 0)),
            pl.BlockSpec(sarea.shape, lambda i: (0, 0)),
            pl.BlockSpec((width, columns), lambda i: (0, 0)),
            pl.BlockSpec(back_map.shape, lambda i: (0, 0, 0, 0)),
            pl.BlockSpec((vars_, size, block), lambda i: (0, 0, i)),
        ]
        + [pl.BlockSpec((width, slots), lambda i: (0, 0))] * (peers - 1),
        out_specs=pl.BlockSpec((size, block // 128 * vars_, 128), lambda i: (0, i, 0)),
        scratch_shapes=[pltpu.VMEM((width, columns), f32)],
        compiler_params=params, name="final",
    )(smap, sarea, sums, back_map, base, *returned)
    final_state = final_state.reshape(size, blocks, vars_, 128).transpose(2, 0, 1, 3)
    final_state = final_state.reshape(vars_, size, columns)
    return (final_state, tracer_out.reshape(tracer.shape))


def solution(mesh):
    in_specs = (
        P(None, None, ("member", "atm", "ocn")),
        P("atm", None, None, None),
        P(),
        P(),
        P(),
        P(("atm", "ocn")),
        P(("atm", "ocn"), None),
        P(("atm", "ocn")),
        P(("atm", "ocn")),
        P(None, "atm", ("member", "ocn")),
        P("atm", "ocn"),
        P(),
        P(),
        P(),
    )
    out_specs = (P(None, None, ("member", "atm", "ocn")), P(None, "atm", ("member", "ocn")))
    return jax.shard_map(
        on_device, mesh=mesh, in_specs=in_specs, out_specs=out_specs, check_vma=False
    )
```

time: 98.5 us -> 62.7 us (0.64)
  local copies, waits for them, and re-layouts: 20.1 us -> 0.02 us
  waiting for transfers between devices: 13.2 us -> 1.04 us
  Pallas kernels: 52 us -> 46.5 us
  starting transfers between devices: 12.1 us -> 14.3 us
    unnamed x25 -> x8, local copies, waits for them, and re-layouts: 20.1 us -> 0.02 us
    ppermute x8 -> x10, waiting for transfers between devices: 13.2 us -> 1.04 us  [swap(): return lax.ppermute(x, axis, pairs)]
    pallas_call x1, Pallas kernels: 6 us -> 2.73 us  [on_device(): pl.pallas_call(functools.partial(receive_kernel, peers, levels, width, bo...]
    pallas_call x1, Pallas kernels: 8.19 us -> 5.36 us  [on_device(): pl.pallas_call(functools.partial(final_kernel, peers, width), out_shape=s...]
    ppermute x8 -> x10, starting transfers between devices: 12.1 us -> 14.3 us  [swap(): return lax.ppermute(x, axis, pairs)]
    pallas_call x1, Pallas kernels: 9.15 us -> 11.2 us  [on_device(): pl.pallas_call(functools.partial(send_kernel, peers, levels, width, borde...]
    pallas_call x3 -> x5, Pallas kernels: 24.8 us -> 24.1 us  [the longest x1 6.68 us: on_device(): pl.pallas_call(functools.partial(inner_kernel, levels, width), out_shape=...]
  transfers between devices with their start and end apart: 8 -> 10, of which waited for: 3 -> 1; matrix products, arithmetic and copies ran while one was open for 1% -> 0% of each run, Pallas kernels for 16% -> 34%
where the time goes in v2:
time: 62.7 us; the launch traced here: 62.6 us
  Pallas kernels  46.5 us (74%)
  starting transfers between devices  14.3 us (23%)
  waiting for transfers between devices  1.04 us (2%)
  between operations  0.78 us (1%)
    ppermute x10, starting transfers between devices, swap(): return lax.ppermute(x, axis, pairs)  14.3 us
    pallas_call x1, Pallas kernels, on_device(): pl.pallas_call(functools.partial(send_kernel, peers, levels, width, borde...  11.2 us
    pallas_call x1, Pallas kernels, on_device(): pl.pallas_call(functools.partial(inner_kernel, levels, width), out_shape=...  6.68 us
    pallas_call x1, Pallas kernels, on_device(): pl.pallas_call(functools.partial(state_kernel, levels), out_shape=[sds((v...  6.36 us
    pallas_call x1, Pallas kernels, on_device(): pl.pallas_call(functools.partial(outer_kernel, levels, width), out_shape=...  5.78 us
    pallas_call x1, Pallas kernels, on_device(): pl.pallas_call(functools.partial(final_kernel, peers, width), out_shape=s...  5.36 us
    pallas_call x1, Pallas kernels, on_device(): pl.pallas_call(functools.partial(sum_kernel, levels, width), out_shape=[s...  5.17 us
    pallas_call x1, Pallas kernels, on_device(): pl.pallas_call(functools.partial(local_kernel, width), out_shape=sds((wid...  3.06 us
  transfers between devices with their start and end apart: 10, of which 1 were waited for; matrix products, arithmetic and copies ran while one was open for 0% of the time, Pallas kernels for 34%

profile of v2, /device:TPU:0, one launch (start us, length us, event | category | flops | bytes accessed | tf_op | source)
XLA Modules:
  0.0 62.6 jit_solution(3400548795580832751)
XLA Ops:
  0.6 0.0 copy-start
  0.6 0.0 copy-start.1
  0.7 0.0 copy-start.2
  0.7 11.2 %send.1 = (bf16[80,1024]{1,0:T(8,128)(2,1)S(1)}, bf16[80,1280]{1,0:T(8,128)(2,1)S(1)}, bf16[80,1280]{1,0:T(8,128)(2,1)S(1)}, bf16[80,512]{1,0:T(8,128)(2,1)S(1)}...) custom-call(f32[64]{0:T(128)} %refs_0_.1, ...), custom_call_target="tpu_custom_call" | custom-call | tf_op jit(solution)/shard_map/send/pallas_call | solution.py:710
  11.9 3.0 %collective-permute-start.2 = (bf16[80,1280]{1,0:T(8,128)(2,1)S(1)}, bf16[80,1280]{1,0:T(8,128)(2,1)S(1)}, u32[]{:S(2)}, u32[]{:S(2)}) collective-permute-start(bf16[80,1280]{1,0:T(8,128)(2,1)S(1)} %get-tuple-element.42), channel_id=1, source_target_pairs={{0,1},{1,0},{2,3},{3,2},{4,5},{5,4},{6,7},{7,6},{8,9},{9,8},{10,11... | collective-permute-start | bytes 614408 | tf_op jit(solution)/shard_map/ppermute | solution.py:693
  14.9 1.5 %collective-permute-start.4 = (bf16[80,1280]{1,0:T(8,128)(2,1)S(1)}, bf16[80,1280]{1,0:T(8,128)(2,1)S(1)}, u32[]{:S(2)}, u32[]{:S(2)}) collective-permute-start(bf16[80,1280]{1,0:T(8,128)(2,1)S(1)} %get-tuple-element.43), channel_id=1, source_target_pairs={{0,3},{1,2},{2,1},{3,0},{4,7},{5,6},{6,5},{7,4},{8,11},{9,10},{10,... | collective-permute-start | bytes 614408 | tf_op jit(solution)/shard_map/ppermute | solution.py:693
  16.4 0.0 collective-permute-start.3
  16.4 2.0 %collective-permute-start = (bf16[80,512]{1,0:T(8,128)(2,1)S(1)}, bf16[80,512]{1,0:T(8,128)(2,1)S(1)}, u32[]{:S(2)}, u32[]{:S(2)}) collective-permute-start(bf16[80,512]{1,0:T(8,128)(2,1)S(1)} %get-tuple-element.33), channel_id=1, source_target_pairs={{0,4},{4,0},{8,12},{12,8},{1,5},{5,1},{9,13},{13,9},{2,6},{6,2},{1... | collective-permute-start | bytes 245768 | tf_op jit(solution)/shard_map/ppermute | solution.py:693
  18.5 2.5 %collective-permute-start.1 = (bf16[80,512]{1,0:T(8,128)(2,1)S(1)}, bf16[80,512]{1,0:T(8,128)(2,1)S(1)}, u32[]{:S(2)}, u32[]{:S(2)}) collective-permute-start(bf16[80,512]{1,0:T(8,128)(2,1)S(1)} %get-tuple-element.34), channel_id=1, source_target_pairs={{0,12},{4,8},{8,4},{12,0},{1,13},{5,9},{9,5},{13,1},{2,14},{6,10},... | collective-permute-start | bytes 245768 | tf_op jit(solution)/shard_map/ppermute | solution.py:693
  20.9 0.0 copy-done
  21.0 0.0 copy-done.1
  21.0 0.0 copy-done.2
  21.0 6.4 %state.1 = (f32[4,137,2048]{2,1,0:T(8,128)S(1)}, bf16[4,2,137,80]{3,2,1,0:T(8,128)(2,1)S(1)}) custom-call(f32[137,4,137]{2,1,0:T(4,128)S(1)} %bitcast.23, f32[137,4,128]{2,1,0:T(4,128)S(1)} %bitcast.24, f32[75,128]{1,0:T(8,128)S(1)} %copy-done.2, f32[137,64,128]{2,1,0:T(8,128)S(1)} %get-tuple-element.36.state_ref), custom_call_target="tpu_custom_call" | custom-call | tf_op jit(solution)/shard_map/state/pallas_call | solution.py:755
  27.3 3.1 %local.1.local_ref = f32[80,4096]{1,0:T(8,128)S(1)} custom-call(bf16[2,80,2048]{2,1,0:T(8,128)(2,1)S(1)} %get-tuple-element.39.forcing_ref, s32[2,4096]{1,0:T(2,128)S(1)} %get-tuple-element.40.omap_ref, f32[1,4096]{1,0:T(1,128)S(1)} %get-tuple-element.41.oarea_ref), custom_call_target="tpu_custom_call" | custom-call | tf_op jit(solution)/shard_map/local/pallas_call | solution.py:742
  30.4 0.0 collective-permute-done.even_ref
  30.4 0.0 collective-permute-done.1.odd_ref
  30.4 0.1 slab.1
  30.5 0.0 collective-permute-done.3.rest_1_
  30.5 0.0 collective-permute-done.2.rest_0_
  30.6 0.0 collective-permute-done.4.rest_2_
  30.6 0.0 copy-start.3
  30.6 2.7 %receive.1 = (f32[80,4096]{1,0:T(8,128)S(1)}, f32[80,1024]{1,0:T(8,128)S(1)}, f32[80,1024]{1,0:T(8,128)S(1)}, s32[2,1024]{1,0:T(2,128)S(1)}, bf16[80,640]{1,0:T(...) custom-call(f32[8,3072]{1,0:T(8,128)S(1)} %get-tuple-element.35.early0.n8, ...), custom_call_target="tpu_custom_call" | custom-call | tf_op jit(solution)/shard_map/receive/pallas_call | solution.py:764
  33.3 0.7 %collective-permute-start.5 = (bf16[80,640]{1,0:T(8,128)(2,1)S(1)}, bf16[80,640]{1,0:T(8,128)(2,1)S(1)}, u32[]{:S(2)}, u32[]{:S(2)}) collective-permute-start(bf16[80,640]{1,0:T(8,128)(2,1)S(1)} %get-tuple-element.48), channel_id=1, source_target_pairs={{0,4},{4,0},{8,12},{12,8},{1,5},{5,1},{9,13},{13,9},{2,6},{6,2},{1... | collective-permute-start | bytes 307208 | tf_op jit(solution)/shard_map/ppermute | solution.py:693
  34.1 0.9 %collective-permute-start.6 = (bf16[80,640]{1,0:T(8,128)(2,1)S(1)}, bf16[80,640]{1,0:T(8,128)(2,1)S(1)}, u32[]{:S(2)}, u32[]{:S(2)}) collective-permute-start(bf16[80,640]{1,0:T(8,128)(2,1)S(1)} %get-tuple-element.49), channel_id=1, source_target_pairs={{0,12},{4,8},{8,4},{12,0},{1,13},{5,9},{9,5},{13,1},{2,14},{6,10},... | collective-permute-start | bytes 307208 | tf_op jit(solution)/shard_map/ppermute | solution.py:693
  35.0 0.0 copy-done.3
  35.0 6.7 %inner.1.inner_ref = f32[80,4096]{1,0:T(8,128)S(1)} custom-call(f32[80,4096]{1,0:T(8,128)S(1)} %get-tuple-element.44.f_ref, f32[80,1024]{1,0:T(8,128)S(1)} %get-tuple-element.46.fs_ref, f32[80,4096]{1,0:T(8,128)S(1)} %get-tuple-element.32.t_ref, f32[80,1024]{1,0:T(8,128)S(1)} %get-tuple-element.47.ts_ref, f32[1,75]{1,0:T(1,128)S(1)} %bitcast.25), custom_call_target="tpu_custom_call" | custom-call | tf_op jit(solution)/shard_map/inner/pallas_call | solution.py:779
  41.7 0.0 collective-permute-done.5.even_ref
  41.7 0.0 collective-permute-done.6.odd_ref
  41.7 5.8 %outer.1 = (f32[80,4096]{1,0:T(8,128)S(1)}, bf16[80,1024]{1,0:T(8,128)(2,1)S(1)}) custom-call(f32[80,4096]{1,0:T(8,128)S(1)} %get-tuple-element.44.f_ref, f32[80,4096]{1,0:T(8,128)S(1)} %get-tuple-element.32.t_ref, f32[80,1024]{1,0:T(8,128)S(1)} %get-tuple-element.45.edge_ref, f32[80,4096]{1,0:T(8,128)S(1)} %inner.1.inner_ref, ...), custom_call_target="tpu_custom_call" | custom-call | tf_op jit(solution)/shard_map/outer/pallas_call | solution.py:788
  47.5 1.6 %collective-permute-start.7 = (bf16[80,1024]{1,0:T(8,128)(2,1)S(1)}, bf16[80,1024]{1,0:T(8,128)(2,1)S(1)}, u32[]{:S(2)}, u32[]{:S(2)}) collective-permute-start(bf16[80,1024]{1,0:T(8,128)(2,1)S(1)} %get-tuple-element.56), channel_id=1, source_target_pairs={{0,1},{1,0},{2,3},{3,2},{4,5},{5,4},{6,7},{7,6},{8,9},{9,8},{10,11... | collective-permute-start | bytes 491528 | tf_op jit(solution)/shard_map/ppermute | solution.py:693
  49.0 1.5 %collective-permute-start.8 = (bf16[80,1024]{1,0:T(8,128)(2,1)S(1)}, bf16[80,1024]{1,0:T(8,128)(2,1)S(1)}, u32[]{:S(2)}, u32[]{:S(2)}) collective-permute-start(bf16[80,1024]{1,0:T(8,128)(2,1)S(1)} %get-tuple-element.56), channel_id=1, source_target_pairs={{0,2},{1,3},{2,0},{3,1},{4,6},{5,7},{6,4},{7,5},{8,10},{9,11},{10,... | collective-permute-start | bytes 491528 | tf_op jit(solution)/shard_map/ppermute | solution.py:693
  50.6 0.5 collective-permute-start.9
  51.0 5.2 %sum.1 = (f32[80,2048]{1,0:T(8,128)S(1)}, f32[2400,128]{1,0:T(8,128)}) custom-call(f32[80,4096]{1,0:T(8,128)S(1)} %get-tuple-element.53.tt_ref, s32[2,4096]{1,0:T(2,128)S(1)} %get-tuple-element.40.omap_ref, f32[1,4096]{1,0:T(1,128)S(1)} %get-tuple-element.41.oarea_ref), custom_call_target="tpu_custom_call" | custom-call | tf_op jit(solution)/shard_map/sum/pallas_call | solution.py:799
  56.2 0.0 collective-permute-done.7.rest_0_
  56.2 1.0 %collective-permute-done.8.rest_1_ = bf16[80,1024]{1,0:T(8,128)(2,1)S(1)} collective-permute-done((bf16[80,1024]{1,0:T(8,128)(2,1)S(1)}, bf16[80,1024]{1,0:T(8,128)(2,1)S(1)}, u32[]{:S(2)}, u32[]{:S(2)}) %collective-permute-start.8) | collective-permute-done | bytes 163872 | tf_op jit(solution)/shard_map/ppermute | solution.py:693
  57.2 0.0 collective-permute-done.9.rest_2_
  57.2 5.4 %final.1 = f32[137,64,128]{2,1,0:T(8,128)} custom-call(s32[3,1024]{1,0:T(4,128)S(1)} %get-tuple-element.30.smap_ref, f32[1,1024]{1,0:T(1,128)S(1)} %get-tuple-element.31.sarea_ref, f32[80,2048]{1,0:T(8,128)S(1)} %get-tuple-element.54.sum_ref, bf16[4,2,137,80]{3,2,1,0:T(8,128)(2,1)S(1)} %get-tuple-element.37.early1.h_ref, ...), custom_call_target="tpu_custom_call" | custom-call | tf_op jit(solution)/shard_map/final/pallas_call | solution.py:806
Async XLA Ops:
  0.6 20.3 %copy-start = (f32[1,4,137,137]{3,1,2,0:T(4,128)S(1)}, f32[1,4,137,137]{3,1,2,0:T(4,128)}, u32[]{:S(2)}) copy-start(f32[1,4,137,137]{3,1,2,0:T(4,128)} %param.15) | copy-start | bytes 900916
  0.6 20.3 %copy-start.1 = (f32[4,137,128]{2,0,1:T(4,128)S(1)}, f32[4,137,128]{2,0,1:T(4,128)}, u32[]{:S(2)}) copy-start(f32[4,137,128]{2,0,1:T(4,128)} %param.17) | copy-start | bytes 841732
  0.7 20.3 %copy-start.2 = (f32[75,128]{1,0:T(8,128)S(1)}, f32[75,128]{1,0:T(8,128)}, u32[]{:S(2)}) copy-start(f32[75,128]{1,0:T(8,128)} %sm_ref.1) | copy-start | bytes 115204
  11.9 18.7 %collective-permute-start.2 = (bf16[80,1280]{1,0:T(8,128)(2,1)S(1)}, bf16[80,1280]{1,0:T(8,128)(2,1)S(1)}, u32[]{:S(2)}, u32[]{:S(2)}) collective-permute-start(bf16[80,1280]{1,0:T(8,128)(2,1)S(1)} %get-tuple-element.42), channel_id=1, source_target_pairs={{0,1},{1,0},{2,3},{3,2},{4,5},{5,4},{6,7},{7,6},{8,9},{9,8},{10,11... | collective-permute-start | bytes 614408 | tf_op jit(solution)/shard_map/ppermute | solution.py:693
  14.9 15.7 %collective-permute-start.4 = (bf16[80,1280]{1,0:T(8,128)(2,1)S(1)}, bf16[80,1280]{1,0:T(8,128)(2,1)S(1)}, u32[]{:S(2)}, u32[]{:S(2)}) collective-permute-start(bf16[80,1280]{1,0:T(8,128)(2,1)S(1)} %get-tuple-element.43), channel_id=1, source_target_pairs={{0,3},{1,2},{2,1},{3,0},{4,7},{5,6},{6,5},{7,4},{8,11},{9,10},{10,... | collective-permute-start | bytes 614408 | tf_op jit(solution)/shard_map/ppermute | solution.py:693
  16.4 14.1 %collective-permute-start.3 = (bf16[80,1024]{1,0:T(8,128)(2,1)S(1)}, bf16[80,1024]{1,0:T(8,128)(2,1)S(1)}, u32[]{:S(2)}, u32[]{:S(2)}) collective-permute-start(bf16[80,1024]{1,0:T(8,128)(2,1)S(1)} %get-tuple-element.38.packed_ref), channel_id=1, source_target_pairs={{0,2},{1,3},{2,0},{3,1},{4,6},{5,7},{6,4},{7,5},{8,10},{9,11},{10,... | collective-permute-start | bytes 491528 | tf_op jit(solution)/shard_map/ppermute | solution.py:693
  16.4 13.9 %collective-permute-start = (bf16[80,512]{1,0:T(8,128)(2,1)S(1)}, bf16[80,512]{1,0:T(8,128)(2,1)S(1)}, u32[]{:S(2)}, u32[]{:S(2)}) collective-permute-start(bf16[80,512]{1,0:T(8,128)(2,1)S(1)} %get-tuple-element.33), channel_id=1, source_target_pairs={{0,4},{4,0},{8,12},{12,8},{1,5},{5,1},{9,13},{13,9},{2,6},{6,2},{1... | collective-permute-start | bytes 245768 | tf_op jit(solution)/shard_map/ppermute | solution.py:693
  18.5 11.9 %collective-permute-start.1 = (bf16[80,512]{1,0:T(8,128)(2,1)S(1)}, bf16[80,512]{1,0:T(8,128)(2,1)S(1)}, u32[]{:S(2)}, u32[]{:S(2)}) collective-permute-start(bf16[80,512]{1,0:T(8,128)(2,1)S(1)} %get-tuple-element.34), channel_id=1, source_target_pairs={{0,12},{4,8},{8,4},{12,0},{1,13},{5,9},{9,5},{13,1},{2,14},{6,10},... | collective-permute-start | bytes 245768 | tf_op jit(solution)/shard_map/ppermute | solution.py:693
  30.6 4.4 %copy-start.3 = (f32[75]{0:T(128)S(1)}, f32[75]{0:T(128)}, u32[]{:S(2)}) copy-start(f32[75]{0:T(128)} %param.27) | copy-start | bytes 904
  33.3 8.3 %collective-permute-start.5 = (bf16[80,640]{1,0:T(8,128)(2,1)S(1)}, bf16[80,640]{1,0:T(8,128)(2,1)S(1)}, u32[]{:S(2)}, u32[]{:S(2)}) collective-permute-start(bf16[80,640]{1,0:T(8,128)(2,1)S(1)} %get-tuple-element.48), channel_id=1, source_target_pairs={{0,4},{4,0},{8,12},{12,8},{1,5},{5,1},{9,13},{13,9},{2,6},{6,2},{1... | collective-permute-start | bytes 307208 | tf_op jit(solution)/shard_map/ppermute | solution.py:693
  34.1 7.6 %collective-permute-start.6 = (bf16[80,640]{1,0:T(8,128)(2,1)S(1)}, bf16[80,640]{1,0:T(8,128)(2,1)S(1)}, u32[]{:S(2)}, u32[]{:S(2)}) collective-permute-start(bf16[80,640]{1,0:T(8,128)(2,1)S(1)} %get-tuple-element.49), channel_id=1, source_target_pairs={{0,12},{4,8},{8,4},{12,0},{1,13},{5,9},{9,5},{13,1},{2,14},{6,10},... | collective-permute-start | bytes 307208 | tf_op jit(solution)/shard_map/ppermute | solution.py:693
  47.5 8.7 %collective-permute-start.7 = (bf16[80,1024]{1,0:T(8,128)(2,1)S(1)}, bf16[80,1024]{1,0:T(8,128)(2,1)S(1)}, u32[]{:S(2)}, u32[]{:S(2)}) collective-permute-start(bf16[80,1024]{1,0:T(8,128)(2,1)S(1)} %get-tuple-element.56), channel_id=1, source_target_pairs={{0,1},{1,0},{2,3},{3,2},{4,5},{5,4},{6,7},{7,6},{8,9},{9,8},{10,11... | collective-permute-start | bytes 491528 | tf_op jit(solution)/shard_map/ppermute | solution.py:693
  49.0 8.2 %collective-permute-start.8 = (bf16[80,1024]{1,0:T(8,128)(2,1)S(1)}, bf16[80,1024]{1,0:T(8,128)(2,1)S(1)}, u32[]{:S(2)}, u32[]{:S(2)}) collective-permute-start(bf16[80,1024]{1,0:T(8,128)(2,1)S(1)} %get-tuple-element.56), channel_id=1, source_target_pairs={{0,2},{1,3},{2,0},{3,1},{4,6},{5,7},{6,4},{7,5},{8,10},{9,11},{10,... | collective-permute-start | bytes 491528 | tf_op jit(solution)/shard_map/ppermute | solution.py:693
  50.6 6.7 %collective-permute-start.9 = (bf16[80,1024]{1,0:T(8,128)(2,1)S(1)}, bf16[80,1024]{1,0:T(8,128)(2,1)S(1)}, u32[]{:S(2)}, u32[]{:S(2)}) collective-permute-start(bf16[80,1024]{1,0:T(8,128)(2,1)S(1)} %get-tuple-element.56), channel_id=1, source_target_pairs={{0,3},{1,2},{2,1},{3,0},{4,7},{5,6},{6,5},{7,4},{8,11},{9,10},{10,... | collective-permute-start | bytes 491528 | tf_op jit(solution)/shard_map/ppermute | solution.py:693

commit v3 on v2

--- a/solution.py
+++ b/solution.py
@@ -7,6 +7,7 @@
 from jax.sharding import PartitionSpec as P
 
 OSTEPS = 4
+PAD = 8
 NVAR = 4
 OY = 32
 OX = 128
@@ -168,14 +169,14 @@
     (area_ref, col_ref, dest_ref, cell_ref, class_ref, inv_ref, flux_ref, fw_ref, tracer_ref,
      land_ref) = staged
     loads = [
-        pltpu.make_async_copy(a, b, sems.at[i])
+        pltpu.make_async_copy(a, b.at[:, pl.ds(0, OY), :] if b is tracer_ref else b, sems.at[i])
         for i, (a, b) in enumerate(zip(sources[:10], staged))
     ]
     for load in loads:
         load.start()
     state_hbm = sources[10]
     parts = state_sems.shape[0]
-    part_rows = state_ref.shape[1] // parts
+    part_rows = state_hbm.shape[1] // parts
     state_loads = []
     for i in range(parts):
         at = pl.ds(i * part_rows, part_rows)
@@ -271,14 +272,18 @@
     fw_pad[...] = jnp.zeros_like(fw_pad)
     fw_pad[0:levels, :] = fw_ref[...]
     fw = fw_pad[...]
-    pulled = []
-    for v in range(NVAR):
-        left = wide(doubled(wide(doubled(fw), flux_ref[:, v, :], nt)), inv_ref[:, v, :])
-        pulled.append(doubled(left))
-
+    size = inv_ref.shape[0]
+    flux = flux_ref[...].reshape(size * NVAR, flux_ref.shape[2])
+    mixed = wide(doubled(fw), flux, nt)
+    which = iota((1, size * NVAR), 1) & (NVAR - 1)
+    masked = jnp.concatenate([jnp.where(which == v, mixed, 0.0) for v in range(NVAR)], axis=0)
+    drawn = wide(doubled(masked), inv_ref[...].reshape(size * NVAR, size))
+    pulled = [doubled(drawn[v * width : (v + 1) * width]) for v in range(NVAR)]
+
+    tracer_lines = tracer_ref.reshape(levels * (OY + PAD), OX)
     for y in range(OY):
         at = pl.ds(y * OX, OX)
-        t_ref[0:levels, at] = tracer_ref[pl.ds(y, levels, stride=OY), :]
+        t_ref[0:levels, at] = tracer_lines[pl.ds(y, levels, stride=OY + PAD), :]
         t_ref[levels : levels + 1, at] = land_ref[y : y + 1, :].astype(f32)
         t_ref[levels + 1 : width, at] = jnp.zeros((width - levels - 1, OX), f32)
 
@@ -456,13 +461,17 @@
     return now
 
 
+def tall(ref, j, count):
+    return jnp.concatenate([tile_row(ref, j)] * (count // 8), axis=0)
+
+
 def merged(line, value, lane, b):
     value = jnp.where(lane < 4, roll(line, -(b * 32 + 16)), value)
     return jnp.where(lane >= 124, roll(line, 120 - b * 32), value)
 
 
 def inner_kernel(
-    levels, width, f_ref, fs_ref, t_ref, ts_ref, dif_ref, tt_ref, w8, n8, ws8, ns8, d8
+    levels, width, f_ref, fs_ref, t_ref, ts_ref, dif_ref, tt_ref, strip, w8, n8, ws8, ns8, d8
 ):
     lane = iota((1, 128), 1)
     w8[...] = jnp.broadcast_to(t_ref[levels : levels + 1, :], w8.shape)
@@ -483,6 +492,26 @@
         ns8[:, j * OX : (j + 1) * OX] = up + down + roll(parts[j], 1) + roll(parts[j], -1)
     fill_diffusivity(d8, dif_ref)
 
+    half = width // 2
+
+    def strip_group(g, carry):
+        lev = pl.ds(pl.multiple_of(g * half, 8), half)
+
+        def load(ref, j):
+            return ref[lev, j * OX : (j + 1) * OX]
+
+        wet = [tall(ws8, j, half) for j in range(STRIPS)]
+        now = substep_strips(
+            [load(ts_ref, j) * wet[j] for j in range(STRIPS)],
+            [load(fs_ref, j) for j in range(STRIPS)], wet,
+            [tall(ns8, j, half) for j in range(STRIPS)], d8[lev, :], ends,
+        )
+        for j in range(STRIPS):
+            strip[lev, j * OX : (j + 1) * OX] = now[j]
+        return carry
+
+    lax.fori_loop(0, 2, strip_group, 0)
+
     def group(g, carry):
         lev = pl.ds(pl.multiple_of(g * 8, 8), 8)
         dif = d8[lev, :]
@@ -494,12 +523,7 @@
             [load(t_ref, y) * tile_row(w8, y) for y in range(OY)], lambda y: load(f_ref, y),
             lambda y: tile_row(w8, y), lambda y: tile_row(n8, y), dif,
         )
-        wet = [tile_row(ws8, j) for j in range(STRIPS)]
-        now = substep_strips(
-            [load(ts_ref, j) * wet[j] for j in range(STRIPS)],
-            [load(fs_ref, j) for j in range(STRIPS)], wet,
-            [tile_row(ns8, j) for j in range(STRIPS)], dif, ends,
-        )
+        now = [load(strip, j) for j in range(STRIPS)]
         for y in range(4, OY - 4):
             value = merged(now[y % 8], rows[y], lane, y // 8)
             tt_ref[lev, y * OX : (y + 1) * OX] = jnp.where(
@@ -583,8 +607,26 @@
     fill_diffusivity(d8, dif_ref)
     tt_ref[:, 4 * OX : 28 * OX] = inner_ref[:, 4 * OX : 28 * OX]
 
+    half = width // 2
+
+    def strip_group(g, carry):
+        lev = pl.ds(pl.multiple_of(g * half, 8), half)
+
+        def load(ref, j):
+            return ref[lev, j * OX : (j + 1) * OX]
+
+        now = substep_strips(
+            [load(se, j) for j in range(6)], [load(se, 6 + j) for j in range(6)],
+            [tall(we8, j, half) for j in range(6)], [tall(ne8, j, half) for j in range(6)],
+            d8[lev, :], ends,
+        )
+        se[lev, 0:OX], se[lev, OX : 2 * OX] = now[1], now[4]
+        return carry
+
+    lax.fori_loop(0, 2, strip_group, 0)
+
     def group(g, carry):
-        lev = pl.ds(pl.multiple_of(g * 8, 8), 8)
+        lev = pl.ds(pl.multiple_of(g * 16, 16), 16)
         dif = d8[lev, :]
 
         def load(ref, j):
@@ -594,42 +636,47 @@
         for base in (0, 12):
             slabs += substep_rows(
                 [load(s, base + y) for y in range(12)], lambda y: load(fx, base + y),
-                lambda y: tile_row(w8, base + y), lambda y: tile_row(n8, base + y), dif,
+                lambda y: tall(w8, base + y, 16), lambda y: tall(n8, base + y, 16), dif,
             )
-        now = substep_strips(
-            [load(se, j) for j in range(6)], [load(se, 6 + j) for j in range(6)],
-            [tile_row(we8, j) for j in range(6)], [tile_row(ne8, j) for j in range(6)], dif, ends,
-        )
         for m in range(4):
-            for y, slab, line in ((m, 4 + m, now[1]), (28 + m, 16 + m, now[4])):
+            for y, slab, line in ((m, 4 + m, load(se, 0)), (28 + m, 16 + m, load(se, 1))):
                 value = merged(line, slabs[slab], lane, m)
                 tt_ref[lev, y * OX : (y + 1) * OX] = jnp.where(
-                    tile_row(w8, slab) > 0.0, value, load(t_ref, y)
+                    tall(w8, slab, 16) > 0.0, value, load(t_ref, y)
                 )
         return carry
 
-    lax.fori_loop(0, width // 8, group, 0)
+    lax.fori_loop(0, width // 16, group, 0)
     source = stacked(tt_ref[...].astype(bf16))
     back_ref[...] = gather(source, cmap_ref[0:1, :], cmap_ref[1:2, :], width).astype(bf16)
 
 
-def state_kernel(levels, inv_ref, sw_ref, sm_ref, state_ref, out_ref, h_ref, sm_pad):
+def state_kernel(levels, inv_ref, sw_ref, sm_ref, state_ref, out_ref, h_ref, sm_pad, square):
     sm_pad[...] = jnp.zeros_like(sm_pad)
     sm_pad[0:levels, :] = sm_ref[...]
-    blocks = state_ref.shape[1] // NVAR
+    h_ref[...] = jnp.zeros_like(h_ref)
+    square[...] = jnp.zeros_like(square)
+    blocks = (state_ref.shape[1] - PAD) // NVAR
+    size = inv_ref.shape[0]
+    room = h_ref.shape[0] // (2 * NVAR)
     for v in range(NVAR):
         inv = inv_ref[:, v, :]
-        both = split(three(nn, inv, three(nt, sw_ref[:, v, :], sm_pad[...])))
-        h_ref[v, 0], h_ref[v, 1] = both
-        high, low = split(three(nn, inv, inv))
+        high, low = split(three(nn, inv, three(nt, sw_ref[:, v, :], sm_pad[...])))
+        h_ref[v * room : v * room + size, :] = high
+        h_ref[(NVAR + v) * room : (NVAR + v) * room + size, :] = low
+        square[v, 0:size, :], square[v, room : room + size, :] = split(three(nn, inv, inv))
+    for v in range(NVAR):
         for c in range(0, blocks, 2):
-            sh, sl = split(column_block(state_ref, v, c, 2))
-            out_ref[v, :, c * 128 : (c + 2) * 128] = nn(high, sh) + nn(high, sl) + nn(low, sh)
-
-
-def sum_kernel(levels, width, tt_ref, omap_ref, oarea_ref, out_ref, tracer_ref):
+            value = wide(square[v], column_block(state_ref, v, c, 2))
+            out_ref[v, :, c * 128 : (c + 2) * 128] = value[:size]
+
+
+def sum_kernel(levels, width, tt_ref, omap_ref, oarea_ref, out_ref, tracer_hbm, rows, sem):
+    lines = rows.reshape(levels * (OY + PAD), OX)
     for y in range(OY):
-        tracer_ref[pl.ds(y, levels, stride=OY), :] = tt_ref[0:levels, y * OX : (y + 1) * OX]
+        lines[pl.ds(y, levels, stride=OY + PAD), :] = tt_ref[0:levels, y * OX : (y + 1) * OX]
+    store = pltpu.make_async_copy(rows.at[:, pl.ds(0, OY), :], tracer_hbm, sem)
+    store.start()
     count = out_ref.shape[1] // 256
     chunk = 1024
     total = None
@@ -640,38 +687,45 @@
         total = part if total is None else total + part
     for h in range(count):
         out_ref[:, h * 256 : (h + 1) * 256] = total[h * width : (h + 1) * width]
+    store.wait()
 
 
 def final_kernel(peers, width, smap_ref, sarea_ref, sum_ref, h_ref, base_ref, *rest):
     got = rest[: peers - 1]
-    out_ref, sums = rest[peers - 1 :]
-    step = pl.program_id(0)
+    out_hbm, rows, sums, sems = rest[peers - 1 :]
     columns = sum_ref.shape[1]
     count = columns // 256
-
-    @pl.when(step == 0)
-    def _():
-        me = lax.axis_index("ocn")
-        segment = smap_ref[2:3, :]
-        total = jnp.zeros((width, segment.shape[1]), f32)
-        for mask in range(1, peers):
-            offset = ((me ^ mask) - me) & (peers - 1)
-            total = jnp.where(segment == offset, got[mask - 1][...].astype(f32), total)
-        part = spread(total * sarea_ref[...], smap_ref[0:1, :], smap_ref[1:2, :], count)
-        for h in range(count):
-            at = slice(h * 256, (h + 1) * 256)
-            sums[:, at] = part[h * width : (h + 1) * width] + sum_ref[:, at]
-
-    size, rows, lanes = out_ref.shape
-    lines = out_ref.reshape(size * rows, lanes)
-    blocks = rows // NVAR
-    first = pl.multiple_of(step * (blocks * 128), blocks * 128)
-    sh, sl = split(sums[:, pl.ds(first, blocks * 128)])
-    for v in range(NVAR):
-        hh, hl = h_ref[v, 0], h_ref[v, 1]
-        value = base_ref[v] + (nn(hh, sh) + nn(hh, sl) + nn(hl, sh))
-        for c in range(blocks):
-            lines[pl.ds(c * NVAR + v, size, stride=rows), :] = value[:, c * 128 : (c + 1) * 128]
+    me = lax.axis_index("ocn")
+    segment = smap_ref[2:3, :]
+    total = jnp.zeros((width, segment.shape[1]), f32)
+    for mask in range(1, peers):
+        offset = ((me ^ mask) - me) & (peers - 1)
+        total = jnp.where(segment == offset, got[mask - 1][...].astype(f32), total)
+    part = spread(total * sarea_ref[...], smap_ref[0:1, :], smap_ref[1:2, :], count)
+    for h in range(count):
+        at = slice(h * 256, (h + 1) * 256)
+        sums[:, at] = part[h * width : (h + 1) * width] + sum_ref[:, at]
+
+    size, stride, lanes = rows.shape
+    lines = rows.reshape(size * stride, lanes)
+    parts = sems.shape[0]
+    room = h_ref.shape[0] // (2 * NVAR)
+    stores = []
+    for i in range(parts):
+        share = columns // parts
+        for c in range(i * share, (i + 1) * share, 256):
+            every = wide(h_ref[...], sums[:, c : c + 256])
+            for v in range(NVAR):
+                value = base_ref[v, :, c : c + 256] + every[v * room : v * room + size]
+                for k in range(2):
+                    first = (c // 128 + k) * NVAR + v
+                    lines[pl.ds(first, size, stride=stride), :] = value[:, k * 128 : k * 128 + 128]
+        at = pl.ds(i * (share // 128 * NVAR), share // 128 * NVAR)
+        store = pltpu.make_async_copy(rows.at[:, at, :], out_hbm.at[:, at, :], sems.at[i])
+        store.start()
+        stores.append(store)
+    for store in stores:
+        store.wait()
 
 
 def on_device(
@@ -696,6 +750,7 @@
         return swap(x, "ocn", [(i, i ^ mask) for i in range(peers)])
 
     blocks = columns // 128
+    room = -(-size // 16) * 16
     by_level = lambda x: x.transpose(1, 0, 2)
     state = atmos_state.reshape(vars_, size, blocks, 128).transpose(1, 2, 0, 3)
     state = state.reshape(size, blocks * vars_, 128)
@@ -705,7 +760,7 @@
     grid_of = lambda x: x.reshape(cells // 128, 128)
     small = [
         area_table, grid_of(xc_column), grid_of(xc_dest), grid_of(xc_cell), grid_of(xc_class),
-        inverse, by_level(flux_weight), forcing_weight, tracer.reshape(levels * OY, OX), land_sea,
+        inverse, by_level(flux_weight), forcing_weight, tracer, land_sea,
     ]
     outs = pl.pallas_call(
         functools.partial(send_kernel, peers, levels, width, borders),
@@ -715,12 +770,13 @@
         + [
             sds((2, width, columns), bf16), sds((width, OCELLS), f32), sds((2, OCELLS), i32),
             sds((1, OCELLS), f32), sds((3, slots), i32), sds((1, slots), f32),
-            sds(state.shape, f32),
+            sds((size, blocks * vars_ + PAD, 128), f32),
         ],
         in_specs=[hbm] * 11,
         out_specs=[vmem] * (10 + len(borders)),
         scratch_shapes=[pltpu.SMEM(small[0].shape, f32)]
-        + [pltpu.VMEM(x.shape, x.dtype) for x in small[1:]]
+        + [pltpu.VMEM(x.shape, x.dtype) for x in small[1:8]]
+        + [pltpu.VMEM((levels, OY + PAD, OX), f32), pltpu.VMEM(land_sea.shape, i32)]
         + [
             pltpu.VMEM((width, forcing_weight.shape[1]), f32),
             pltpu.SemaphoreType.DMA((len(small),)), pltpu.SemaphoreType.DMA((4,)),
@@ -754,9 +810,12 @@
 
     base, back_map = pl.pallas_call(
         functools.partial(state_kernel, levels),
-        out_shape=[sds((vars_, size, columns), f32), sds((vars_, 2, size, width), bf16)],
+        out_shape=[sds((vars_, size, columns), f32), sds((2 * vars_ * room, width), bf16)],
         in_specs=[vmem] * 4, out_specs=[vmem] * 2,
-        scratch_shapes=[pltpu.VMEM((width, surface_map.shape[1]), f32)],
+        scratch_shapes=[
+            pltpu.VMEM((width, surface_map.shape[1]), f32),
+            pltpu.VMEM((vars_, 2 * room, size), bf16),
+        ],
         compiler_params=params, name="state",
     )(inverse, by_level(surface_weight), surface_map, state)
 
@@ -781,7 +840,8 @@
         out_shape=sds((width, OCELLS), f32),
         in_specs=[vmem] * 5, out_specs=vmem,
         scratch_shapes=scratch(
-            (8, OCELLS), (8, OCELLS), (8, STRIPS * OX), (8, STRIPS * OX), (width, OX),
+            (width, STRIPS * OX), (8, OCELLS), (8, OCELLS), (8, STRIPS * OX), (8, STRIPS * OX),
+            (width, OX),
         ),
         compiler_params=params, name="inner",
     )(f_all, fs, t0, ts, dif)
@@ -798,30 +858,25 @@
     returned = [xor_swap(back, mask) for mask in range(1, peers)]
     sums, tracer_out = pl.pallas_call(
         functools.partial(sum_kernel, levels, width),
-        out_shape=[sds((width, columns), f32), sds((levels * OY, OX), f32)],
-        in_specs=[vmem] * 3, out_specs=[vmem] * 2, compiler_params=params, name="sum",
+        out_shape=[sds((width, columns), f32), pltpu.HBM(tracer.shape, f32)],
+        in_specs=[vmem] * 3, out_specs=[vmem, hbm],
+        scratch_shapes=[pltpu.VMEM((levels, OY + PAD, OX), f32), pltpu.SemaphoreType.DMA],
+        compiler_params=params, name="sum",
     )(t4, omap, oarea)
 
-    block = 512
     final_state = pl.pallas_call(
         functools.partial(final_kernel, peers, width),
-        out_shape=sds((size, blocks * vars_, 128), f32),
-        grid=(columns // block,),
-        in_specs=[
-            pl.BlockSpec(smap.shape, lambda i: (0, 0)),
-            pl.BlockSpec(sarea.shape, lambda i: (0, 0)),
-            pl.BlockSpec((width, columns), lambda i: (0, 0)),
-            pl.BlockSpec(back_map.shape, lambda i: (0, 0, 0, 0)),
-            pl.BlockSpec((vars_, size, block), lambda i: (0, 0, i)),
-        ]
-        + [pl.BlockSpec((width, slots), lambda i: (0, 0))] * (peers - 1),
-        out_specs=pl.BlockSpec((size, block // 128 * vars_, 128), lambda i: (0, i, 0)),
-        scratch_shapes=[pltpu.VMEM((width, columns), f32)],
+        out_shape=pltpu.HBM((size, blocks * vars_, 128), f32),
+        in_specs=[vmem] * (4 + peers), out_specs=hbm,
+        scratch_shapes=[
+            pltpu.VMEM((size, blocks * vars_ + PAD, 128), f32), pltpu.VMEM((width, columns), f32),
+            pltpu.SemaphoreType.DMA((4,)),
+        ],
         compiler_params=params, name="final",
     )(smap, sarea, sums, back_map, base, *returned)
     final_state = final_state.reshape(size, blocks, vars_, 128).transpose(2, 0, 1, 3)
     final_state = final_state.reshape(vars_, size, columns)
-    return (final_state, tracer_out.reshape(tracer.shape))
+    return (final_state, tracer_out)
 
 
 def solution(mesh):

time: 62.7 us -> 55.5 us (0.89)
  Pallas kernels: 46.5 us -> 38.1 us
  waiting for transfers between devices: 1.04 us -> 1.97 us
    pallas_call x1, Pallas kernels: 11.2 us -> 7.47 us  [on_device(): pl.pallas_call(functools.partial(send_kernel, peers, levels, width, borde...]
    pallas_call x1, Pallas kernels: 6.36 us -> 4.87 us  [on_device(): pl.pallas_call(functools.partial(state_kernel, levels), out_shape=[sds((v...]
    pallas_call x1, Pallas kernels: 5.78 us -> 4.59 us  [on_device(): pl.pallas_call(functools.partial(outer_kernel, levels, width), out_shape=...]
    pallas_call x1, Pallas kernels: 6.68 us -> 5.56 us  [on_device(): pl.pallas_call(functools.partial(inner_kernel, levels, width), out_shape=...]
    ppermute x10, waiting for transfers between devices: 1.04 us -> 1.97 us  [swap(): return lax.ppermute(x, axis, pairs)]
    pallas_call x1, Pallas kernels: 5.17 us -> 4.25 us  [on_device(): pl.pallas_call(functools.partial(sum_kernel, levels, width), out_shape=[s...]
  transfers between devices with their start and end apart: 10 -> 10, of which waited for: 1 -> 2; matrix products, arithmetic and copies ran while one was open for 0% -> 0% of each run, Pallas kernels for 34% -> 33%
where the time goes in v3:
time: 55.5 us; the launch traced here: 55.3 us
  Pallas kernels  38.1 us (69%)
  starting transfers between devices  14.3 us (26%)
  waiting for transfers between devices  1.97 us (4%)
  between operations  0.94 us (2%)
    ppermute x10, starting transfers between devices, swap(): return lax.ppermute(x, axis, pairs)  14.3 us
    pallas_call x1, Pallas kernels, on_device(): pl.pallas_call(functools.partial(send_kernel, peers, levels, width, borde...  7.47 us
    pallas_call x1, Pallas kernels, on_device(): pl.pallas_call(functools.partial(inner_kernel, levels, width), out_shape=...  5.56 us
    pallas_call x1, Pallas kernels, on_device(): pl.pallas_call(functools.partial(final_kernel, peers, width), out_shape=p...  5.27 us
    pallas_call x1, Pallas kernels, on_device(): pl.pallas_call(functools.partial(state_kernel, levels), out_shape=[sds((v...  4.87 us
    pallas_call x1, Pallas kernels, on_device(): pl.pallas_call(functools.partial(outer_kernel, levels, width), out_shape=...  4.59 us
    pallas_call x1, Pallas kernels, on_device(): pl.pallas_call(functools.partial(sum_kernel, levels, width), out_shape=[s...  4.25 us
    pallas_call x1, Pallas kernels, on_device(): pl.pallas_call(functools.partial(local_kernel, width), out_shape=sds((wid...  3.27 us
  transfers between devices with their start and end apart: 10, of which 2 were waited for; matrix products, arithmetic and copies ran while one was open for 0% of the time, Pallas kernels for 33%

profile of v3, /device:TPU:0, one launch (start us, length us, event | category | flops | bytes accessed | tf_op | source)
XLA Modules:
  0.0 55.3 jit_solution(2985221243347633589)
XLA Ops:
  0.6 0.0 copy-start
  0.6 0.0 copy-start.1
  0.7 0.0 copy-start.2
  0.7 7.5 %send.1 = (bf16[80,1024]{1,0:T(8,128)(2,1)S(1)}, bf16[80,1280]{1,0:T(8,128)(2,1)S(1)}, bf16[80,1280]{1,0:T(8,128)(2,1)S(1)}, bf16[80,512]{1,0:T(8,128)(2,1)S(1)}...) custom-call(f32[64]{0:T(128)} %refs_0_.1, ...), custom_call_target="tpu_custom_call" | custom-call | tf_op jit(solution)/shard_map/send/pallas_call | solution.py:765
  8.1 3.0 %collective-permute-start.2 = (bf16[80,1280]{1,0:T(8,128)(2,1)S(1)}, bf16[80,1280]{1,0:T(8,128)(2,1)S(1)}, u32[]{:S(2)}, u32[]{:S(2)}) collective-permute-start(bf16[80,1280]{1,0:T(8,128)(2,1)S(1)} %get-tuple-element.42), channel_id=1, source_target_pairs={{0,1},{1,0},{2,3},{3,2},{4,5},{5,4},{6,7},{7,6},{8,9},{9,8},{10,11... | collective-permute-start | bytes 614408 | tf_op jit(solution)/shard_map/ppermute | solution.py:747
  11.1 1.5 %collective-permute-start.4 = (bf16[80,1280]{1,0:T(8,128)(2,1)S(1)}, bf16[80,1280]{1,0:T(8,128)(2,1)S(1)}, u32[]{:S(2)}, u32[]{:S(2)}) collective-permute-start(bf16[80,1280]{1,0:T(8,128)(2,1)S(1)} %get-tuple-element.43), channel_id=1, source_target_pairs={{0,3},{1,2},{2,1},{3,0},{4,7},{5,6},{6,5},{7,4},{8,11},{9,10},{10,... | collective-permute-start | bytes 614408 | tf_op jit(solution)/shard_map/ppermute | solution.py:747
  12.6 0.0 collective-permute-start.3
  12.7 2.0 %collective-permute-start = (bf16[80,512]{1,0:T(8,128)(2,1)S(1)}, bf16[80,512]{1,0:T(8,128)(2,1)S(1)}, u32[]{:S(2)}, u32[]{:S(2)}) collective-permute-start(bf16[80,512]{1,0:T(8,128)(2,1)S(1)} %get-tuple-element.33), channel_id=1, source_target_pairs={{0,4},{4,0},{8,12},{12,8},{1,5},{5,1},{9,13},{13,9},{2,6},{6,2},{1... | collective-permute-start | bytes 245768 | tf_op jit(solution)/shard_map/ppermute | solution.py:747
  14.7 2.5 %collective-permute-start.1 = (bf16[80,512]{1,0:T(8,128)(2,1)S(1)}, bf16[80,512]{1,0:T(8,128)(2,1)S(1)}, u32[]{:S(2)}, u32[]{:S(2)}) collective-permute-start(bf16[80,512]{1,0:T(8,128)(2,1)S(1)} %get-tuple-element.34), channel_id=1, source_target_pairs={{0,12},{4,8},{8,4},{12,0},{1,13},{5,9},{9,5},{13,1},{2,14},{6,10},... | collective-permute-start | bytes 245768 | tf_op jit(solution)/shard_map/ppermute | solution.py:747
  17.2 0.0 copy-done
  17.2 0.0 copy-done.1
  17.2 0.0 copy-done.2
  17.2 4.9 %state.1 = (f32[4,137,2048]{2,1,0:T(8,128)S(1)}, bf16[1152,80]{1,0:T(8,128)(2,1)S(1)}) custom-call(f32[137,4,137]{2,1,0:T(4,128)S(1)} %bitcast.21, f32[137,4,128]{2,1,0:T(4,128)S(1)} %bitcast.22, f32[75,128]{1,0:T(8,128)S(1)} %copy-done.2, f32[137,72,128]{2,1,0:T(8,128)S(1)} %get-tuple-element.36.state_ref), custom_call_target="tpu_custom_call" | custom-call | tf_op jit(solution)/shard_map/state/pallas_call | solution.py:811
  22.1 3.3 %local.1.local_ref = f32[80,4096]{1,0:T(8,128)S(1)} custom-call(bf16[2,80,2048]{2,1,0:T(8,128)(2,1)S(1)} %get-tuple-element.39.forcing_ref, s32[2,4096]{1,0:T(2,128)S(1)} %get-tuple-element.40.omap_ref, f32[1,4096]{1,0:T(1,128)S(1)} %get-tuple-element.41.oarea_ref), custom_call_target="tpu_custom_call" | custom-call | tf_op jit(solution)/shard_map/local/pallas_call | solution.py:798
  25.3 0.0 collective-permute-done.even_ref
  25.3 0.0 collective-permute-done.1.odd_ref
  25.4 0.1 slab.1
  25.5 0.0 collective-permute-done.3.rest_1_
  25.5 0.0 collective-permute-done.2.rest_0_
  25.5 0.0 collective-permute-done.4.rest_2_
  25.5 0.0 copy-start.3
  25.5 2.7 %receive.1 = (f32[80,4096]{1,0:T(8,128)S(1)}, f32[80,1024]{1,0:T(8,128)S(1)}, f32[80,1024]{1,0:T(8,128)S(1)}, s32[2,1024]{1,0:T(2,128)S(1)}, bf16[80,640]{1,0:T(...) custom-call(f32[8,3072]{1,0:T(8,128)S(1)} %get-tuple-element.35.early0.n8, ...), custom_call_target="tpu_custom_call" | custom-call | tf_op jit(solution)/shard_map/receive/pallas_call | solution.py:823
  28.3 0.7 %collective-permute-start.5 = (bf16[80,640]{1,0:T(8,128)(2,1)S(1)}, bf16[80,640]{1,0:T(8,128)(2,1)S(1)}, u32[]{:S(2)}, u32[]{:S(2)}) collective-permute-start(bf16[80,640]{1,0:T(8,128)(2,1)S(1)} %get-tuple-element.48), channel_id=1, source_target_pairs={{0,4},{4,0},{8,12},{12,8},{1,5},{5,1},{9,13},{13,9},{2,6},{6,2},{1... | collective-permute-start | bytes 307208 | tf_op jit(solution)/shard_map/ppermute | solution.py:747
  29.0 0.9 %collective-permute-start.6 = (bf16[80,640]{1,0:T(8,128)(2,1)S(1)}, bf16[80,640]{1,0:T(8,128)(2,1)S(1)}, u32[]{:S(2)}, u32[]{:S(2)}) collective-permute-start(bf16[80,640]{1,0:T(8,128)(2,1)S(1)} %get-tuple-element.49), channel_id=1, source_target_pairs={{0,12},{4,8},{8,4},{12,0},{1,13},{5,9},{9,5},{13,1},{2,14},{6,10},... | collective-permute-start | bytes 307208 | tf_op jit(solution)/shard_map/ppermute | solution.py:747
  29.9 0.0 copy-done.3
  29.9 5.6 %inner.1.inner_ref = f32[80,4096]{1,0:T(8,128)S(1)} custom-call(f32[80,4096]{1,0:T(8,128)S(1)} %get-tuple-element.44.f_ref, f32[80,1024]{1,0:T(8,128)S(1)} %get-tuple-element.46.fs_ref, f32[80,4096]{1,0:T(8,128)S(1)} %get-tuple-element.32.t_ref, f32[80,1024]{1,0:T(8,128)S(1)} %get-tuple-element.47.ts_ref, f32[1,75]{1,0:T(1,128)S(1)} %bitcast.23), custom_call_target="tpu_custom_call" | custom-call | tf_op jit(solution)/shard_map/inner/pallas_call | solution.py:838
  35.5 0.0 collective-permute-done.5.even_ref
  35.5 0.1 collective-permute-done.6.odd_ref
  35.6 4.6 %outer.1 = (f32[80,4096]{1,0:T(8,128)S(1)}, bf16[80,1024]{1,0:T(8,128)(2,1)S(1)}) custom-call(f32[80,4096]{1,0:T(8,128)S(1)} %get-tuple-element.44.f_ref, f32[80,4096]{1,0:T(8,128)S(1)} %get-tuple-element.32.t_ref, f32[80,1024]{1,0:T(8,128)S(1)} %get-tuple-element.45.edge_ref, f32[80,4096]{1,0:T(8,128)S(1)} %inner.1.inner_ref, ...), custom_call_target="tpu_custom_call" | custom-call | tf_op jit(solution)/shard_map/outer/pallas_call | solution.py:848
  40.2 1.6 %collective-permute-start.7 = (bf16[80,1024]{1,0:T(8,128)(2,1)S(1)}, bf16[80,1024]{1,0:T(8,128)(2,1)S(1)}, u32[]{:S(2)}, u32[]{:S(2)}) collective-permute-start(bf16[80,1024]{1,0:T(8,128)(2,1)S(1)} %get-tuple-element.56), channel_id=1, source_target_pairs={{0,1},{1,0},{2,3},{3,2},{4,5},{5,4},{6,7},{7,6},{8,9},{9,8},{10,11... | collective-permute-start | bytes 491528 | tf_op jit(solution)/shard_map/ppermute | solution.py:747
  41.7 1.5 %collective-permute-start.8 = (bf16[80,1024]{1,0:T(8,128)(2,1)S(1)}, bf16[80,1024]{1,0:T(8,128)(2,1)S(1)}, u32[]{:S(2)}, u32[]{:S(2)}) collective-permute-start(bf16[80,1024]{1,0:T(8,128)(2,1)S(1)} %get-tuple-element.56), channel_id=1, source_target_pairs={{0,2},{1,3},{2,0},{3,1},{4,6},{5,7},{6,4},{7,5},{8,10},{9,11},{10,... | collective-permute-start | bytes 491528 | tf_op jit(solution)/shard_map/ppermute | solution.py:747
  43.3 0.5 collective-permute-start.9
  43.7 4.2 %sum.1 = (f32[80,2048]{1,0:T(8,128)S(1)}, f32[75,32,128]{2,1,0:T(8,128)}) custom-call(f32[80,4096]{1,0:T(8,128)S(1)} %get-tuple-element.53.tt_ref, s32[2,4096]{1,0:T(2,128)S(1)} %get-tuple-element.40.omap_ref, f32[1,4096]{1,0:T(1,128)S(1)} %get-tuple-element.41.oarea_ref), custom_call_target="tpu_custom_call" | custom-call | tf_op jit(solution)/shard_map/sum/pallas_call | solution.py:859
  48.0 0.0 collective-permute-done.7.rest_0_
  48.0 1.9 %collective-permute-done.8.rest_1_ = bf16[80,1024]{1,0:T(8,128)(2,1)S(1)} collective-permute-done((bf16[80,1024]{1,0:T(8,128)(2,1)S(1)}, bf16[80,1024]{1,0:T(8,128)(2,1)S(1)}, u32[]{:S(2)}, u32[]{:S(2)}) %collective-permute-start.8) | collective-permute-done | bytes 163872 | tf_op jit(solution)/shard_map/ppermute | solution.py:747
  49.9 0.0 collective-permute-done.9.rest_2_
  49.9 5.3 %final.1 = f32[137,64,128]{2,1,0:T(8,128)} custom-call(s32[3,1024]{1,0:T(4,128)S(1)} %get-tuple-element.30.smap_ref, f32[1,1024]{1,0:T(1,128)S(1)} %get-tuple-element.31.sarea_ref, f32[80,2048]{1,0:T(8,128)S(1)} %get-tuple-element.54.sum_ref, bf16[1152,80]{1,0:T(8,128)(2,1)S(1)} %get-tuple-element.37.early1.h_ref, ...), custom_call_target="tpu_custom_call" | custom-call | tf_op jit(solution)/shard_map/final/pallas_call | solution.py:867
Async XLA Ops:
  0.6 16.5 %copy-start = (f32[1,4,137,137]{3,1,2,0:T(4,128)S(1)}, f32[1,4,137,137]{3,1,2,0:T(4,128)}, u32[]{:S(2)}) copy-start(f32[1,4,137,137]{3,1,2,0:T(4,128)} %param.15) | copy-start | bytes 900916
  0.6 16.5 %copy-start.1 = (f32[4,137,128]{2,0,1:T(4,128)S(1)}, f32[4,137,128]{2,0,1:T(4,128)}, u32[]{:S(2)}) copy-start(f32[4,137,128]{2,0,1:T(4,128)} %param.17) | copy-start | bytes 841732
  0.7 16.5 %copy-start.2 = (f32[75,128]{1,0:T(8,128)S(1)}, f32[75,128]{1,0:T(8,128)}, u32[]{:S(2)}) copy-start(f32[75,128]{1,0:T(8,128)} %sm_ref.1) | copy-start | bytes 115204
  8.1 17.4 %collective-permute-start.2 = (bf16[80,1280]{1,0:T(8,128)(2,1)S(1)}, bf16[80,1280]{1,0:T(8,128)(2,1)S(1)}, u32[]{:S(2)}, u32[]{:S(2)}) collective-permute-start(bf16[80,1280]{1,0:T(8,128)(2,1)S(1)} %get-tuple-element.42), channel_id=1, source_target_pairs={{0,1},{1,0},{2,3},{3,2},{4,5},{5,4},{6,7},{7,6},{8,9},{9,8},{10,11... | collective-permute-start | bytes 614408 | tf_op jit(solution)/shard_map/ppermute | solution.py:747
  11.1 14.4 %collective-permute-start.4 = (bf16[80,1280]{1,0:T(8,128)(2,1)S(1)}, bf16[80,1280]{1,0:T(8,128)(2,1)S(1)}, u32[]{:S(2)}, u32[]{:S(2)}) collective-permute-start(bf16[80,1280]{1,0:T(8,128)(2,1)S(1)} %get-tuple-element.43), channel_id=1, source_target_pairs={{0,3},{1,2},{2,1},{3,0},{4,7},{5,6},{6,5},{7,4},{8,11},{9,10},{10,... | collective-permute-start | bytes 614408 | tf_op jit(solution)/shard_map/ppermute | solution.py:747
  12.6 12.9 %collective-permute-start.3 = (bf16[80,1024]{1,0:T(8,128)(2,1)S(1)}, bf16[80,1024]{1,0:T(8,128)(2,1)S(1)}, u32[]{:S(2)}, u32[]{:S(2)}) collective-permute-start(bf16[80,1024]{1,0:T(8,128)(2,1)S(1)} %get-tuple-element.38.packed_ref), channel_id=1, source_target_pairs={{0,2},{1,3},{2,0},{3,1},{4,6},{5,7},{6,4},{7,5},{8,10},{9,11},{10,... | collective-permute-start | bytes 491528 | tf_op jit(solution)/shard_map/ppermute | solution.py:747
  12.7 12.7 %collective-permute-start = (bf16[80,512]{1,0:T(8,128)(2,1)S(1)}, bf16[80,512]{1,0:T(8,128)(2,1)S(1)}, u32[]{:S(2)}, u32[]{:S(2)}) collective-permute-start(bf16[80,512]{1,0:T(8,128)(2,1)S(1)} %get-tuple-element.33), channel_id=1, source_target_pairs={{0,4},{4,0},{8,12},{12,8},{1,5},{5,1},{9,13},{13,9},{2,6},{6,2},{1... | collective-permute-start | bytes 245768 | tf_op jit(solution)/shard_map/ppermute | solution.py:747
  14.7 10.6 %collective-permute-start.1 = (bf16[80,512]{1,0:T(8,128)(2,1)S(1)}, bf16[80,512]{1,0:T(8,128)(2,1)S(1)}, u32[]{:S(2)}, u32[]{:S(2)}) collective-permute-start(bf16[80,512]{1,0:T(8,128)(2,1)S(1)} %get-tuple-element.34), channel_id=1, source_target_pairs={{0,12},{4,8},{8,4},{12,0},{1,13},{5,9},{9,5},{13,1},{2,14},{6,10},... | collective-permute-start | bytes 245768 | tf_op jit(solution)/shard_map/ppermute | solution.py:747
  25.5 4.4 %copy-start.3 = (f32[75]{0:T(128)S(1)}, f32[75]{0:T(128)}, u32[]{:S(2)}) copy-start(f32[75]{0:T(128)} %param.27) | copy-start | bytes 904
  28.3 7.2 %collective-permute-start.5 = (bf16[80,640]{1,0:T(8,128)(2,1)S(1)}, bf16[80,640]{1,0:T(8,128)(2,1)S(1)}, u32[]{:S(2)}, u32[]{:S(2)}) collective-permute-start(bf16[80,640]{1,0:T(8,128)(2,1)S(1)} %get-tuple-element.48), channel_id=1, source_target_pairs={{0,4},{4,0},{8,12},{12,8},{1,5},{5,1},{9,13},{13,9},{2,6},{6,2},{1... | collective-permute-start | bytes 307208 | tf_op jit(solution)/shard_map/ppermute | solution.py:747
  29.0 6.6 %collective-permute-start.6 = (bf16[80,640]{1,0:T(8,128)(2,1)S(1)}, bf16[80,640]{1,0:T(8,128)(2,1)S(1)}, u32[]{:S(2)}, u32[]{:S(2)}) collective-permute-start(bf16[80,640]{1,0:T(8,128)(2,1)S(1)} %get-tuple-element.49), channel_id=1, source_target_pairs={{0,12},{4,8},{8,4},{12,0},{1,13},{5,9},{9,5},{13,1},{2,14},{6,10},... | collective-permute-start | bytes 307208 | tf_op jit(solution)/shard_map/ppermute | solution.py:747
  40.2 7.8 %collective-permute-start.7 = (bf16[80,1024]{1,0:T(8,128)(2,1)S(1)}, bf16[80,1024]{1,0:T(8,128)(2,1)S(1)}, u32[]{:S(2)}, u32[]{:S(2)}) collective-permute-start(bf16[80,1024]{1,0:T(8,128)(2,1)S(1)} %get-tuple-element.56), channel_id=1, source_target_pairs={{0,1},{1,0},{2,3},{3,2},{4,5},{5,4},{6,7},{7,6},{8,9},{9,8},{10,11... | collective-permute-start | bytes 491528 | tf_op jit(solution)/shard_map/ppermute | solution.py:747
  41.7 8.1 %collective-permute-start.8 = (bf16[80,1024]{1,0:T(8,128)(2,1)S(1)}, bf16[80,1024]{1,0:T(8,128)(2,1)S(1)}, u32[]{:S(2)}, u32[]{:S(2)}) collective-permute-start(bf16[80,1024]{1,0:T(8,128)(2,1)S(1)} %get-tuple-element.56), channel_id=1, source_target_pairs={{0,2},{1,3},{2,0},{3,1},{4,6},{5,7},{6,4},{7,5},{8,10},{9,11},{10,... | collective-permute-start | bytes 491528 | tf_op jit(solution)/shard_map/ppermute | solution.py:747
  43.3 6.6 %collective-permute-start.9 = (bf16[80,1024]{1,0:T(8,128)(2,1)S(1)}, bf16[80,1024]{1,0:T(8,128)(2,1)S(1)}, u32[]{:S(2)}, u32[]{:S(2)}) collective-permute-start(bf16[80,1024]{1,0:T(8,128)(2,1)S(1)} %get-tuple-element.56), channel_id=1, source_target_pairs={{0,3},{1,2},{2,1},{3,0},{4,7},{5,6},{6,5},{7,4},{8,11},{9,10},{10,... | collective-permute-start | bytes 491528 | tf_op jit(solution)/shard_map/ppermute | solution.py:747

commit v4 on v3

--- a/solution.py
+++ b/solution.py
@@ -103,13 +103,8 @@
 
 
 def spread(value, low, high, count):
-    vh, vl = split(value)
-    hot = onehot(low, 256)
-    outs = []
-    for term in (vh, vl):
-        parts = [jnp.where(high == h, term.astype(f32), 0.0) for h in range(count)]
-        outs.append(nt(jnp.concatenate(parts, axis=0).astype(bf16), hot))
-    return outs[0] + outs[1]
+    parts = [jnp.where(high == h, value, 0.0) for h in range(count)]
+    return nt(jnp.concatenate(parts, axis=0).astype(bf16), onehot(low, 256))
 
 
 def pick(level_rows, lane_rows, base):
@@ -444,7 +439,7 @@
         new = list(rows)
         for y in range(step + 1, len(rows) - 1 - step):
             here = rows[y]
-            lap = rows[y - 1] + rows[y + 1] + roll(here, 1) + roll(here, -1) - counts(y) * here
+            lap = (rows[y - 1] + rows[y + 1] - counts(y) * here) + (roll(here, 1) + roll(here, -1))
             new[y] = here + wet(y) * (dif * lap + forcing(y))
         rows = new
     return rows
@@ -455,7 +450,7 @@
         new = []
         for j, here in enumerate(now):
             up, down = ends(now, j)
-            lap = up + down + roll(here, 1) + roll(here, -1) - counts[j] * here
+            lap = (roll(here, 1) + roll(here, -1) - counts[j] * here) + (up + down)
             new.append(here + wet[j] * (dif * lap + forcing[j]))
         now = new
     return now
@@ -492,46 +487,42 @@
         ns8[:, j * OX : (j + 1) * OX] = up + down + roll(parts[j], 1) + roll(parts[j], -1)
     fill_diffusivity(d8, dif_ref)
 
-    half = width // 2
-
-    def strip_group(g, carry):
-        lev = pl.ds(pl.multiple_of(g * half, 8), half)
+    lev = slice(0, width)
+
+    def strip_group():
 
         def load(ref, j):
             return ref[lev, j * OX : (j + 1) * OX]
 
-        wet = [tall(ws8, j, half) for j in range(STRIPS)]
+        wet = [tall(ws8, j, width) for j in range(STRIPS)]
         now = substep_strips(
             [load(ts_ref, j) * wet[j] for j in range(STRIPS)],
             [load(fs_ref, j) for j in range(STRIPS)], wet,
-            [tall(ns8, j, half) for j in range(STRIPS)], d8[lev, :], ends,
+            [tall(ns8, j, width) for j in range(STRIPS)], d8[lev, :], ends,
         )
         for j in range(STRIPS):
             strip[lev, j * OX : (j + 1) * OX] = now[j]
-        return carry
-
-    lax.fori_loop(0, 2, strip_group, 0)
-
-    def group(g, carry):
-        lev = pl.ds(pl.multiple_of(g * 8, 8), 8)
+
+    strip_group()
+
+    def main():
         dif = d8[lev, :]
 
         def load(ref, j):
             return ref[lev, j * OX : (j + 1) * OX]
 
         rows = substep_rows(
-            [load(t_ref, y) * tile_row(w8, y) for y in range(OY)], lambda y: load(f_ref, y),
-            lambda y: tile_row(w8, y), lambda y: tile_row(n8, y), dif,
+            [load(t_ref, y) * tall(w8, y, width) for y in range(OY)], lambda y: load(f_ref, y),
+            lambda y: tall(w8, y, width), lambda y: tall(n8, y, width), dif,
         )
         now = [load(strip, j) for j in range(STRIPS)]
         for y in range(4, OY - 4):
             value = merged(now[y % 8], rows[y], lane, y // 8)
             tt_ref[lev, y * OX : (y + 1) * OX] = jnp.where(
-                tile_row(w8, y) > 0.0, value, load(t_ref, y)
+                tall(w8, y, width) > 0.0, value, load(t_ref, y)
             )
-        return carry
-
-    lax.fori_loop(0, width // 8, group, 0)
+
+    main()
 
 
 def slab_kernel(levels, t_ref, even_ref, odd_ref, s, w8, n8):
@@ -607,26 +598,23 @@
     fill_diffusivity(d8, dif_ref)
     tt_ref[:, 4 * OX : 28 * OX] = inner_ref[:, 4 * OX : 28 * OX]
 
-    half = width // 2
-
-    def strip_group(g, carry):
-        lev = pl.ds(pl.multiple_of(g * half, 8), half)
+    lev = slice(0, width)
+
+    def strip_group():
 
         def load(ref, j):
             return ref[lev, j * OX : (j + 1) * OX]
 
         now = substep_strips(
             [load(se, j) for j in range(6)], [load(se, 6 + j) for j in range(6)],
-            [tall(we8, j, half) for j in range(6)], [tall(ne8, j, half) for j in range(6)],
+            [tall(we8, j, width) for j in range(6)], [tall(ne8, j, width) for j in range(6)],
             d8[lev, :], ends,
         )
         se[lev, 0:OX], se[lev, OX : 2 * OX] = now[1], now[4]
-        return carry
-
-    lax.fori_loop(0, 2, strip_group, 0)
-
-    def group(g, carry):
-        lev = pl.ds(pl.multiple_of(g * 16, 16), 16)
+
+    strip_group()
+
+    def main():
         dif = d8[lev, :]
 
         def load(ref, j):
@@ -636,17 +624,16 @@
         for base in (0, 12):
             slabs += substep_rows(
                 [load(s, base + y) for y in range(12)], lambda y: load(fx, base + y),
-                lambda y: tall(w8, base + y, 16), lambda y: tall(n8, base + y, 16), dif,
+                lambda y: tall(w8, base + y, width), lambda y: tall(n8, base + y, width), dif,
             )
         for m in range(4):
             for y, slab, line in ((m, 4 + m, load(se, 0)), (28 + m, 16 + m, load(se, 1))):
                 value = merged(line, slabs[slab], lane, m)
                 tt_ref[lev, y * OX : (y + 1) * OX] = jnp.where(
-                    tall(w8, slab, 16) > 0.0, value, load(t_ref, y)
+                    tall(w8, slab, width) > 0.0, value, load(t_ref, y)
                 )
-        return carry
-
-    lax.fori_loop(0, width // 16, group, 0)
+
+    main()
     source = stacked(tt_ref[...].astype(bf16))
     back_ref[...] = gather(source, cmap_ref[0:1, :], cmap_ref[1:2, :], width).astype(bf16)
 
@@ -664,11 +651,25 @@
         high, low = split(three(nn, inv, three(nt, sw_ref[:, v, :], sm_pad[...])))
         h_ref[v * room : v * room + size, :] = high
         h_ref[(NVAR + v) * room : (NVAR + v) * room + size, :] = low
-        square[v, 0:size, :], square[v, room : room + size, :] = split(three(nn, inv, inv))
-    for v in range(NVAR):
+        if v < NVAR - 1:
+            square[v, 0:size, :], square[v, room : room + size, :] = split(three(nn, inv, inv))
+    for v in range(NVAR - 1):
         for c in range(0, blocks, 2):
             value = wide(square[v], column_block(state_ref, v, c, 2))
             out_ref[v, :, c * 128 : (c + 2) * 128] = value[:size]
+
+
+def late_state_kernel(after, inv_ref, state_ref, out_ref, square):
+    square[...] = jnp.zeros_like(square)
+    blocks = (state_ref.shape[1] - PAD) // NVAR
+    size = inv_ref.shape[0]
+    room = square.shape[0] // 2
+    last = NVAR - 1
+    inv = inv_ref[:, last, :]
+    square[0:size, :], square[room : room + size, :] = split(three(nn, inv, inv))
+    for c in range(0, blocks, 2):
+        value = wide(square[...], column_block(state_ref, last, c, 2))
+        out_ref[:, c * 128 : (c + 2) * 128] = value[:size]
 
 
 def sum_kernel(levels, width, tt_ref, omap_ref, oarea_ref, out_ref, tracer_hbm, rows, sem):
@@ -683,14 +684,18 @@
     for start in range(0, OCELLS, chunk):
         at = slice(start, start + chunk)
         value = tt_ref[:, at] * oarea_ref[:, at]
+        value, rest = (term.astype(f32) for term in split(value))
         part = spread(value, omap_ref[0:1, at], omap_ref[1:2, at], count)
+        part = part + spread(rest, omap_ref[0:1, at], omap_ref[1:2, at], count)
         total = part if total is None else total + part
     for h in range(count):
         out_ref[:, h * 256 : (h + 1) * 256] = total[h * width : (h + 1) * width]
     store.wait()
 
 
-def final_kernel(peers, width, smap_ref, sarea_ref, sum_ref, h_ref, base_ref, *rest):
+def final_kernel(
+    peers, width, smap_ref, sarea_ref, sum_ref, h_ref, base_ref, last_ref, *rest
+):
     got = rest[: peers - 1]
     out_hbm, rows, sums, sems = rest[peers - 1 :]
     columns = sum_ref.shape[1]
@@ -716,7 +721,9 @@
         for c in range(i * share, (i + 1) * share, 256):
             every = wide(h_ref[...], sums[:, c : c + 256])
             for v in range(NVAR):
-                value = base_ref[v, :, c : c + 256] + every[v * room : v * room + size]
+                at = slice(c, c + 256)
+                base = base_ref[v, :, at] if v < NVAR - 1 else last_ref[:, at]
+                value = base + every[v * room : v * room + size]
                 for k in range(2):
                     first = (c // 128 + k) * NVAR + v
                     lines[pl.ds(first, size, stride=stride), :] = value[:, k * 128 : k * 128 + 128]
@@ -810,11 +817,11 @@
 
     base, back_map = pl.pallas_call(
         functools.partial(state_kernel, levels),
-        out_shape=[sds((vars_, size, columns), f32), sds((2 * vars_ * room, width), bf16)],
+        out_shape=[sds((vars_ - 1, size, columns), f32), sds((2 * vars_ * room, width), bf16)],
         in_specs=[vmem] * 4, out_specs=[vmem] * 2,
         scratch_shapes=[
             pltpu.VMEM((width, surface_map.shape[1]), f32),
-            pltpu.VMEM((vars_, 2 * room, size), bf16),
+            pltpu.VMEM((vars_ - 1, 2 * room, size), bf16),
         ],
         compiler_params=params, name="state",
     )(inverse, by_level(surface_weight), surface_map, state)
@@ -864,16 +871,24 @@
         compiler_params=params, name="sum",
     )(t4, omap, oarea)
 
+    last = pl.pallas_call(
+        late_state_kernel,
+        out_shape=sds((size, columns), f32),
+        in_specs=[anywhere] + [vmem] * 2, out_specs=vmem,
+        scratch_shapes=[pltpu.VMEM((2 * room, size), bf16)],
+        compiler_params=params, name="late_state",
+    )(back, inverse, state)
+
     final_state = pl.pallas_call(
         functools.partial(final_kernel, peers, width),
         out_shape=pltpu.HBM((size, blocks * vars_, 128), f32),
-        in_specs=[vmem] * (4 + peers), out_specs=hbm,
+        in_specs=[vmem] * (5 + peers), out_specs=hbm,
         scratch_shapes=[
             pltpu.VMEM((size, blocks * vars_ + PAD, 128), f32), pltpu.VMEM((width, columns), f32),
             pltpu.SemaphoreType.DMA((4,)),
         ],
         compiler_params=params, name="final",
-    )(smap, sarea, sums, back_map, base, *returned)
+    )(smap, sarea, sums, back_map, base, last, *returned)
     final_state = final_state.reshape(size, blocks, vars_, 128).transpose(2, 0, 1, 3)
     final_state = final_state.reshape(vars_, size, columns)
     return (final_state, tracer_out)

time: 55.5 us -> 52.3 us (0.942)
  Pallas kernels: 38.1 us -> 35.3 us
    pallas_call x1, Pallas kernels: 4.59 us -> 3.12 us  [on_device(): pl.pallas_call(functools.partial(outer_kernel, levels, width), out_shape=...]
    pallas_call x1, Pallas kernels: 5.56 us -> 4.16 us  [on_device(): pl.pallas_call(functools.partial(inner_kernel, levels, width), out_shape=...]
    pallas_call x0 -> x1, Pallas kernels: none -> 1.27 us  [on_device(): pl.pallas_call(late_state_kernel, out_shape=sds((size, columns), f32), in...]
    pallas_call x1, Pallas kernels: 5.27 us -> 4.32 us  [on_device(): pl.pallas_call(functools.partial(final_kernel, peers, width), out_shape=p...]
  transfers between devices with their start and end apart: 10 -> 10, of which waited for: 2 -> 1; matrix products, arithmetic and copies ran while one was open for 0% -> 0% of each run, Pallas kernels for 33% -> 34%
where the time goes in v4:
time: 52.3 us; the launch traced here: 52.1 us
  Pallas kernels  35.3 us (67%)
  starting transfers between devices  14.3 us (27%)
  waiting for transfers between devices  1.49 us (3%)
  between operations  1 us (2%)
    ppermute x10, starting transfers between devices, swap(): return lax.ppermute(x, axis, pairs)  14.3 us
    pallas_call x1, Pallas kernels, on_device(): pl.pallas_call(functools.partial(send_kernel, peers, levels, width, borde...  7.45 us
    pallas_call x1, Pallas kernels, on_device(): pl.pallas_call(functools.partial(sum_kernel, levels, width), out_shape=[s...  4.49 us
    pallas_call x1, Pallas kernels, on_device(): pl.pallas_call(functools.partial(state_kernel, levels), out_shape=[sds((v...  4.38 us
    pallas_call x1, Pallas kernels, on_device(): pl.pallas_call(functools.partial(final_kernel, peers, width), out_shape=p...  4.32 us
    pallas_call x1, Pallas kernels, on_device(): pl.pallas_call(functools.partial(inner_kernel, levels, width), out_shape=...  4.16 us
    pallas_call x1, Pallas kernels, on_device(): pl.pallas_call(functools.partial(outer_kernel, levels, width), out_shape=...  3.12 us
    pallas_call x1, Pallas kernels, on_device(): pl.pallas_call(functools.partial(local_kernel, width), out_shape=sds((wid...  3.06 us
  transfers between devices with their start and end apart: 10, of which 1 were waited for; matrix products, arithmetic and copies ran while one was open for 0% of the time, Pallas kernels for 34%

profile of v4, /device:TPU:0, one launch (start us, length us, event | category | flops | bytes accessed | tf_op | source)
XLA Modules:
  0.0 52.1 jit_solution(591382799885600575)
XLA Ops:
  0.6 7.5 %send.1 = (bf16[80,1024]{1,0:T(8,128)(2,1)S(1)}, bf16[80,1280]{1,0:T(8,128)(2,1)S(1)}, bf16[80,1280]{1,0:T(8,128)(2,1)S(1)}, bf16[80,512]{1,0:T(8,128)(2,1)S(1)}...) custom-call(f32[64]{0:T(128)} %refs_0_.1, ...), custom_call_target="tpu_custom_call" | custom-call | tf_op jit(solution)/shard_map/send/pallas_call | solution.py:772
  8.1 0.0 copy-start
  8.1 0.0 copy-start.1
  8.1 0.0 copy-start.2
  8.1 3.0 %collective-permute-start.2 = (bf16[80,1280]{1,0:T(8,128)(2,1)S(1)}, bf16[80,1280]{1,0:T(8,128)(2,1)S(1)}, u32[]{:S(2)}, u32[]{:S(2)}) collective-permute-start(bf16[80,1280]{1,0:T(8,128)(2,1)S(1)} %get-tuple-element.42), channel_id=1, source_target_pairs={{0,1},{1,0},{2,3},{3,2},{4,5},{5,4},{6,7},{7,6},{8,9},{9,8},{10,11... | collective-permute-start | bytes 614408 | tf_op jit(solution)/shard_map/ppermute | solution.py:754
  11.1 1.5 %collective-permute-start.4 = (bf16[80,1280]{1,0:T(8,128)(2,1)S(1)}, bf16[80,1280]{1,0:T(8,128)(2,1)S(1)}, u32[]{:S(2)}, u32[]{:S(2)}) collective-permute-start(bf16[80,1280]{1,0:T(8,128)(2,1)S(1)} %get-tuple-element.43), channel_id=1, source_target_pairs={{0,3},{1,2},{2,1},{3,0},{4,7},{5,6},{6,5},{7,4},{8,11},{9,10},{10,... | collective-permute-start | bytes 614408 | tf_op jit(solution)/shard_map/ppermute | solution.py:754
  12.6 0.1 collective-permute-start.3
  12.7 2.0 %collective-permute-start = (bf16[80,512]{1,0:T(8,128)(2,1)S(1)}, bf16[80,512]{1,0:T(8,128)(2,1)S(1)}, u32[]{:S(2)}, u32[]{:S(2)}) collective-permute-start(bf16[80,512]{1,0:T(8,128)(2,1)S(1)} %get-tuple-element.33), channel_id=1, source_target_pairs={{0,4},{4,0},{8,12},{12,8},{1,5},{5,1},{9,13},{13,9},{2,6},{6,2},{1... | collective-permute-start | bytes 245768 | tf_op jit(solution)/shard_map/ppermute | solution.py:754
  14.7 2.5 %collective-permute-start.1 = (bf16[80,512]{1,0:T(8,128)(2,1)S(1)}, bf16[80,512]{1,0:T(8,128)(2,1)S(1)}, u32[]{:S(2)}, u32[]{:S(2)}) collective-permute-start(bf16[80,512]{1,0:T(8,128)(2,1)S(1)} %get-tuple-element.34), channel_id=1, source_target_pairs={{0,12},{4,8},{8,4},{12,0},{1,13},{5,9},{9,5},{13,1},{2,14},{6,10},... | collective-permute-start | bytes 245768 | tf_op jit(solution)/shard_map/ppermute | solution.py:754
  17.2 3.1 %local.1.local_ref = f32[80,4096]{1,0:T(8,128)S(1)} custom-call(bf16[2,80,2048]{2,1,0:T(8,128)(2,1)S(1)} %get-tuple-element.39.forcing_ref, s32[2,4096]{1,0:T(2,128)S(1)} %get-tuple-element.40.omap_ref, f32[1,4096]{1,0:T(1,128)S(1)} %get-tuple-element.41.oarea_ref), custom_call_target="tpu_custom_call" | custom-call | tf_op jit(solution)/shard_map/local/pallas_call | solution.py:805
  20.3 0.0 copy-done
  20.3 0.0 copy-done.1
  20.3 0.0 copy-done.2
  20.3 4.4 %state.1 = (f32[3,137,2048]{2,1,0:T(8,128)S(1)}, bf16[1152,80]{1,0:T(8,128)(2,1)S(1)}) custom-call(f32[137,4,137]{2,1,0:T(4,128)S(1)} %bitcast.21, f32[137,4,128]{2,1,0:T(4,128)S(1)} %bitcast.23, f32[75,128]{1,0:T(8,128)S(1)} %copy-done.2, f32[137,72,128]{2,1,0:T(8,128)S(1)} %get-tuple-element.36.state_ref), custom_call_target="tpu_custom_call" | custom-call | tf_op jit(solution)/shard_map/state/pallas_call | solution.py:818
  24.7 0.0 collective-permute-done.even_ref
  24.7 0.0 collective-permute-done.1.odd_ref
  24.7 0.1 slab.1
  24.8 0.0 collective-permute-done.3.rest_1_
  24.8 0.0 collective-permute-done.2.rest_0_
  24.8 0.0 collective-permute-done.4.rest_2_
  24.9 0.0 copy-start.3
  24.9 2.9 %receive.1 = (f32[80,4096]{1,0:T(8,128)S(1)}, f32[80,1024]{1,0:T(8,128)S(1)}, f32[80,1024]{1,0:T(8,128)S(1)}, s32[2,1024]{1,0:T(2,128)S(1)}, bf16[80,640]{1,0:T(...) custom-call(f32[8,3072]{1,0:T(8,128)S(1)} %get-tuple-element.35.early0.n8, ...), custom_call_target="tpu_custom_call" | custom-call | tf_op jit(solution)/shard_map/receive/pallas_call | solution.py:830
  27.8 0.7 %collective-permute-start.5 = (bf16[80,640]{1,0:T(8,128)(2,1)S(1)}, bf16[80,640]{1,0:T(8,128)(2,1)S(1)}, u32[]{:S(2)}, u32[]{:S(2)}) collective-permute-start(bf16[80,640]{1,0:T(8,128)(2,1)S(1)} %get-tuple-element.48), channel_id=1, source_target_pairs={{0,4},{4,0},{8,12},{12,8},{1,5},{5,1},{9,13},{13,9},{2,6},{6,2},{1... | collective-permute-start | bytes 307208 | tf_op jit(solution)/shard_map/ppermute | solution.py:754
  28.6 0.9 %collective-permute-start.6 = (bf16[80,640]{1,0:T(8,128)(2,1)S(1)}, bf16[80,640]{1,0:T(8,128)(2,1)S(1)}, u32[]{:S(2)}, u32[]{:S(2)}) collective-permute-start(bf16[80,640]{1,0:T(8,128)(2,1)S(1)} %get-tuple-element.49), channel_id=1, source_target_pairs={{0,12},{4,8},{8,4},{12,0},{1,13},{5,9},{9,5},{13,1},{2,14},{6,10},... | collective-permute-start | bytes 307208 | tf_op jit(solution)/shard_map/ppermute | solution.py:754
  29.5 0.0 copy-done.3
  29.5 4.2 %inner.1.inner_ref = f32[80,4096]{1,0:T(8,128)S(1)} custom-call(f32[80,4096]{1,0:T(8,128)S(1)} %get-tuple-element.44.f_ref, f32[80,1024]{1,0:T(8,128)S(1)} %get-tuple-element.46.fs_ref, f32[80,4096]{1,0:T(8,128)S(1)} %get-tuple-element.32.t_ref, f32[80,1024]{1,0:T(8,128)S(1)} %get-tuple-element.47.ts_ref, f32[1,75]{1,0:T(1,128)S(1)} %bitcast.24), custom_call_target="tpu_custom_call" | custom-call | tf_op jit(solution)/shard_map/inner/pallas_call | solution.py:845
  33.6 0.0 collective-permute-done.5.even_ref
  33.7 1.5 %collective-permute-done.6.odd_ref = bf16[80,640]{1,0:T(8,128)(2,1)S(1)} collective-permute-done((bf16[80,640]{1,0:T(8,128)(2,1)S(1)}, bf16[80,640]{1,0:T(8,128)(2,1)S(1)}, u32[]{:S(2)}, u32[]{:S(2)}) %collective-permute-start.6) | collective-permute-done | bytes 102432 | tf_op jit(solution)/shard_map/ppermute | solution.py:754
  35.1 3.1 %outer.1 = (f32[80,4096]{1,0:T(8,128)S(1)}, bf16[80,1024]{1,0:T(8,128)(2,1)S(1)}) custom-call(f32[80,4096]{1,0:T(8,128)S(1)} %get-tuple-element.44.f_ref, f32[80,4096]{1,0:T(8,128)S(1)} %get-tuple-element.32.t_ref, f32[80,1024]{1,0:T(8,128)S(1)} %get-tuple-element.45.edge_ref, f32[80,4096]{1,0:T(8,128)S(1)} %inner.1.inner_ref, ...), custom_call_target="tpu_custom_call" | custom-call | tf_op jit(solution)/shard_map/outer/pallas_call | solution.py:855
  38.3 2.5 %collective-permute-start.9 = (bf16[80,1024]{1,0:T(8,128)(2,1)S(1)}, bf16[80,1024]{1,0:T(8,128)(2,1)S(1)}, u32[]{:S(2)}, u32[]{:S(2)}) collective-permute-start(bf16[80,1024]{1,0:T(8,128)(2,1)S(1)} %get-tuple-element.56.after), channel_id=1, source_target_pairs={{0,3},{1,2},{2,1},{3,0},{4,7},{5,6},{6,5},{7,4},{8,11},{9,10},{10,... | collective-permute-start | bytes 491528 | tf_op jit(solution)/shard_map/ppermute | solution.py:754
  40.8 0.5 collective-permute-start.8
  41.3 0.5 %collective-permute-start.7 = (bf16[80,1024]{1,0:T(8,128)(2,1)S(1)}, bf16[80,1024]{1,0:T(8,128)(2,1)S(1)}, u32[]{:S(2)}, u32[]{:S(2)}) collective-permute-start(bf16[80,1024]{1,0:T(8,128)(2,1)S(1)} %get-tuple-element.56.after), channel_id=1, source_target_pairs={{0,1},{1,0},{2,3},{3,2},{4,5},{5,4},{6,7},{7,6},{8,9},{9,8},{10,11... | collective-permute-start | bytes 491528 | tf_op jit(solution)/shard_map/ppermute | solution.py:754
  41.8 1.3 %late_state.1.last_ref = f32[137,2048]{1,0:T(8,128)S(1)} custom-call(bf16[80,1024]{1,0:T(8,128)(2,1)S(1)} %get-tuple-element.56.after, f32[137,4,137]{2,1,0:T(4,128)S(1)} %bitcast.22, f32[137,72,128]{2,1,0:T(8,128)S(1)} %get-tuple-element.36.state_ref), custom_call_target="tpu_custom_call" | custom-call | tf_op jit(solution)/shard_map/late_state/pallas_call | solution.py:874
  43.1 4.5 %sum.1 = (f32[80,2048]{1,0:T(8,128)S(1)}, f32[75,32,128]{2,1,0:T(8,128)}) custom-call(f32[80,4096]{1,0:T(8,128)S(1)} %get-tuple-element.53.tt_ref, s32[2,4096]{1,0:T(2,128)S(1)} %get-tuple-element.40.omap_ref, f32[1,4096]{1,0:T(1,128)S(1)} %get-tuple-element.41.oarea_ref), custom_call_target="tpu_custom_call" | custom-call | tf_op jit(solution)/shard_map/sum/pallas_call | solution.py:866
  47.6 0.0 collective-permute-done.9.rest_2_
  47.6 0.0 collective-permute-done.8.rest_1_
  47.6 0.0 collective-permute-done.7.rest_0_
  47.6 4.3 %final.1 = f32[137,64,128]{2,1,0:T(8,128)} custom-call(s32[3,1024]{1,0:T(4,128)S(1)} %get-tuple-element.30.smap_ref, f32[1,1024]{1,0:T(1,128)S(1)} %get-tuple-element.31.sarea_ref, f32[80,2048]{1,0:T(8,128)S(1)} %get-tuple-element.54.sum_ref, bf16[1152,80]{1,0:T(8,128)(2,1)S(1)} %get-tuple-element.37.early1.h_ref, ...), custom_call_target="tpu_custom_call" | custom-call | tf_op jit(solution)/shard_map/final/pallas_call | solution.py:882
Async XLA Ops:
  8.1 12.2 %copy-start = (f32[1,4,137,137]{3,1,2,0:T(4,128)S(1)}, f32[1,4,137,137]{3,1,2,0:T(4,128)}, u32[]{:S(2)}) copy-start(f32[1,4,137,137]{3,1,2,0:T(4,128)} %param.15) | copy-start | bytes 900916
  8.1 12.2 %copy-start.1 = (f32[4,137,128]{2,0,1:T(4,128)S(1)}, f32[4,137,128]{2,0,1:T(4,128)}, u32[]{:S(2)}) copy-start(f32[4,137,128]{2,0,1:T(4,128)} %param.17) | copy-start | bytes 841732
  8.1 12.2 %copy-start.2 = (f32[75,128]{1,0:T(8,128)S(1)}, f32[75,128]{1,0:T(8,128)}, u32[]{:S(2)}) copy-start(f32[75,128]{1,0:T(8,128)} %sm_ref.1) | copy-start | bytes 115204
  8.1 16.7 %collective-permute-start.2 = (bf16[80,1280]{1,0:T(8,128)(2,1)S(1)}, bf16[80,1280]{1,0:T(8,128)(2,1)S(1)}, u32[]{:S(2)}, u32[]{:S(2)}) collective-permute-start(bf16[80,1280]{1,0:T(8,128)(2,1)S(1)} %get-tuple-element.42), channel_id=1, source_target_pairs={{0,1},{1,0},{2,3},{3,2},{4,5},{5,4},{6,7},{7,6},{8,9},{9,8},{10,11... | collective-permute-start | bytes 614408 | tf_op jit(solution)/shard_map/ppermute | solution.py:754
  11.1 13.7 %collective-permute-start.4 = (bf16[80,1280]{1,0:T(8,128)(2,1)S(1)}, bf16[80,1280]{1,0:T(8,128)(2,1)S(1)}, u32[]{:S(2)}, u32[]{:S(2)}) collective-permute-start(bf16[80,1280]{1,0:T(8,128)(2,1)S(1)} %get-tuple-element.43), channel_id=1, source_target_pairs={{0,3},{1,2},{2,1},{3,0},{4,7},{5,6},{6,5},{7,4},{8,11},{9,10},{10,... | collective-permute-start | bytes 614408 | tf_op jit(solution)/shard_map/ppermute | solution.py:754
  12.6 12.2 %collective-permute-start.3 = (bf16[80,1024]{1,0:T(8,128)(2,1)S(1)}, bf16[80,1024]{1,0:T(8,128)(2,1)S(1)}, u32[]{:S(2)}, u32[]{:S(2)}) collective-permute-start(bf16[80,1024]{1,0:T(8,128)(2,1)S(1)} %get-tuple-element.38.packed_ref), channel_id=1, source_target_pairs={{0,2},{1,3},{2,0},{3,1},{4,6},{5,7},{6,4},{7,5},{8,10},{9,11},{10,... | collective-permute-start | bytes 491528 | tf_op jit(solution)/shard_map/ppermute | solution.py:754
  12.7 12.0 %collective-permute-start = (bf16[80,512]{1,0:T(8,128)(2,1)S(1)}, bf16[80,512]{1,0:T(8,128)(2,1)S(1)}, u32[]{:S(2)}, u32[]{:S(2)}) collective-permute-start(bf16[80,512]{1,0:T(8,128)(2,1)S(1)} %get-tuple-element.33), channel_id=1, source_target_pairs={{0,4},{4,0},{8,12},{12,8},{1,5},{5,1},{9,13},{13,9},{2,6},{6,2},{1... | collective-permute-start | bytes 245768 | tf_op jit(solution)/shard_map/ppermute | solution.py:754
  14.7 10.0 %collective-permute-start.1 = (bf16[80,512]{1,0:T(8,128)(2,1)S(1)}, bf16[80,512]{1,0:T(8,128)(2,1)S(1)}, u32[]{:S(2)}, u32[]{:S(2)}) collective-permute-start(bf16[80,512]{1,0:T(8,128)(2,1)S(1)} %get-tuple-element.34), channel_id=1, source_target_pairs={{0,12},{4,8},{8,4},{12,0},{1,13},{5,9},{9,5},{13,1},{2,14},{6,10},... | collective-permute-start | bytes 245768 | tf_op jit(solution)/shard_map/ppermute | solution.py:754
  24.9 4.6 %copy-start.3 = (f32[75]{0:T(128)S(1)}, f32[75]{0:T(128)}, u32[]{:S(2)}) copy-start(f32[75]{0:T(128)} %param.27) | copy-start | bytes 904
  27.8 5.8 %collective-permute-start.5 = (bf16[80,640]{1,0:T(8,128)(2,1)S(1)}, bf16[80,640]{1,0:T(8,128)(2,1)S(1)}, u32[]{:S(2)}, u32[]{:S(2)}) collective-permute-start(bf16[80,640]{1,0:T(8,128)(2,1)S(1)} %get-tuple-element.48), channel_id=1, source_target_pairs={{0,4},{4,0},{8,12},{12,8},{1,5},{5,1},{9,13},{13,9},{2,6},{6,2},{1... | collective-permute-start | bytes 307208 | tf_op jit(solution)/shard_map/ppermute | solution.py:754
  28.6 6.6 %collective-permute-start.6 = (bf16[80,640]{1,0:T(8,128)(2,1)S(1)}, bf16[80,640]{1,0:T(8,128)(2,1)S(1)}, u32[]{:S(2)}, u32[]{:S(2)}) collective-permute-start(bf16[80,640]{1,0:T(8,128)(2,1)S(1)} %get-tuple-element.49), channel_id=1, source_target_pairs={{0,12},{4,8},{8,4},{12,0},{1,13},{5,9},{9,5},{13,1},{2,14},{6,10},... | collective-permute-start | bytes 307208 | tf_op jit(solution)/shard_map/ppermute | solution.py:754
  38.3 9.3 %collective-permute-start.9 = (bf16[80,1024]{1,0:T(8,128)(2,1)S(1)}, bf16[80,1024]{1,0:T(8,128)(2,1)S(1)}, u32[]{:S(2)}, u32[]{:S(2)}) collective-permute-start(bf16[80,1024]{1,0:T(8,128)(2,1)S(1)} %get-tuple-element.56.after), channel_id=1, source_target_pairs={{0,3},{1,2},{2,1},{3,0},{4,7},{5,6},{6,5},{7,4},{8,11},{9,10},{10,... | collective-permute-start | bytes 491528 | tf_op jit(solution)/shard_map/ppermute | solution.py:754
  40.8 6.8 %collective-permute-start.8 = (bf16[80,1024]{1,0:T(8,128)(2,1)S(1)}, bf16[80,1024]{1,0:T(8,128)(2,1)S(1)}, u32[]{:S(2)}, u32[]{:S(2)}) collective-permute-start(bf16[80,1024]{1,0:T(8,128)(2,1)S(1)} %get-tuple-element.56.after), channel_id=1, source_target_pairs={{0,2},{1,3},{2,0},{3,1},{4,6},{5,7},{6,4},{7,5},{8,10},{9,11},{10,... | collective-permute-start | bytes 491528 | tf_op jit(solution)/shard_map/ppermute | solution.py:754
  41.3 6.3 %collective-permute-start.7 = (bf16[80,1024]{1,0:T(8,128)(2,1)S(1)}, bf16[80,1024]{1,0:T(8,128)(2,1)S(1)}, u32[]{:S(2)}, u32[]{:S(2)}) collective-permute-start(bf16[80,1024]{1,0:T(8,128)(2,1)S(1)} %get-tuple-element.56.after), channel_id=1, source_target_pairs={{0,1},{1,0},{2,3},{3,2},{4,5},{5,4},{6,7},{7,6},{8,9},{9,8},{10,11... | collective-permute-start | bytes 491528 | tf_op jit(solution)/shard_map/ppermute | solution.py:754

commit v5 on v4

--- a/solution.py
+++ b/solution.py
@@ -885,7 +885,7 @@
         in_specs=[vmem] * (5 + peers), out_specs=hbm,
         scratch_shapes=[
             pltpu.VMEM((size, blocks * vars_ + PAD, 128), f32), pltpu.VMEM((width, columns), f32),
-            pltpu.SemaphoreType.DMA((4,)),
+            pltpu.SemaphoreType.DMA((8,)),
         ],
         compiler_params=params, name="final",
     )(smap, sarea, sums, back_map, base, last, *returned)

time: 52.3 us -> 52.1 us (level)
  no operation moved by 1% of the time
where the time goes in v5:
time: 52.1 us; the launch traced here: 52 us
  Pallas kernels  35.2 us (68%)
  starting transfers between devices  14.3 us (27%)
  waiting for transfers between devices  1.49 us (3%)
  between operations  1 us (2%)
    ppermute x10, starting transfers between devices, swap(): return lax.ppermute(x, axis, pairs)  14.3 us
    pallas_call x1, Pallas kernels, on_device(): pl.pallas_call(functools.partial(send_kernel, peers, levels, width, borde...  7.45 us
    pallas_call x1, Pallas kernels, on_device(): pl.pallas_call(functools.partial(sum_kernel, levels, width), out_shape=[s...  4.49 us
    pallas_call x1, Pallas kernels, on_device(): pl.pallas_call(functools.partial(state_kernel, levels), out_shape=[sds((v...  4.38 us
    pallas_call x1, Pallas kernels, on_device(): pl.pallas_call(functools.partial(final_kernel, peers, width), out_shape=p...  4.17 us
    pallas_call x1, Pallas kernels, on_device(): pl.pallas_call(functools.partial(inner_kernel, levels, width), out_shape=...  4.16 us
    pallas_call x1, Pallas kernels, on_device(): pl.pallas_call(functools.partial(outer_kernel, levels, width), out_shape=...  3.12 us
    pallas_call x1, Pallas kernels, on_device(): pl.pallas_call(functools.partial(local_kernel, width), out_shape=sds((wid...  3.06 us
  transfers between devices with their start and end apart: 10, of which 1 were waited for; matrix products, arithmetic and copies ran while one was open for 0% of the time, Pallas kernels for 34%

profile of v5, /device:TPU:0, one launch (start us, length us, event | category | flops | bytes accessed | tf_op | source)
XLA Modules:
  0.0 52.0 jit_solution(1943704236991325817)
XLA Ops:
  0.6 7.5 %send.1 = (bf16[80,1024]{1,0:T(8,128)(2,1)S(1)}, bf16[80,1280]{1,0:T(8,128)(2,1)S(1)}, bf16[80,1280]{1,0:T(8,128)(2,1)S(1)}, bf16[80,512]{1,0:T(8,128)(2,1)S(1)}...) custom-call(f32[64]{0:T(128)} %refs_0_.1, ...), custom_call_target="tpu_custom_call" | custom-call | tf_op jit(solution)/shard_map/send/pallas_call | solution.py:772
  8.1 0.0 copy-start
  8.1 0.0 copy-start.1
  8.1 0.0 copy-start.2
  8.1 3.0 %collective-permute-start.2 = (bf16[80,1280]{1,0:T(8,128)(2,1)S(1)}, bf16[80,1280]{1,0:T(8,128)(2,1)S(1)}, u32[]{:S(2)}, u32[]{:S(2)}) collective-permute-start(bf16[80,1280]{1,0:T(8,128)(2,1)S(1)} %get-tuple-element.42), channel_id=1, source_target_pairs={{0,1},{1,0},{2,3},{3,2},{4,5},{5,4},{6,7},{7,6},{8,9},{9,8},{10,11... | collective-permute-start | bytes 614408 | tf_op jit(solution)/shard_map/ppermute | solution.py:754
  11.1 1.5 %collective-permute-start.4 = (bf16[80,1280]{1,0:T(8,128)(2,1)S(1)}, bf16[80,1280]{1,0:T(8,128)(2,1)S(1)}, u32[]{:S(2)}, u32[]{:S(2)}) collective-permute-start(bf16[80,1280]{1,0:T(8,128)(2,1)S(1)} %get-tuple-element.43), channel_id=1, source_target_pairs={{0,3},{1,2},{2,1},{3,0},{4,7},{5,6},{6,5},{7,4},{8,11},{9,10},{10,... | collective-permute-start | bytes 614408 | tf_op jit(solution)/shard_map/ppermute | solution.py:754
  12.6 0.1 collective-permute-start.3
  12.7 2.0 %collective-permute-start = (bf16[80,512]{1,0:T(8,128)(2,1)S(1)}, bf16[80,512]{1,0:T(8,128)(2,1)S(1)}, u32[]{:S(2)}, u32[]{:S(2)}) collective-permute-start(bf16[80,512]{1,0:T(8,128)(2,1)S(1)} %get-tuple-element.33), channel_id=1, source_target_pairs={{0,4},{4,0},{8,12},{12,8},{1,5},{5,1},{9,13},{13,9},{2,6},{6,2},{1... | collective-permute-start | bytes 245768 | tf_op jit(solution)/shard_map/ppermute | solution.py:754
  14.7 2.5 %collective-permute-start.1 = (bf16[80,512]{1,0:T(8,128)(2,1)S(1)}, bf16[80,512]{1,0:T(8,128)(2,1)S(1)}, u32[]{:S(2)}, u32[]{:S(2)}) collective-permute-start(bf16[80,512]{1,0:T(8,128)(2,1)S(1)} %get-tuple-element.34), channel_id=1, source_target_pairs={{0,12},{4,8},{8,4},{12,0},{1,13},{5,9},{9,5},{13,1},{2,14},{6,10},... | collective-permute-start | bytes 245768 | tf_op jit(solution)/shard_map/ppermute | solution.py:754
  17.2 3.1 %local.1.local_ref = f32[80,4096]{1,0:T(8,128)S(1)} custom-call(bf16[2,80,2048]{2,1,0:T(8,128)(2,1)S(1)} %get-tuple-element.39.forcing_ref, s32[2,4096]{1,0:T(2,128)S(1)} %get-tuple-element.40.omap_ref, f32[1,4096]{1,0:T(1,128)S(1)} %get-tuple-element.41.oarea_ref), custom_call_target="tpu_custom_call" | custom-call | tf_op jit(solution)/shard_map/local/pallas_call | solution.py:805
  20.3 0.0 copy-done
  20.3 0.0 copy-done.1
  20.3 0.0 copy-done.2
  20.3 4.4 %state.1 = (f32[3,137,2048]{2,1,0:T(8,128)S(1)}, bf16[1152,80]{1,0:T(8,128)(2,1)S(1)}) custom-call(f32[137,4,137]{2,1,0:T(4,128)S(1)} %bitcast.21, f32[137,4,128]{2,1,0:T(4,128)S(1)} %bitcast.23, f32[75,128]{1,0:T(8,128)S(1)} %copy-done.2, f32[137,72,128]{2,1,0:T(8,128)S(1)} %get-tuple-element.36.state_ref), custom_call_target="tpu_custom_call" | custom-call | tf_op jit(solution)/shard_map/state/pallas_call | solution.py:818
  24.7 0.0 collective-permute-done.even_ref
  24.7 0.0 collective-permute-done.1.odd_ref
  24.7 0.1 slab.1
  24.8 0.0 collective-permute-done.3.rest_1_
  24.8 0.0 collective-permute-done.2.rest_0_
  24.8 0.0 collective-permute-done.4.rest_2_
  24.9 0.0 copy-start.3
  24.9 2.9 %receive.1 = (f32[80,4096]{1,0:T(8,128)S(1)}, f32[80,1024]{1,0:T(8,128)S(1)}, f32[80,1024]{1,0:T(8,128)S(1)}, s32[2,1024]{1,0:T(2,128)S(1)}, bf16[80,640]{1,0:T(...) custom-call(f32[8,3072]{1,0:T(8,128)S(1)} %get-tuple-element.35.early0.n8, ...), custom_call_target="tpu_custom_call" | custom-call | tf_op jit(solution)/shard_map/receive/pallas_call | solution.py:830
  27.8 0.7 %collective-permute-start.5 = (bf16[80,640]{1,0:T(8,128)(2,1)S(1)}, bf16[80,640]{1,0:T(8,128)(2,1)S(1)}, u32[]{:S(2)}, u32[]{:S(2)}) collective-permute-start(bf16[80,640]{1,0:T(8,128)(2,1)S(1)} %get-tuple-element.48), channel_id=1, source_target_pairs={{0,4},{4,0},{8,12},{12,8},{1,5},{5,1},{9,13},{13,9},{2,6},{6,2},{1... | collective-permute-start | bytes 307208 | tf_op jit(solution)/shard_map/ppermute | solution.py:754
  28.6 0.9 %collective-permute-start.6 = (bf16[80,640]{1,0:T(8,128)(2,1)S(1)}, bf16[80,640]{1,0:T(8,128)(2,1)S(1)}, u32[]{:S(2)}, u32[]{:S(2)}) collective-permute-start(bf16[80,640]{1,0:T(8,128)(2,1)S(1)} %get-tuple-element.49), channel_id=1, source_target_pairs={{0,12},{4,8},{8,4},{12,0},{1,13},{5,9},{9,5},{13,1},{2,14},{6,10},... | collective-permute-start | bytes 307208 | tf_op jit(solution)/shard_map/ppermute | solution.py:754
  29.5 0.0 copy-done.3
  29.5 4.2 %inner.1.inner_ref = f32[80,4096]{1,0:T(8,128)S(1)} custom-call(f32[80,4096]{1,0:T(8,128)S(1)} %get-tuple-element.44.f_ref, f32[80,1024]{1,0:T(8,128)S(1)} %get-tuple-element.46.fs_ref, f32[80,4096]{1,0:T(8,128)S(1)} %get-tuple-element.32.t_ref, f32[80,1024]{1,0:T(8,128)S(1)} %get-tuple-element.47.ts_ref, f32[1,75]{1,0:T(1,128)S(1)} %bitcast.24), custom_call_target="tpu_custom_call" | custom-call | tf_op jit(solution)/shard_map/inner/pallas_call | solution.py:845
  33.6 0.0 collective-permute-done.5.even_ref
  33.7 1.5 %collective-permute-done.6.odd_ref = bf16[80,640]{1,0:T(8,128)(2,1)S(1)} collective-permute-done((bf16[80,640]{1,0:T(8,128)(2,1)S(1)}, bf16[80,640]{1,0:T(8,128)(2,1)S(1)}, u32[]{:S(2)}, u32[]{:S(2)}) %collective-permute-start.6) | collective-permute-done | bytes 102432 | tf_op jit(solution)/shard_map/ppermute | solution.py:754
  35.1 3.1 %outer.1 = (f32[80,4096]{1,0:T(8,128)S(1)}, bf16[80,1024]{1,0:T(8,128)(2,1)S(1)}) custom-call(f32[80,4096]{1,0:T(8,128)S(1)} %get-tuple-element.44.f_ref, f32[80,4096]{1,0:T(8,128)S(1)} %get-tuple-element.32.t_ref, f32[80,1024]{1,0:T(8,128)S(1)} %get-tuple-element.45.edge_ref, f32[80,4096]{1,0:T(8,128)S(1)} %inner.1.inner_ref, ...), custom_call_target="tpu_custom_call" | custom-call | tf_op jit(solution)/shard_map/outer/pallas_call | solution.py:855
  38.3 2.5 %collective-permute-start.9 = (bf16[80,1024]{1,0:T(8,128)(2,1)S(1)}, bf16[80,1024]{1,0:T(8,128)(2,1)S(1)}, u32[]{:S(2)}, u32[]{:S(2)}) collective-permute-start(bf16[80,1024]{1,0:T(8,128)(2,1)S(1)} %get-tuple-element.56.after), channel_id=1, source_target_pairs={{0,3},{1,2},{2,1},{3,0},{4,7},{5,6},{6,5},{7,4},{8,11},{9,10},{10,... | collective-permute-start | bytes 491528 | tf_op jit(solution)/shard_map/ppermute | solution.py:754
  40.8 0.5 collective-permute-start.8
  41.3 0.5 %collective-permute-start.7 = (bf16[80,1024]{1,0:T(8,128)(2,1)S(1)}, bf16[80,1024]{1,0:T(8,128)(2,1)S(1)}, u32[]{:S(2)}, u32[]{:S(2)}) collective-permute-start(bf16[80,1024]{1,0:T(8,128)(2,1)S(1)} %get-tuple-element.56.after), channel_id=1, source_target_pairs={{0,1},{1,0},{2,3},{3,2},{4,5},{5,4},{6,7},{7,6},{8,9},{9,8},{10,11... | collective-permute-start | bytes 491528 | tf_op jit(solution)/shard_map/ppermute | solution.py:754
  41.8 1.3 %late_state.1.last_ref = f32[137,2048]{1,0:T(8,128)S(1)} custom-call(bf16[80,1024]{1,0:T(8,128)(2,1)S(1)} %get-tuple-element.56.after, f32[137,4,137]{2,1,0:T(4,128)S(1)} %bitcast.22, f32[137,72,128]{2,1,0:T(8,128)S(1)} %get-tuple-element.36.state_ref), custom_call_target="tpu_custom_call" | custom-call | tf_op jit(solution)/shard_map/late_state/pallas_call | solution.py:874
  43.1 4.5 %sum.1 = (f32[80,2048]{1,0:T(8,128)S(1)}, f32[75,32,128]{2,1,0:T(8,128)}) custom-call(f32[80,4096]{1,0:T(8,128)S(1)} %get-tuple-element.53.tt_ref, s32[2,4096]{1,0:T(2,128)S(1)} %get-tuple-element.40.omap_ref, f32[1,4096]{1,0:T(1,128)S(1)} %get-tuple-element.41.oarea_ref), custom_call_target="tpu_custom_call" | custom-call | tf_op jit(solution)/shard_map/sum/pallas_call | solution.py:866
  47.6 0.0 collective-permute-done.9.rest_2_
  47.6 0.0 collective-permute-done.8.rest_1_
  47.6 0.0 collective-permute-done.7.rest_0_
  47.6 4.2 %final.1 = f32[137,64,128]{2,1,0:T(8,128)} custom-call(s32[3,1024]{1,0:T(4,128)S(1)} %get-tuple-element.30.smap_ref, f32[1,1024]{1,0:T(1,128)S(1)} %get-tuple-element.31.sarea_ref, f32[80,2048]{1,0:T(8,128)S(1)} %get-tuple-element.54.sum_ref, bf16[1152,80]{1,0:T(8,128)(2,1)S(1)} %get-tuple-element.37.early1.h_ref, ...), custom_call_target="tpu_custom_call" | custom-call | tf_op jit(solution)/shard_map/final/pallas_call | solution.py:882
Async XLA Ops:
  8.1 12.2 %copy-start = (f32[1,4,137,137]{3,1,2,0:T(4,128)S(1)}, f32[1,4,137,137]{3,1,2,0:T(4,128)}, u32[]{:S(2)}) copy-start(f32[1,4,137,137]{3,1,2,0:T(4,128)} %param.15) | copy-start | bytes 900916
  8.1 12.2 %copy-start.1 = (f32[4,137,128]{2,0,1:T(4,128)S(1)}, f32[4,137,128]{2,0,1:T(4,128)}, u32[]{:S(2)}) copy-start(f32[4,137,128]{2,0,1:T(4,128)} %param.17) | copy-start | bytes 841732
  8.1 12.2 %copy-start.2 = (f32[75,128]{1,0:T(8,128)S(1)}, f32[75,128]{1,0:T(8,128)}, u32[]{:S(2)}) copy-start(f32[75,128]{1,0:T(8,128)} %sm_ref.1) | copy-start | bytes 115204
  8.1 16.7 %collective-permute-start.2 = (bf16[80,1280]{1,0:T(8,128)(2,1)S(1)}, bf16[80,1280]{1,0:T(8,128)(2,1)S(1)}, u32[]{:S(2)}, u32[]{:S(2)}) collective-permute-start(bf16[80,1280]{1,0:T(8,128)(2,1)S(1)} %get-tuple-element.42), channel_id=1, source_target_pairs={{0,1},{1,0},{2,3},{3,2},{4,5},{5,4},{6,7},{7,6},{8,9},{9,8},{10,11... | collective-permute-start | bytes 614408 | tf_op jit(solution)/shard_map/ppermute | solution.py:754
  11.1 13.7 %collective-permute-start.4 = (bf16[80,1280]{1,0:T(8,128)(2,1)S(1)}, bf16[80,1280]{1,0:T(8,128)(2,1)S(1)}, u32[]{:S(2)}, u32[]{:S(2)}) collective-permute-start(bf16[80,1280]{1,0:T(8,128)(2,1)S(1)} %get-tuple-element.43), channel_id=1, source_target_pairs={{0,3},{1,2},{2,1},{3,0},{4,7},{5,6},{6,5},{7,4},{8,11},{9,10},{10,... | collective-permute-start | bytes 614408 | tf_op jit(solution)/shard_map/ppermute | solution.py:754
  12.6 12.2 %collective-permute-start.3 = (bf16[80,1024]{1,0:T(8,128)(2,1)S(1)}, bf16[80,1024]{1,0:T(8,128)(2,1)S(1)}, u32[]{:S(2)}, u32[]{:S(2)}) collective-permute-start(bf16[80,1024]{1,0:T(8,128)(2,1)S(1)} %get-tuple-element.38.packed_ref), channel_id=1, source_target_pairs={{0,2},{1,3},{2,0},{3,1},{4,6},{5,7},{6,4},{7,5},{8,10},{9,11},{10,... | collective-permute-start | bytes 491528 | tf_op jit(solution)/shard_map/ppermute | solution.py:754
  12.7 12.0 %collective-permute-start = (bf16[80,512]{1,0:T(8,128)(2,1)S(1)}, bf16[80,512]{1,0:T(8,128)(2,1)S(1)}, u32[]{:S(2)}, u32[]{:S(2)}) collective-permute-start(bf16[80,512]{1,0:T(8,128)(2,1)S(1)} %get-tuple-element.33), channel_id=1, source_target_pairs={{0,4},{4,0},{8,12},{12,8},{1,5},{5,1},{9,13},{13,9},{2,6},{6,2},{1... | collective-permute-start | bytes 245768 | tf_op jit(solution)/shard_map/ppermute | solution.py:754
  14.7 10.0 %collective-permute-start.1 = (bf16[80,512]{1,0:T(8,128)(2,1)S(1)}, bf16[80,512]{1,0:T(8,128)(2,1)S(1)}, u32[]{:S(2)}, u32[]{:S(2)}) collective-permute-start(bf16[80,512]{1,0:T(8,128)(2,1)S(1)} %get-tuple-element.34), channel_id=1, source_target_pairs={{0,12},{4,8},{8,4},{12,0},{1,13},{5,9},{9,5},{13,1},{2,14},{6,10},... | collective-permute-start | bytes 245768 | tf_op jit(solution)/shard_map/ppermute | solution.py:754
  24.9 4.6 %copy-start.3 = (f32[75]{0:T(128)S(1)}, f32[75]{0:T(128)}, u32[]{:S(2)}) copy-start(f32[75]{0:T(128)} %param.27) | copy-start | bytes 904
  27.8 5.8 %collective-permute-start.5 = (bf16[80,640]{1,0:T(8,128)(2,1)S(1)}, bf16[80,640]{1,0:T(8,128)(2,1)S(1)}, u32[]{:S(2)}, u32[]{:S(2)}) collective-permute-start(bf16[80,640]{1,0:T(8,128)(2,1)S(1)} %get-tuple-element.48), channel_id=1, source_target_pairs={{0,4},{4,0},{8,12},{12,8},{1,5},{5,1},{9,13},{13,9},{2,6},{6,2},{1... | collective-permute-start | bytes 307208 | tf_op jit(solution)/shard_map/ppermute | solution.py:754
  28.6 6.6 %collective-permute-start.6 = (bf16[80,640]{1,0:T(8,128)(2,1)S(1)}, bf16[80,640]{1,0:T(8,128)(2,1)S(1)}, u32[]{:S(2)}, u32[]{:S(2)}) collective-permute-start(bf16[80,640]{1,0:T(8,128)(2,1)S(1)} %get-tuple-element.49), channel_id=1, source_target_pairs={{0,12},{4,8},{8,4},{12,0},{1,13},{5,9},{9,5},{13,1},{2,14},{6,10},... | collective-permute-start | bytes 307208 | tf_op jit(solution)/shard_map/ppermute | solution.py:754
  38.3 9.3 %collective-permute-start.9 = (bf16[80,1024]{1,0:T(8,128)(2,1)S(1)}, bf16[80,1024]{1,0:T(8,128)(2,1)S(1)}, u32[]{:S(2)}, u32[]{:S(2)}) collective-permute-start(bf16[80,1024]{1,0:T(8,128)(2,1)S(1)} %get-tuple-element.56.after), channel_id=1, source_target_pairs={{0,3},{1,2},{2,1},{3,0},{4,7},{5,6},{6,5},{7,4},{8,11},{9,10},{10,... | collective-permute-start | bytes 491528 | tf_op jit(solution)/shard_map/ppermute | solution.py:754
  40.8 6.8 %collective-permute-start.8 = (bf16[80,1024]{1,0:T(8,128)(2,1)S(1)}, bf16[80,1024]{1,0:T(8,128)(2,1)S(1)}, u32[]{:S(2)}, u32[]{:S(2)}) collective-permute-start(bf16[80,1024]{1,0:T(8,128)(2,1)S(1)} %get-tuple-element.56.after), channel_id=1, source_target_pairs={{0,2},{1,3},{2,0},{3,1},{4,6},{5,7},{6,4},{7,5},{8,10},{9,11},{10,... | collective-permute-start | bytes 491528 | tf_op jit(solution)/shard_map/ppermute | solution.py:754
  41.3 6.3 %collective-permute-start.7 = (bf16[80,1024]{1,0:T(8,128)(2,1)S(1)}, bf16[80,1024]{1,0:T(8,128)(2,1)S(1)}, u32[]{:S(2)}, u32[]{:S(2)}) collective-permute-start(bf16[80,1024]{1,0:T(8,128)(2,1)S(1)} %get-tuple-element.56.after), channel_id=1, source_target_pairs={{0,1},{1,0},{2,3},{3,2},{4,5},{5,4},{6,7},{7,6},{8,9},{9,8},{10,11... | collective-permute-start | bytes 491528 | tf_op jit(solution)/shard_map/ppermute | solution.py:754
